TPU v7x, 32 devices: a whole 2x2x4 slice. The times are simulated.
32 devices in a mesh: term: 8 (over z, core), doc: 4 (over y, x).
Axes of the slice: x: 2, y: 2, z: 4, core: 2. Of those that a mesh axis runs over, the one named last changes fastest.
Arguments:
- tile_values: bfloat16 [384, 512, 128], P('term', 'doc'), may hold values from 0.001 to 1, as said below
- tile_rows: int32 [8, 192], P('term', 'doc'), may hold values from 0 to 15, as said below
- tile_cols: int32 [8, 192], P('term', 'doc'), may hold values from 0 to 15, as said below
- tile_count: int32 [8, 4], P('term', 'doc'), may hold values from 16 to 48, as said below
- start_block: bfloat16 [8192, 256], P('doc'), may hold values from -6 to 6
Outputs:
- row_scale: float32 [16384], P('term')
- col_scale: float32 [8192], P('doc')
- left_basis: bfloat16 [16384, 256], P('term')
- right_basis: bfloat16 [8192, 256], P('doc')
Inputs may be any that keep to these rules, and one draw needn't show every extreme that they name: `tile_values`: entries are positive. `tile_rows`: within one block pair the occupied (row, column) pairs are distinct, and every tile row and tile column of every block pair holds an occupied tile. `tile_cols`: paired with tile_rows slot by slot. `tile_count`: some block pair has all 48 slots occupied.
All inputs are finite; a program needn't handle non-finite values.
Results may differ from a plain program's by a relative error of at most 0.006.
The roundings to bfloat16 on the way count: a program that leaves them out, or rounds other values in their place, can miss the bound.
Values may be sent and summed in bfloat16 or wider, within the bound.
A program may use at most 64 MiB of HBM per device.

v0:
```python
import functools

import jax
import jax.numpy as jnp
from jax import lax
from jax.experimental import pallas as pl
from jax.experimental.pallas import tpu as pltpu
from jax.sharding import PartitionSpec as P

TILE = 128
PASSES = 2
RB = 16
CB = 16


PRECISE = lax.Precision.HIGHEST
MESH = pl.DeviceIdType.MESH
VMEM = pl.BlockSpec(memory_space=pltpu.VMEM)
SMEM = pl.BlockSpec(memory_space=pltpu.SMEM)


BLOCK = 64
GROUP = 8


def block_inverse(block, low, high):
    rows = lax.broadcasted_iota(jnp.int32, block.shape, 0)
    pivots = jnp.ones_like(block)
    for base in range(0, BLOCK, GROUP):
        factors = []
        for at in range(base, base + GROUP):
            column = jnp.broadcast_to(block[:, low + at : low + at + 1], block.shape)
            for past, factor in enumerate(factors):
                column = column - factor * column[base + past : base + past + 1, :]
            pivots = jnp.where(rows == at, column, pivots)
            ratio = column * (1.0 / column[at : at + 1, :])
            factors.append(jnp.where(rows > at, ratio, 0.0))
        for at, factor in enumerate(factors):
            block = block - factor * block[base + at : base + at + 1, :]
    lanes = lax.broadcasted_iota(jnp.int32, block.shape, 1)
    inside = (lanes >= high) & (lanes < high + BLOCK)
    return jnp.where(inside, block * lax.rsqrt(pivots), 0.0)


def inverse_kernel(gram_ref, o_ref, work):
    width = gram_ref.shape[0]
    work[:, :width] = gram_ref[...]
    rows = lax.broadcasted_iota(jnp.int32, (width, width), 0)
    lanes = lax.broadcasted_iota(jnp.int32, (width, width), 1)
    work[:, width:] = jnp.where(rows == lanes, 1.0, 0.0)
    for index in range(width // BLOCK):
        start = index * BLOCK
        near = start // TILE * TILE
        low = start - near
        high = TILE - BLOCK - low
        block = work[start : start + BLOCK, near : near + TILE]
        rows = lax.broadcasted_iota(jnp.int32, block.shape, 0)
        lanes = lax.broadcasted_iota(jnp.int32, block.shape, 1)
        inside = (lanes >= low) & (lanes < low + BLOCK)
        block = jnp.where(inside, block, jnp.where(lanes - high == rows, 1.0, 0.0))
        inverse = block_inverse(block, low, high)
        panel = work[start : start + BLOCK, :]
        solved = jnp.dot(
            inverse,
            jnp.concatenate([panel, panel], axis=0),
            precision=PRECISE,
            preferred_element_type=jnp.float32,
        )
        o_ref[start : start + BLOCK, :] = solved[:, width:]
        if start + BLOCK < width:
            update = lax.dot_general(
                solved[:, :width],
                solved,
                (((0,), (0,)), ((), ())),
                precision=PRECISE,
                preferred_element_type=jnp.float32,
            )
            work[start + BLOCK :, :] = work[start + BLOCK :, :] - update[start + BLOCK :, :]


def factor_inverse(gram):
    width = gram.shape[0]
    return pl.pallas_call(
        inverse_kernel,
        out_shape=jax.ShapeDtypeStruct(gram.shape, gram.dtype),
        in_specs=[VMEM],
        out_specs=VMEM,
        scratch_shapes=[pltpu.VMEM((width, 2 * width), jnp.float32)],
        compiler_params=pltpu.CompilerParams(vmem_limit_bytes=16 << 20),
        name="inverse",
    )(gram).T


def params(identifier):
    return pltpu.CompilerParams(
        collective_id=identifier, has_side_effects=True, vmem_limit_bytes=32 << 20
    )


def greet(axes):
    barrier = pltpu.get_barrier_semaphore()
    total = 0
    for axis in axes:
        n = lax.axis_size(axis)
        me = lax.axis_index(axis)
        for step in range(1, n):
            pl.semaphore_signal(
                barrier, inc=1, device_id={axis: lax.rem(me + step, n)}, device_id_type=MESH
            )
        total += n - 1
    pl.semaphore_wait(barrier, total)


def remote(source, target, send_sem, recv_sem, axis, peer):
    return pltpu.make_async_remote_copy(
        src_ref=source,
        dst_ref=target,
        send_sem=send_sem,
        recv_sem=recv_sem,
        device_id={axis: peer},
        device_id_type=MESH,
    )


def all_sum_kernel(axis, x_ref, o_ref, held, send_sem, recv_sem):
    n = lax.axis_size(axis)
    me = lax.axis_index(axis)
    greet((axis,))
    copies = []
    for step in range(1, n):
        copy = remote(
            x_ref, held.at[step], send_sem.at[step], recv_sem.at[step], axis, lax.rem(me + step, n)
        )
        copy.start()
        copies.append(copy)
    held[0] = x_ref[...]
    for copy in copies:
        copy.wait()
    total = held[me]
    for source in range(1, n):
        total = total + held[lax.rem(me - source + n, n)]
    o_ref[...] = total


def all_sum(x, axis, identifier):
    n = lax.axis_size(axis)
    return pl.pallas_call(
        functools.partial(all_sum_kernel, axis),
        out_shape=jax.ShapeDtypeStruct(x.shape, x.dtype),
        in_specs=[VMEM],
        out_specs=VMEM,
        scratch_shapes=[
            pltpu.VMEM((n,) + x.shape, x.dtype),
            pltpu.SemaphoreType.DMA((n,)),
            pltpu.SemaphoreType.DMA((n,)),
        ],
        compiler_params=params(identifier),
        name="all_sum",
    )(x)


def scatter_sum_kernel(axis, x_ref, o_ref, held, send_sem, recv_sem):
    n = lax.axis_size(axis)
    me = lax.axis_index(axis)
    greet((axis,))
    copies = []
    for step in range(1, n):
        peer = lax.rem(me + step, n)
        copy = remote(
            x_ref.at[peer], held.at[step], send_sem.at[step], recv_sem.at[step], axis, peer
        )
        copy.start()
        copies.append(copy)
    o_ref[...] = x_ref[me]
    for step, copy in enumerate(copies):
        copy.wait()
        o_ref[...] += held[step + 1]


def scatter_sum(x, axis, identifier):
    n = lax.axis_size(axis)
    return pl.pallas_call(
        functools.partial(scatter_sum_kernel, axis),
        out_shape=jax.ShapeDtypeStruct(x.shape[1:], x.dtype),
        in_specs=[VMEM],
        out_specs=VMEM,
        scratch_shapes=[
            pltpu.VMEM(x.shape, x.dtype),
            pltpu.SemaphoreType.DMA((n,)),
            pltpu.SemaphoreType.DMA((n,)),
        ],
        compiler_params=params(identifier),
        name="scatter_sum",
    )(x)


def gather_kernel(axis, x_ref, o_ref, send_sem, recv_sem):
    n = lax.axis_size(axis)
    me = lax.axis_index(axis)
    greet((axis,))
    copies = []
    for step in range(1, n):
        copy = remote(
            x_ref, o_ref.at[me], send_sem.at[step], recv_sem.at[step], axis, lax.rem(me + step, n)
        )
        copy.start()
        copies.append(copy)
    o_ref[me] = x_ref[...]
    for copy in copies:
        copy.wait()


def gather(x, axis, identifier):
    n = lax.axis_size(axis)
    return pl.pallas_call(
        functools.partial(gather_kernel, axis),
        out_shape=jax.ShapeDtypeStruct((n,) + x.shape, x.dtype),
        in_specs=[VMEM],
        out_specs=VMEM,
        scratch_shapes=[
            pltpu.SemaphoreType.DMA((n,)),
            pltpu.SemaphoreType.DMA((n,)),
        ],
        compiler_params=params(identifier),
        name="gather",
    )(x)


def paired():
    n, me = lax.axis_size("term"), lax.axis_index("term")
    return n // 2, me // 2, lax.rem(me, 2)


def greet_paired(with_doc):
    nz, z, c = paired()
    barrier = pltpu.get_barrier_semaphore()
    targets = [("term", 2 * z + 1 - c)]
    targets += [("term", 2 * lax.rem(z + step, nz) + c) for step in range(1, nz)]
    if with_doc:
        m, my = lax.axis_size("doc"), lax.axis_index("doc")
        targets += [("doc", lax.rem(my + step, m)) for step in range(1, m)]
    for axis, peer in targets:
        pl.semaphore_signal(barrier, inc=1, device_id={axis: peer}, device_id_type=MESH)
    pl.semaphore_wait(barrier, len(targets))


def scatter_paired(x_ref, near, mid, far, total_ref, near_send, near_recv, far_send, far_recv):
    nz, z, c = paired()
    order = list(range(1, nz)) + [0]
    near_copies = {}
    for step in order:
        near_copies[step] = remote(
            x_ref.at[lax.rem(z + step, nz), 1 - c],
            near.at[step],
            near_send.at[step],
            near_recv.at[step],
            "term",
            2 * z + 1 - c,
        )
        near_copies[step].start()
    far_copies = []
    for step in range(1, nz):
        near_copies[step].wait()
        there = lax.rem(z + step, nz)
        mid[step] = x_ref[there, c] + near[step]
        copy = remote(
            mid.at[step], far.at[step], far_send.at[step], far_recv.at[step], "term", 2 * there + c
        )
        copy.start()
        far_copies.append(copy)
    near_copies[0].wait()
    total_ref[...] = x_ref[z, c] + near[0]
    for step, copy in enumerate(far_copies):
        copy.wait()
        total_ref[...] += far[step + 1]


def gather_paired(x_ref, o_ref, near_send, near_recv, far_send, far_recv):
    nz, z, c = paired()
    sibling = 2 * z + 1 - c
    far_copies = []
    for step in range(1, nz):
        copy = remote(
            x_ref,
            o_ref.at[z, c],
            far_send.at[step],
            far_recv.at[step],
            "term",
            2 * lax.rem(z + step, nz) + c,
        )
        copy.start()
        far_copies.append(copy)
    copy = remote(x_ref, o_ref.at[z, c], near_send.at[0], near_recv.at[0], "term", sibling)
    copy.start()
    near_copies = [copy]
    o_ref[z, c] = x_ref[...]
    for step in range(1, nz):
        far_copies[step - 1].wait()
        here = o_ref.at[lax.rem(z - step + nz, nz), c]
        copy = remote(here, here, near_send.at[step], near_recv.at[step], "term", sibling)
        copy.start()
        near_copies.append(copy)
    for copy in near_copies:
        copy.wait()


def semaphores(*sizes):
    return [pltpu.SemaphoreType.DMA((size,)) for size in sizes]


def scatter_term_kernel(x_ref, o_ref, near, mid, far, *sems):
    greet_paired(False)
    scatter_paired(x_ref, near, mid, far, o_ref, *sems)


def scatter_term(x, identifier):
    nz = x.shape[0]
    share = x.shape[2:]
    return pl.pallas_call(
        scatter_term_kernel,
        out_shape=jax.ShapeDtypeStruct(share, x.dtype),
        in_specs=[VMEM],
        out_specs=VMEM,
        scratch_shapes=[pltpu.VMEM((nz,) + share, x.dtype)] * 3 + semaphores(nz, nz, nz, nz),
        compiler_params=params(identifier),
        name="scatter_term",
    )(x)


def gather_term_kernel(x_ref, o_ref, *sems):
    greet_paired(False)
    gather_paired(x_ref, o_ref, *sems)


def gather_term(x, identifier):
    nz = lax.axis_size("term") // 2
    return pl.pallas_call(
        gather_term_kernel,
        out_shape=jax.ShapeDtypeStruct((nz, 2) + x.shape, x.dtype),
        in_specs=[VMEM],
        out_specs=VMEM,
        scratch_shapes=semaphores(nz, nz, nz, nz),
        compiler_params=params(identifier),
        name="gather_term",
    )(x)


def gram_sum_kernel(x_ref, o_ref, near, mid, far, second, part, done, *sems):
    m, my = lax.axis_size("doc"), lax.axis_index("doc")
    send_b, recv_b = sems[4:6]
    greet_paired(True)
    scatter_paired(x_ref, near, mid, far, part, *sems[:4])
    copies = []
    for step in range(1, m):
        copy = remote(
            part, second.at[step], send_b.at[step], recv_b.at[step], "doc", lax.rem(my + step, m)
        )
        copy.start()
        copies.append(copy)
    second[0] = part[...]
    for copy in copies:
        copy.wait()
    total = second[my]
    for source in range(1, m):
        total = total + second[lax.rem(my - source + m, m)]
    done[...] = total
    gather_paired(done, o_ref, *sems[6:])


def gram_sum(x, identifier):
    nz, m = x.shape[0], lax.axis_size("doc")
    share = x.shape[2:]
    return pl.pallas_call(
        gram_sum_kernel,
        out_shape=jax.ShapeDtypeStruct(x.shape, x.dtype),
        in_specs=[VMEM],
        out_specs=VMEM,
        scratch_shapes=[pltpu.VMEM((nz,) + share, x.dtype)] * 3
        + [
            pltpu.VMEM((m,) + share, x.dtype),
            pltpu.VMEM(share, x.dtype),
            pltpu.VMEM(share, x.dtype),
        ]
        + semaphores(nz, nz, nz, nz, m, m, nz, nz, nz, nz),
        compiler_params=params(identifier),
        name="gram_sum",
    )(x)


def dense_kernel(rows_ref, cols_ref, count_ref, tiles_ref, o_ref, t_ref):
    def clear(index, carry):
        at = pl.multiple_of(index * 32, 32)
        o_ref[pl.ds(at, 32), :] = jnp.zeros((32, o_ref.shape[1]), o_ref.dtype)
        t_ref[pl.ds(at, 32), :] = jnp.zeros((32, t_ref.shape[1]), t_ref.dtype)
        return carry

    lax.fori_loop(0, o_ref.shape[0] // 32, clear, 0)

    def place(slot, carry):
        row = pl.multiple_of(rows_ref[0, slot] * TILE, TILE)
        col = pl.multiple_of(cols_ref[0, slot] * TILE, TILE)
        tile = tiles_ref[slot]
        o_ref[pl.ds(row, TILE), pl.ds(col, TILE)] = tile
        t_ref[pl.ds(col, TILE), pl.ds(row, TILE)] = tile.T
        return carry

    lax.fori_loop(0, count_ref[0, 0], place, 0)


def dense_matrix(tile_values, tile_rows, tile_cols, tile_count):
    return pl.pallas_call(
        dense_kernel,
        out_shape=[
            jax.ShapeDtypeStruct((RB * TILE, CB * TILE), tile_values.dtype),
            jax.ShapeDtypeStruct((CB * TILE, RB * TILE), tile_values.dtype),
        ],
        in_specs=[SMEM, SMEM, SMEM, VMEM],
        out_specs=[VMEM, VMEM],
        compiler_params=pltpu.CompilerParams(vmem_limit_bytes=32 << 20),
        name="dense",
    )(tile_rows, tile_cols, tile_count, tile_values)


def row_sums(matrix, scale):
    return jnp.sum(matrix.astype(jnp.float32) * scale[None, :], axis=1)


def col_sums(matrix, scale):
    return jnp.sum(matrix.astype(jnp.float32) * scale[:, None], axis=0)


def vector_sum(x, axis, identifier):
    return all_sum(x.reshape(-1, TILE), axis, identifier).reshape(-1)


def total_gram(block, extra, scale, identifier):
    n = lax.axis_size("term")
    width = block.shape[1]
    gram = jnp.dot(block.T, block, precision=PRECISE) / scale
    rows = [gram]
    if extra is not None:
        rows += [extra[None, :], jnp.zeros((8 * n - 1, width), jnp.float32)]
    stacked = jnp.concatenate(rows, axis=0) if extra is not None else gram
    summed = gram_sum(stacked.reshape(n // 2, 2, -1, width), identifier).reshape(stacked.shape)
    return summed[:width], (summed[width] if extra is not None else None)


def per_device(tile_values, tile_rows, tile_cols, tile_count, start_block):
    terms_total = RB * TILE * lax.axis_size("term")
    docs_total = CB * TILE * lax.axis_size("doc")
    width = start_block.shape[1]
    matrix, turned = dense_matrix(tile_values, tile_rows, tile_cols, tile_count)

    mean_part = jnp.sum(start_block.astype(jnp.float32), axis=0)
    col_flat = jnp.ones((CB * TILE,), jnp.float32)
    for sweep_index in range(PASSES):
        row_part = row_sums(matrix, col_flat)
        if sweep_index == 0:
            pad = jnp.zeros((8 * TILE - width % (8 * TILE),), jnp.float32)
            joined = vector_sum(jnp.concatenate([row_part, mean_part, pad]), "doc", 0)
            row_total = joined[: RB * TILE]
            start_mean = joined[RB * TILE : RB * TILE + width]
        else:
            row_total = vector_sum(row_part, "doc", 1 + 2 * sweep_index)
        row_flat = 1.0 / row_total
        col_part = col_sums(matrix, row_flat)
        col_flat = 1.0 / vector_sum(col_part, "term", 2 + 2 * sweep_index)
    scaled_start = (col_flat[:, None] * start_block.astype(jnp.float32)).astype(jnp.bfloat16)
    left_part = jnp.dot(matrix, scaled_start, preferred_element_type=jnp.float32)
    doc_size = lax.axis_size("doc")
    left_share = RB * TILE // doc_size
    left_offset = lax.axis_index("doc") * left_share
    weight_sum = vector_sum(row_sums(matrix, col_flat), "doc", 16)
    left_raw = scatter_sum(left_part.reshape(doc_size, left_share, width), "doc", 17)
    row_rows = lax.dynamic_slice_in_dim(row_flat, left_offset, left_share)
    row_weight = row_rows * lax.dynamic_slice_in_dim(weight_sum, left_offset, left_share)
    left_block = (
        row_rows[:, None] * left_raw - row_weight[:, None] * start_mean[None, :] / docs_total
    )
    weighted = jnp.sum(row_weight[:, None] * left_block, axis=0)
    left_gram, weighted = total_gram(left_block, weighted, terms_total, 18)
    left_inverse = factor_inverse(left_gram)
    share_float = jnp.dot(left_block, left_inverse, precision=PRECISE)
    lean = jnp.dot(weighted, left_inverse, precision=PRECISE)
    left_basis = gather(share_float.astype(jnp.bfloat16), "doc", 19).reshape(RB * TILE, width)
    scaled_left = (row_flat[:, None] * left_basis.astype(jnp.float32)).astype(jnp.bfloat16)
    right_part = jnp.dot(turned, scaled_left, preferred_element_type=jnp.float32)
    term_size = lax.axis_size("term")
    right_share = CB * TILE // term_size
    right_offset = lax.axis_index("term") * right_share
    right_raw = scatter_term(right_part.reshape(term_size // 2, 2, right_share, width), 20)
    col_rows = lax.dynamic_slice_in_dim(col_flat, right_offset, right_share)
    right_block = col_rows[:, None] * right_raw - lean[None, :] / docs_total
    right_gram, _ = total_gram(right_block, None, docs_total, 21)
    right_inverse = factor_inverse(right_gram)
    right_piece = jnp.dot(right_block, right_inverse, precision=PRECISE).astype(jnp.bfloat16)
    right_basis = gather_term(right_piece, 22).reshape(CB * TILE, width)
    return (row_flat, col_flat, left_basis, right_basis)


def solution(mesh):
    placed = (
        P("term", "doc", None),
        P("term", "doc"),
        P("term", "doc"),
        P("term", "doc"),
        P("doc", None),
    )
    return jax.shard_map(
        per_device,
        mesh=mesh,
        in_specs=placed,
        out_specs=(P("term"), P("doc"), P("term", None), P("doc", None)),
        check_vma=False,
    )
```

profile of v0, /device:TPU:0, one launch (start us, length us, event | category | flops | bytes accessed | tf_op | source)
XLA Modules:
  0.0 204.9 jit_solution(12962711590300432678)
XLA Ops:
  1.3 1.5 convert_reduce_fusion.1
  2.8 0.1 pad.2.clone
  2.9 0.0 copy-start.2
  2.9 1.4 copy-done.2
  4.3 0.0 copy-start.3
  4.3 0.7 copy-done.3
  4.9 0.0 copy-start.4
  4.9 0.7 copy-done.4
  5.6 5.3 %dense.1 = (bf16[2048,2048]{1,0:T(8,128)(2,1)S(1)}, bf16[2048,2048]{1,0:T(8,128)(2,1)S(1)}) custom-call(s32[1,48]{1,0:T(1,128)S(1)} %copy-done.3, s32[1,48]{1,0:T(1,128)S(1)} %copy-done.4, s32[1,1]{1,0:T(1,128)S(6)} %copy.12.count_ref, bf16[48,128,128]{2,1,0:T(8,128)(2,1)S(1)} %copy-done.2), custom_call_target="tpu_custom_call" | custom-call | tf_op jit(solution)/shard_map/dense/pallas_call | solution.py:411
  10.9 0.0 copy-start.5
  10.9 3.2 %copy-done.5 = bf16[2048,2048]{1,0:T(8,128)(2,1)} copy-done((bf16[2048,2048]{1,0:T(8,128)(2,1)}, bf16[2048,2048]{1,0:T(8,128)(2,1)S(1)}, u32[]{:S(2)}) %copy-start.5) | copy-done | bytes 8388632
  14.1 0.0 copy-start
  14.1 1.2 convert_reduce_fusion
  15.3 6.1 %all_sum.5 = f32[24,128]{1,0:T(8,128)S(1)} custom-call(f32[24,128]{1,0:T(8,128)S(1)} %maximum_bitcast_fusion.x_ref), custom_call_target="tpu_custom_call" | custom-call | tf_op jit(solution)/shard_map/all_sum/pallas_call | solution.py:147
  21.5 1.7 fusion
  23.2 6.5 %all_sum.6 = f32[16,128]{1,0:T(8,128)S(1)} custom-call(f32[16,128]{1,0:T(8,128)S(1)} %bitcast.53), custom_call_target="tpu_custom_call" | custom-call | tf_op jit(solution)/shard_map/all_sum/pallas_call | solution.py:147
  29.7 0.0 copy-done
  29.7 1.7 fusion.1
  31.4 4.8 %all_sum.7 = f32[16,128]{1,0:T(8,128)S(1)} custom-call(f32[16,128]{1,0:T(8,128)S(1)} %bitcast.54), custom_call_target="tpu_custom_call" | custom-call | tf_op jit(solution)/shard_map/all_sum/pallas_call | solution.py:147
  36.2 0.0 copy-start.7
  36.3 0.0 copy-start.1
  36.3 0.0 copy-start.6
  36.3 5.2 %fusion.2 = f32[2048]{0:T(1024)S(1)} fusion(bf16[2048,2048]{1,0:T(8,128)(2,1)} %copy-done, f32[2048]{0:T(1024)S(1)} %get-tuple-element.16), kind=kLoop, calls=%fused_computation.7 | loop fusion | flops 12580864 | bytes 8404992 | tf_op jit(solution)/shard_map/reduce_sum | solution.py:429
  41.5 6.1 %all_sum.8 = f32[16,128]{1,0:T(8,128)S(1)} custom-call(f32[16,128]{1,0:T(8,128)S(1)} %bitcast.55), custom_call_target="tpu_custom_call" | custom-call | tf_op jit(solution)/shard_map/all_sum/pallas_call | solution.py:147
  47.7 0.0 copy-start.8
  47.7 0.1 dynamic_slice.11
  47.8 0.0 copy-done.1
  47.8 0.0 slice-start
  47.8 1.7 fusion.3
  49.5 0.0 copy-done.6
  49.5 0.0 slice-start.1
  49.5 2.6 %fusion.5 = f32[2048,256]{1,0:T(8,128)S(1)} fusion(bf16[2048,2048]{1,0:T(8,128)(2,1)S(1)} %copy-done.1, bf16[2048,256]{1,0:T(8,128)(2,1)S(1)} %copy-done.6, f32[2048]{0:T(1024)S(1)} %divide_bitcast_fusion), kind=kOutput, calls=%fused_computation.17 | convolution fusion | flops 2149056512 | bytes 11542528 | tf_op jit(solution)/shard_map/dot_general | solution.py:469
  52.1 0.0 copy-done.8
  52.1 26.3 %scatter_sum.1 = f32[512,256]{1,0:T(8,128)S(1)} custom-call(f32[4,512,256]{2,1,0:T(8,128)S(1)} %bitcast.46), custom_call_target="tpu_custom_call" | custom-call | tf_op jit(solution)/shard_map/scatter_sum/pallas_call | solution.py:182
  78.4 4.7 %all_sum.9 = f32[16,128]{1,0:T(8,128)S(1)} custom-call(f32[16,128]{1,0:T(8,128)S(1)} %bitcast.52), custom_call_target="tpu_custom_call" | custom-call | tf_op jit(solution)/shard_map/all_sum/pallas_call | solution.py:147
  83.1 0.0 copy-done.7
  83.1 0.1 fusion.25
  83.2 0.2 multiply_reduce_fusion
  83.4 1.5 convolution_multiply_fusion.1
  84.9 0.1 maximum_maximum_fusion
  85.0 19.4 %gram_sum.2 = f32[4,2,40,256]{3,2,1,0:T(8,128)S(1)} custom-call(f32[4,2,40,256]{3,2,1,0:T(8,128)S(1)} %bitcast.47), custom_call_target="tpu_custom_call" | custom-call | tf_op jit(solution)/shard_map/gram_sum/pallas_call | solution.py:373
  104.5 9.4 %inverse.2 = f32[256,256]{1,0:T(8,128)S(1)} custom-call(f32[256,256]{1,0:T(8,128)S(1)} %slice.18.gram_ref), custom_call_target="tpu_custom_call" | custom-call | tf_op jit(solution)/shard_map/inverse/pallas_call | solution.py:83
  113.9 0.3 fusion.8
  114.2 0.7 convolution_convert_fusion.x_ref
  114.9 14.9 %gather.1 = bf16[4,512,256]{2,1,0:T(8,128)(2,1)S(1)} custom-call(bf16[512,256]{1,0:T(8,128)(2,1)S(1)} %convolution_convert_fusion.x_ref), custom_call_target="tpu_custom_call" | custom-call | tf_op jit(solution)/shard_map/gather/pallas_call | solution.py:215
  129.8 0.3 multiply_convert_fusion
  130.1 0.0 slice-done
  130.1 0.0 slice-done.1
  130.1 2.5 %fusion.26.x_ref = f32[4,2,256,256]{3,2,1,0:T(8,128)S(1)} fusion(bf16[4,2,256,2048]{3,2,1,0:T(8,128)(2,1)S(1)} %bitcast.59, bf16[2048,256,1,1]{1,0,3,2:T(8,128)(2,1)S(1)} %bitcast.60), kind=kOutput, calls=%fused_computation.50 | convolution fusion | flops 2147483648 | bytes 11534336 | tf_op jit(solution)/shard_map/dot_general | solution.py:487
  132.6 23.2 %scatter_term.1 = f32[256,256]{1,0:T(8,128)S(1)} custom-call(f32[4,2,256,256]{3,2,1,0:T(8,128)S(1)} %fusion.26.x_ref), custom_call_target="tpu_custom_call" | custom-call | tf_op jit(solution)/shard_map/scatter_term/pallas_call | solution.py:319
  155.9 0.9 convolution_multiply_fusion
  156.8 22.1 %gram_sum.3 = f32[4,2,32,256]{3,2,1,0:T(8,128)S(1)} custom-call(f32[4,2,32,256]{3,2,1,0:T(8,128)S(1)} %bitcast.51), custom_call_target="tpu_custom_call" | custom-call | tf_op jit(solution)/shard_map/gram_sum/pallas_call | solution.py:373
  178.8 9.4 %inverse.3 = f32[256,256]{1,0:T(8,128)S(1)} custom-call(f32[256,256]{1,0:T(8,128)S(1)} %bitcast.50), custom_call_target="tpu_custom_call" | custom-call | tf_op jit(solution)/shard_map/inverse/pallas_call | solution.py:83
  188.2 0.4 convolution_convert_fusion.1.x_ref
  188.6 14.3 %gather_term.1 = bf16[4,2,256,256]{3,2,1,0:T(8,128)(2,1)S(1)} custom-call(bf16[256,256]{1,0:T(8,128)(2,1)S(1)} %convolution_convert_fusion.1.x_ref), custom_call_target="tpu_custom_call" | custom-call | tf_op jit(solution)/shard_map/gather_term/pallas_call | solution.py:337
  203.0 1.0 copy.13
  203.9 1.0 copy.14
  (12 shorter events, 0.1 us)
Async XLA Ops:
  2.9 1.4 copy-start.2
  4.3 0.7 copy-start.3
  4.9 0.7 copy-start.4
  10.9 3.2 %copy-start.5 = (bf16[2048,2048]{1,0:T(8,128)(2,1)}, bf16[2048,2048]{1,0:T(8,128)(2,1)S(1)}, u32[]{:S(2)}) copy-start(bf16[2048,2048]{1,0:T(8,128)(2,1)S(1)} %get-tuple-element.7) | copy-start | bytes 25165828
  14.1 15.6 %copy-start = (bf16[2048,2048]{1,0:T(8,128)(2,1)}, bf16[2048,2048]{1,0:T(8,128)(2,1)S(1)}, u32[]{:S(2)}) copy-start(bf16[2048,2048]{1,0:T(8,128)(2,1)S(1)} %get-tuple-element.6) | copy-start | bytes 25165828
  36.2 46.9 %copy-start.7 = (f32[2048]{0:T(1024)}, f32[2048]{0:T(1024)S(1)}, u32[]{:S(2)}) copy-start(f32[2048]{0:T(1024)S(1)} %get-tuple-element.16) | copy-start | bytes 24580
  36.3 11.5 %copy-start.1 = (bf16[2048,2048]{1,0:T(8,128)(2,1)S(1)}, bf16[2048,2048]{1,0:T(8,128)(2,1)}, u32[]{:S(2)}) copy-start(bf16[2048,2048]{1,0:T(8,128)(2,1)} %copy-done) | copy-start | bytes 25165828
  36.3 13.2 %copy-start.6 = (bf16[2048,256]{1,0:T(8,128)(2,1)S(1)}, bf16[2048,256]{1,0:T(8,128)(2,1)}, u32[]{:S(2)}) copy-start(bf16[2048,256]{1,0:T(8,128)(2,1)} %param.9) | copy-start | bytes 3145732
  47.7 4.4 %copy-start.8 = (f32[2048]{0:T(1024)}, f32[2048]{0:T(1024)S(1)}, u32[]{:S(2)}) copy-start(f32[2048]{0:T(1024)S(1)} %divide_bitcast_fusion) | copy-start | bytes 24580
  47.8 82.4 %slice-start = ((s8[8388608]{0:T(1024)(128)(4,1)}), s8[4194304]{0:T(1024)(128)(4,1)S(1)}, s32[]{:S(2)}) async-start(s8[8388608]{0:T(1024)(128)(4,1)} %bitcast.57), calls=%async_computation | async-start | bytes 8388608
  49.5 80.6 %slice-start.1 = ((s8[8388608]{0:T(1024)(128)(4,1)}), s8[4194304]{0:T(1024)(128)(4,1)S(1)}, s32[]{:S(2)}) async-start(s8[8388608]{0:T(1024)(128)(4,1)} %bitcast.57), calls=%async_computation.1 | async-start | bytes 8388608
where the time goes:
time: 204 us; the launch traced here: 205 us
  Pallas kernels  173 us (85%)
  other arithmetic  13.8 us (7%)
  matrix products  8.81 us (4%)
  local copies, waits for them, and re-layouts  8.1 us (4%)
    pallas_call x2, Pallas kernels, gram_sum(): pl.pallas_call(gram_sum_kernel, out_shape=jax.ShapeDtypeStruct(x.shape, x...  41.5 us
    pallas_call x5, Pallas kernels, all_sum(): pl.pallas_call(functools.partial(all_sum_kernel, axis), out_shape=jax.Sha...  28.3 us
    pallas_call x1, Pallas kernels, scatter_sum(): pl.pallas_call(functools.partial(scatter_sum_kernel, axis), out_shape=jax...  26.3 us
    pallas_call x1, Pallas kernels, scatter_term(): pl.pallas_call(scatter_term_kernel, out_shape=jax.ShapeDtypeStruct(share,...  23.2 us
    pallas_call x2, Pallas kernels, factor_inverse(): pl.pallas_call(inverse_kernel, out_shape=jax.ShapeDtypeStruct(gram.shape,...  18.7 us
    pallas_call x1, Pallas kernels, gather(): pl.pallas_call(functools.partial(gather_kernel, axis), out_shape=jax.Shap...  14.9 us
    pallas_call x1, Pallas kernels, gather_term(): pl.pallas_call(gather_term_kernel, out_shape=jax.ShapeDtypeStruct((nz, 2)...  14.3 us
    unnamed x24, local copies, waits for them, and re-layouts  7.91 us

commit v1 on v0

--- a/solution.py
+++ b/solution.py
@@ -8,7 +8,6 @@
 from jax.sharding import PartitionSpec as P
 
 TILE = 128
-PASSES = 2
 RB = 16
 CB = 16
 
@@ -122,43 +121,6 @@
     )
 
 
-def all_sum_kernel(axis, x_ref, o_ref, held, send_sem, recv_sem):
-    n = lax.axis_size(axis)
-    me = lax.axis_index(axis)
-    greet((axis,))
-    copies = []
-    for step in range(1, n):
-        copy = remote(
-            x_ref, held.at[step], send_sem.at[step], recv_sem.at[step], axis, lax.rem(me + step, n)
-        )
-        copy.start()
-        copies.append(copy)
-    held[0] = x_ref[...]
-    for copy in copies:
-        copy.wait()
-    total = held[me]
-    for source in range(1, n):
-        total = total + held[lax.rem(me - source + n, n)]
-    o_ref[...] = total
-
-
-def all_sum(x, axis, identifier):
-    n = lax.axis_size(axis)
-    return pl.pallas_call(
-        functools.partial(all_sum_kernel, axis),
-        out_shape=jax.ShapeDtypeStruct(x.shape, x.dtype),
-        in_specs=[VMEM],
-        out_specs=VMEM,
-        scratch_shapes=[
-            pltpu.VMEM((n,) + x.shape, x.dtype),
-            pltpu.SemaphoreType.DMA((n,)),
-            pltpu.SemaphoreType.DMA((n,)),
-        ],
-        compiler_params=params(identifier),
-        name="all_sum",
-    )(x)
-
-
 def scatter_sum_kernel(axis, x_ref, o_ref, held, send_sem, recv_sem):
     n = lax.axis_size(axis)
     me = lax.axis_index(axis)
@@ -387,50 +349,190 @@
     )(x)
 
 
-def dense_kernel(rows_ref, cols_ref, count_ref, tiles_ref, o_ref, t_ref):
-    def clear(index, carry):
-        at = pl.multiple_of(index * 32, 32)
-        o_ref[pl.ds(at, 32), :] = jnp.zeros((32, o_ref.shape[1]), o_ref.dtype)
-        t_ref[pl.ds(at, 32), :] = jnp.zeros((32, t_ref.shape[1]), t_ref.dtype)
+def split3(value):
+    high = value.astype(jnp.bfloat16)
+    rest = value - high.astype(jnp.float32)
+    middle = rest.astype(jnp.bfloat16)
+    return high, middle, (rest - middle.astype(jnp.float32)).astype(jnp.bfloat16)
+
+
+def spread(value, parts):
+    high, middle, low = (part.astype(jnp.float32) for part in split3(value))
+    blocks, depth, lanes = parts.shape
+    rows = lax.broadcasted_iota(jnp.int32, (depth, lanes), 0)
+    for block in range(blocks):
+        at = slice(block, block + 1)
+        picked = jnp.where(rows == 0, high[at], jnp.where(rows == 1, middle[at], low[at]))
+        parts[block] = jnp.where(rows < 3, picked, 0.0).astype(jnp.bfloat16)
+
+
+def tile_sums(tiles, source_ids, parts, sums, target, forward):
+    slots = sums.shape[0]
+    for slot in range(slots):
+        product = lax.dot_general(
+            parts[source_ids[slot]],
+            tiles[slot],
+            (((1,), (1 if forward else 0,)), ((), ())),
+            preferred_element_type=jnp.float32,
+        )
+        sums[slot : slot + 1, :] = product[0:1] + product[1:2] + product[2:3]
+    stacked = jnp.concatenate(split3(sums[...]), axis=0)
+    return jnp.dot(target, stacked, preferred_element_type=jnp.float32)
+
+
+def start_exchange(held, axis, send_sem, recv_sem):
+    n, me = lax.axis_size(axis), lax.axis_index(axis)
+    copies = []
+    for step in range(1, n):
+        copy = remote(
+            held.at[0], held.at[step], send_sem.at[step], recv_sem.at[step], axis, lax.rem(me + step, n)
+        )
+        copy.start()
+        copies.append(copy)
+    return copies
+
+
+def finish_exchange(copies, held, axis):
+    n, me = lax.axis_size(axis), lax.axis_index(axis)
+    for copy in copies:
+        copy.wait()
+    total = held[me]
+    for source in range(1, n):
+        total = total + held[lax.rem(me - source + n, n)]
+    return total
+
+
+def scale_kernel(
+    ids,
+    live,
+    tiles_hbm,
+    start_ref,
+    row_ref,
+    col_ref,
+    weight_ref,
+    mean_ref,
+    dense_ref,
+    turned_ref,
+    tiles,
+    flipped,
+    parts,
+    sums,
+    held_a,
+    held_b,
+    held_c,
+    held_d,
+    held_e,
+    load_sem,
+    *sems,
+):
+    slots = tiles_hbm.shape[0]
+    load = pltpu.make_async_copy(tiles_hbm, tiles.at[pl.ds(0, slots)], load_sem)
+    load.start()
+    greet(("term", "doc"))
+    tiles[slots] = jnp.zeros(tiles.shape[1:], tiles.dtype)
+    flipped[slots] = jnp.zeros(tiles.shape[1:], tiles.dtype)
+    blocks = row_ref.shape[0]
+    places = lax.broadcasted_iota(jnp.int32, (blocks, live.shape[1]), 0)
+    to_rows = jnp.where(places == live[0:1, :], 1.0, 0.0).astype(jnp.bfloat16)
+    to_cols = jnp.where(places == live[1:2, :], 1.0, 0.0).astype(jnp.bfloat16)
+    row_ids, col_ids = ids.at[pl.ds(0, slots)], ids.at[pl.ds(slots, slots)]
+
+    def build(out_ref, source, turn):
+        def place_row(outer, carry):
+            at = pl.multiple_of(outer * TILE, TILE)
+            for inner in range(blocks):
+                place = inner * blocks + outer if turn else outer * blocks + inner
+                tile = source[ids[2 * slots + place]]
+                out_ref[pl.ds(at, TILE), inner * TILE : (inner + 1) * TILE] = tile
+            return carry
+
+        lax.fori_loop(0, blocks, place_row, 0)
+
+    def flip(slot, carry):
+        flipped[slot] = tiles[slot].T
         return carry
 
-    lax.fori_loop(0, o_ref.shape[0] // 32, clear, 0)
-
-    def place(slot, carry):
-        row = pl.multiple_of(rows_ref[0, slot] * TILE, TILE)
-        col = pl.multiple_of(cols_ref[0, slot] * TILE, TILE)
-        tile = tiles_ref[slot]
-        o_ref[pl.ds(row, TILE), pl.ds(col, TILE)] = tile
-        t_ref[pl.ds(col, TILE), pl.ds(row, TILE)] = tile.T
-        return carry
-
-    lax.fori_loop(0, count_ref[0, 0], place, 0)
-
-
-def dense_matrix(tile_values, tile_rows, tile_cols, tile_count):
+    spread(jnp.ones(row_ref.shape, jnp.float32), parts)
+    mean = jnp.sum(start_ref[...].astype(jnp.float32), axis=0, keepdims=True)
+    load.wait()
+    held_a[0, :blocks, :] = tile_sums(tiles, col_ids, parts, sums, to_rows, True)
+    extra = held_a.shape[1] - blocks
+    pieces = [mean[:, at : at + TILE] for at in range(0, mean.shape[1], TILE)]
+    pieces.append(jnp.zeros((extra - len(pieces), TILE), jnp.float32))
+    held_a[0, blocks:, :] = jnp.concatenate(pieces, axis=0)
+    copies = start_exchange(held_a, "doc", *sems[0:2])
+    build(dense_ref, tiles, False)
+    joined = finish_exchange(copies, held_a, "doc")
+    mean_ref[...] = joined[blocks:, :]
+    spread(1.0 / joined[:blocks], parts)
+
+    held_b[0] = tile_sums(tiles, row_ids, parts, sums, to_cols, False)
+    copies = start_exchange(held_b, "term", *sems[2:4])
+    lax.fori_loop(0, slots, flip, 0)
+    spread(1.0 / finish_exchange(copies, held_b, "term"), parts)
+
+    held_c[0] = tile_sums(tiles, col_ids, parts, sums, to_rows, True)
+    copies = start_exchange(held_c, "doc", *sems[4:6])
+    build(turned_ref, flipped, True)
+    row_scale = 1.0 / finish_exchange(copies, held_c, "doc")
+    row_ref[...] = row_scale
+    spread(row_scale, parts)
+
+    held_d[0] = tile_sums(tiles, row_ids, parts, sums, to_cols, False)
+    copies = start_exchange(held_d, "term", *sems[6:8])
+    col_scale = 1.0 / finish_exchange(copies, held_d, "term")
+    col_ref[...] = col_scale
+    spread(col_scale, parts)
+
+    held_e[0] = tile_sums(tiles, col_ids, parts, sums, to_rows, True)
+    copies = start_exchange(held_e, "doc", *sems[8:10])
+    weight_ref[...] = row_scale * finish_exchange(copies, held_e, "doc")
+
+
+def scale_stage(tile_values, tile_rows, tile_cols, tile_count, start_block, identifier):
+    slots = tile_values.shape[0]
+    m, n = lax.axis_size("doc"), lax.axis_size("term")
+    slot = jnp.arange(slots, dtype=jnp.int32)
+    used = slot < tile_count[0, 0]
+    rows, cols = tile_rows[0], tile_cols[0]
+    cell = jnp.arange(RB * CB, dtype=jnp.int32)
+    found = ((rows * CB + cols)[None, :] == cell[:, None]) & used[None, :]
+    lookup = slots + jnp.sum(jnp.where(found, slot[None, :] - slots, 0), axis=1)
+    ids = jnp.concatenate([rows, cols, lookup])
+    live = jnp.stack([jnp.where(used, rows, RB), jnp.where(used, cols, CB)])
+    live = jnp.concatenate([live, live, live], axis=1)
+    vector = jax.ShapeDtypeStruct((RB, TILE), jnp.float32)
+    extra = -(-start_block.shape[1] // (8 * TILE)) * 8
+    square = jax.ShapeDtypeStruct((RB * TILE, CB * TILE), tile_values.dtype)
+    held = pltpu.VMEM((m, RB, TILE), jnp.float32)
     return pl.pallas_call(
-        dense_kernel,
+        scale_kernel,
         out_shape=[
-            jax.ShapeDtypeStruct((RB * TILE, CB * TILE), tile_values.dtype),
-            jax.ShapeDtypeStruct((CB * TILE, RB * TILE), tile_values.dtype),
+            vector,
+            vector,
+            vector,
+            jax.ShapeDtypeStruct((extra, TILE), jnp.float32),
+            square,
+            square,
         ],
-        in_specs=[SMEM, SMEM, SMEM, VMEM],
-        out_specs=[VMEM, VMEM],
-        compiler_params=pltpu.CompilerParams(vmem_limit_bytes=32 << 20),
-        name="dense",
-    )(tile_rows, tile_cols, tile_count, tile_values)
-
-
-def row_sums(matrix, scale):
-    return jnp.sum(matrix.astype(jnp.float32) * scale[None, :], axis=1)
-
-
-def col_sums(matrix, scale):
-    return jnp.sum(matrix.astype(jnp.float32) * scale[:, None], axis=0)
-
-
-def vector_sum(x, axis, identifier):
-    return all_sum(x.reshape(-1, TILE), axis, identifier).reshape(-1)
+        in_specs=[SMEM, VMEM, pl.BlockSpec(memory_space=pl.ANY), VMEM],
+        out_specs=[VMEM] * 6,
+        scratch_shapes=[
+            pltpu.VMEM((slots + 1, TILE, TILE), tile_values.dtype),
+            pltpu.VMEM((slots + 1, TILE, TILE), tile_values.dtype),
+            pltpu.VMEM((RB, 16, TILE), jnp.bfloat16),
+            pltpu.VMEM((slots, TILE), jnp.float32),
+            pltpu.VMEM((m, RB + extra, TILE), jnp.float32),
+            pltpu.VMEM((n, RB, TILE), jnp.float32),
+            held,
+            pltpu.VMEM((n, RB, TILE), jnp.float32),
+            held,
+            pltpu.SemaphoreType.DMA(()),
+        ]
+        + semaphores(m, m, n, n, m, m, n, n, m, m),
+        compiler_params=params(identifier),
+        name="scale",
+    )(ids, live, tile_values, start_block)
 
 
 def total_gram(block, extra, scale, identifier):
@@ -449,31 +551,19 @@
     terms_total = RB * TILE * lax.axis_size("term")
     docs_total = CB * TILE * lax.axis_size("doc")
     width = start_block.shape[1]
-    matrix, turned = dense_matrix(tile_values, tile_rows, tile_cols, tile_count)
-
-    mean_part = jnp.sum(start_block.astype(jnp.float32), axis=0)
-    col_flat = jnp.ones((CB * TILE,), jnp.float32)
-    for sweep_index in range(PASSES):
-        row_part = row_sums(matrix, col_flat)
-        if sweep_index == 0:
-            pad = jnp.zeros((8 * TILE - width % (8 * TILE),), jnp.float32)
-            joined = vector_sum(jnp.concatenate([row_part, mean_part, pad]), "doc", 0)
-            row_total = joined[: RB * TILE]
-            start_mean = joined[RB * TILE : RB * TILE + width]
-        else:
-            row_total = vector_sum(row_part, "doc", 1 + 2 * sweep_index)
-        row_flat = 1.0 / row_total
-        col_part = col_sums(matrix, row_flat)
-        col_flat = 1.0 / vector_sum(col_part, "term", 2 + 2 * sweep_index)
+    rows_out, cols_out, weights, means, matrix, turned = scale_stage(
+        tile_values, tile_rows, tile_cols, tile_count, start_block, 0
+    )
+    row_flat, col_flat, weight_flat = (x.reshape(-1) for x in (rows_out, cols_out, weights))
+    start_mean = means[: width // TILE].reshape(-1)
     scaled_start = (col_flat[:, None] * start_block.astype(jnp.float32)).astype(jnp.bfloat16)
     left_part = jnp.dot(matrix, scaled_start, preferred_element_type=jnp.float32)
     doc_size = lax.axis_size("doc")
     left_share = RB * TILE // doc_size
     left_offset = lax.axis_index("doc") * left_share
-    weight_sum = vector_sum(row_sums(matrix, col_flat), "doc", 16)
     left_raw = scatter_sum(left_part.reshape(doc_size, left_share, width), "doc", 17)
     row_rows = lax.dynamic_slice_in_dim(row_flat, left_offset, left_share)
-    row_weight = row_rows * lax.dynamic_slice_in_dim(weight_sum, left_offset, left_share)
+    row_weight = lax.dynamic_slice_in_dim(weight_flat, left_offset, left_share)
     left_block = (
         row_rows[:, None] * left_raw - row_weight[:, None] * start_mean[None, :] / docs_total
     )

time: 204 us -> 187 us (0.917)
  other arithmetic: 13.8 us -> 2.29 us
  Pallas kernels: 173 us -> 165 us
  matrix products: 8.81 us -> 11.8 us
    reduce_sum x6 -> x1, other arithmetic: 13 us -> 0.1 us  [scale_stage(): lookup = slots + jnp.sum(jnp.where(found, slot[None, :] - slots, 0), axis=1)]
    pallas_call x6 -> x1, Pallas kernels: 33.6 us -> 29 us  [scale_stage(): pl.pallas_call(scale_kernel, out_shape=[vector, vector, vector, jax.Shape...]
    dot_general x1, matrix products: 2.47 us -> 5.74 us  [per_device(): jnp.dot(turned, scaled_left, preferred_element_type=jnp.float32)]
    unnamed x24 -> x12, local copies, waits for them, and re-layouts: 7.91 us -> 6.32 us
where the time goes in v1:
time: 187 us
  Pallas kernels  165 us (88%)
  matrix products  11.8 us (6%)
  local copies, waits for them, and re-layouts  6.66 us (4%)
  other arithmetic  2.29 us (1%)
    pallas_call x2, Pallas kernels, gram_sum(): pl.pallas_call(gram_sum_kernel, out_shape=jax.ShapeDtypeStruct(x.shape, x...  39.9 us
    pallas_call x1, Pallas kernels, scale_stage(): pl.pallas_call(scale_kernel, out_shape=[vector, vector, vector, jax.Shape...  29 us
    pallas_call x1, Pallas kernels, scatter_sum(): pl.pallas_call(functools.partial(scatter_sum_kernel, axis), out_shape=jax...  24.6 us
    pallas_call x1, Pallas kernels, scatter_term(): pl.pallas_call(scatter_term_kernel, out_shape=jax.ShapeDtypeStruct(share,...  23.2 us
    pallas_call x2, Pallas kernels, factor_inverse(): pl.pallas_call(inverse_kernel, out_shape=jax.ShapeDtypeStruct(gram.shape,...  18.9 us
    pallas_call x1, Pallas kernels, gather(): pl.pallas_call(functools.partial(gather_kernel, axis), out_shape=jax.Shap...  14.9 us
    pallas_call x1, Pallas kernels, gather_term(): pl.pallas_call(gather_term_kernel, out_shape=jax.ShapeDtypeStruct((nz, 2)...  14.3 us
    unnamed x12, local copies, waits for them, and re-layouts  6.32 us

profile of v1, /device:TPU:0, one launch (start us, length us, event | category | flops | bytes accessed | tf_op | source)
XLA Modules:
  0.0 187.1 jit_solution(13549262634640747872)
XLA Ops:
  1.3 0.7 compare_select_fusion.1
  2.0 0.1 add_add_fusion.live
  2.1 0.1 select_reduce_fusion
  2.2 0.8 pad_add_fusion.ids
  2.9 0.0 copy-start
  2.9 1.4 copy-done
  4.3 0.0 copy-start.1
  4.3 1.2 copy-done.1
  5.6 0.0 copy-start.2
  5.6 29.0 %scale.1 = (f32[16,128]{1,0:T(8,128)S(1)}, f32[16,128]{1,0:T(8,128)S(1)}, f32[16,128]{1,0:T(8,128)S(1)}, f32[8,128]{1,0:T(8,128)S(1)}, bf16[2048,2048]{1,0:T(8,128)(2,1)S(1)}, /*index=5*/bf16[2048,2048]{1,0:T(8,128)(2,1)S(1)}) custom-call(s32[352]{0:T(512)S(1)} %pad_add_fusion.ids, s32[2,144]{1,0:T(2,128)S(1)} %add_add_fusion.live, ...), custom_call_target="tpu_custom_call" | custom-call | tf_op jit(solution)/shard_map/scale/pallas_call | solution.py:508
  34.6 0.0 copy-start.3
  34.6 0.0 copy-done.2
  34.6 2.6 %fusion = f32[2048,256]{1,0:T(8,128)S(1)} fusion(bf16[2048,2048]{1,0:T(8,128)(2,1)S(1)} %get-tuple-element.12, bf16[2048,256]{1,0:T(8,128)(2,1)S(1)} %copy-done.2, f32[2048]{0:T(1024)S(1)} %bitcast.49), kind=kOutput, calls=%fused_computation.6 | convolution fusion | flops 2149056512 | bytes 11542528 | tf_op jit(solution)/shard_map/dot_general | solution.py:560
  37.3 0.5 copy-done.3
  37.8 24.6 %scatter_sum.1 = f32[512,256]{1,0:T(8,128)S(1)} custom-call(f32[4,512,256]{2,1,0:T(8,128)S(1)} %bitcast.41), custom_call_target="tpu_custom_call" | custom-call | tf_op jit(solution)/shard_map/scatter_sum/pallas_call | solution.py:144
  62.4 0.1 dynamic_slice.9
  62.5 0.1 dynamic_slice.10
  62.6 1.3 convolution_multiply_fusion.1
  63.9 0.2 multiply_reduce_fusion
  64.1 0.1 pad.2.clone
  64.2 0.1 maximum_maximum_fusion
  64.3 17.7 %gram_sum.2 = f32[4,2,40,256]{3,2,1,0:T(8,128)S(1)} custom-call(f32[4,2,40,256]{3,2,1,0:T(8,128)S(1)} %bitcast.42), custom_call_target="tpu_custom_call" | custom-call | tf_op jit(solution)/shard_map/gram_sum/pallas_call | solution.py:335
  82.1 9.5 %inverse.2 = f32[256,256]{1,0:T(8,128)S(1)} custom-call(f32[256,256]{1,0:T(8,128)S(1)} %slice.12.gram_ref), custom_call_target="tpu_custom_call" | custom-call | tf_op jit(solution)/shard_map/inverse/pallas_call | solution.py:82
  91.6 0.3 fusion.2
  91.9 0.7 convolution_convert_fusion.x_ref
  92.6 14.9 %gather.1 = bf16[4,512,256]{2,1,0:T(8,128)(2,1)S(1)} custom-call(bf16[512,256]{1,0:T(8,128)(2,1)S(1)} %convolution_convert_fusion.x_ref), custom_call_target="tpu_custom_call" | custom-call | tf_op jit(solution)/shard_map/gather/pallas_call | solution.py:177
  107.5 0.3 multiply_convert_fusion
  107.9 5.7 %fusion.19.x_ref = f32[4,2,256,256]{3,2,1,0:T(8,128)S(1)} fusion(bf16[4,2,256,2048]{3,2,1,0:T(8,128)(2,1)} %bitcast.53, bf16[2048,256,1,1]{1,0,3,2:T(8,128)(2,1)S(1)} %bitcast.54), kind=kOutput, calls=%fused_computation.42 | convolution fusion | flops 2147483648 | bytes 11534336 | tf_op jit(solution)/shard_map/dot_general | solution.py:577
  113.6 23.2 %scatter_term.1 = f32[256,256]{1,0:T(8,128)S(1)} custom-call(f32[4,2,256,256]{3,2,1,0:T(8,128)S(1)} %fusion.19.x_ref), custom_call_target="tpu_custom_call" | custom-call | tf_op jit(solution)/shard_map/scatter_term/pallas_call | solution.py:281
  136.9 0.1 dynamic_slice.11
  136.9 0.7 convolution_multiply_fusion
  137.6 22.2 %gram_sum.3 = f32[4,2,32,256]{3,2,1,0:T(8,128)S(1)} custom-call(f32[4,2,32,256]{3,2,1,0:T(8,128)S(1)} %bitcast.46), custom_call_target="tpu_custom_call" | custom-call | tf_op jit(solution)/shard_map/gram_sum/pallas_call | solution.py:335
  159.8 9.4 %inverse.3 = f32[256,256]{1,0:T(8,128)S(1)} custom-call(f32[256,256]{1,0:T(8,128)S(1)} %bitcast.45), custom_call_target="tpu_custom_call" | custom-call | tf_op jit(solution)/shard_map/inverse/pallas_call | solution.py:82
  169.2 0.4 convolution_convert_fusion.1.x_ref
  169.6 14.3 %gather_term.1 = bf16[4,2,256,256]{3,2,1,0:T(8,128)(2,1)S(1)} custom-call(bf16[256,256]{1,0:T(8,128)(2,1)S(1)} %convolution_convert_fusion.1.x_ref), custom_call_target="tpu_custom_call" | custom-call | tf_op jit(solution)/shard_map/gather_term/pallas_call | solution.py:299
  183.9 0.6 copy.15
  184.6 0.6 copy.16
  185.2 1.0 copy.17
  186.1 1.0 copy.18
  (8 shorter events, 0.1 us)
Async XLA Ops:
  2.9 1.4 copy-start
  4.3 1.2 copy-start.1
  5.6 29.0 %copy-start.2 = (bf16[2048,256]{1,0:T(8,128)(2,1)S(1)}, bf16[2048,256]{1,0:T(8,128)(2,1)}, u32[]{:S(2)}) copy-start(bf16[2048,256]{1,0:T(8,128)(2,1)} %start_ref.1) | copy-start | bytes 3145732
  34.6 3.2 %copy-start.3 = (bf16[2048,2048]{1,0:T(8,128)(2,1)}, bf16[2048,2048]{1,0:T(8,128)(2,1)S(1)}, u32[]{:S(2)}) copy-start(bf16[2048,2048]{1,0:T(8,128)(2,1)S(1)} %get-tuple-element.15) | copy-start | bytes 25165828

commit v2 on v1

v2 whole, which is shorter than its diff:
```python
import math

import jax
import jax.numpy as jnp
from jax import lax
from jax.experimental import pallas as pl
from jax.experimental.pallas import tpu as pltpu
from jax.sharding import PartitionSpec as P

TILE = 128
RB = 16
CB = 16


PRECISE = lax.Precision.HIGHEST
MESH = pl.DeviceIdType.MESH
VMEM = pl.BlockSpec(memory_space=pltpu.VMEM)
SMEM = pl.BlockSpec(memory_space=pltpu.SMEM)


BLOCK = 64
GROUP = 8


def block_inverse(block, low, high):
    rows = lax.broadcasted_iota(jnp.int32, block.shape, 0)
    pivots = jnp.ones_like(block)
    for base in range(0, BLOCK, GROUP):
        factors = []
        for at in range(base, base + GROUP):
            column = jnp.broadcast_to(block[:, low + at : low + at + 1], block.shape)
            for past, factor in enumerate(factors):
                column = column - factor * column[base + past : base + past + 1, :]
            pivots = jnp.where(rows == at, column, pivots)
            ratio = column * (1.0 / column[at : at + 1, :])
            factors.append(jnp.where(rows > at, ratio, 0.0))
        for at, factor in enumerate(factors):
            block = block - factor * block[base + at : base + at + 1, :]
    lanes = lax.broadcasted_iota(jnp.int32, block.shape, 1)
    inside = (lanes >= high) & (lanes < high + BLOCK)
    return jnp.where(inside, block * lax.rsqrt(pivots), 0.0)


def inverse_kernel(gram_ref, o_ref, work):
    width = gram_ref.shape[0]
    work[:, :width] = gram_ref[...]
    rows = lax.broadcasted_iota(jnp.int32, (width, width), 0)
    lanes = lax.broadcasted_iota(jnp.int32, (width, width), 1)
    work[:, width:] = jnp.where(rows == lanes, 1.0, 0.0)
    for index in range(width // BLOCK):
        start = index * BLOCK
        near = start // TILE * TILE
        low = start - near
        high = TILE - BLOCK - low
        block = work[start : start + BLOCK, near : near + TILE]
        rows = lax.broadcasted_iota(jnp.int32, block.shape, 0)
        lanes = lax.broadcasted_iota(jnp.int32, block.shape, 1)
        inside = (lanes >= low) & (lanes < low + BLOCK)
        block = jnp.where(inside, block, jnp.where(lanes - high == rows, 1.0, 0.0))
        inverse = block_inverse(block, low, high)
        panel = work[start : start + BLOCK, :]
        solved = jnp.dot(
            inverse,
            jnp.concatenate([panel, panel], axis=0),
            precision=PRECISE,
            preferred_element_type=jnp.float32,
        )
        o_ref[start : start + BLOCK, :] = solved[:, width:]
        if start + BLOCK < width:
            update = lax.dot_general(
                solved[:, :width],
                solved,
                (((0,), (0,)), ((), ())),
                precision=PRECISE,
                preferred_element_type=jnp.float32,
            )
            work[start + BLOCK :, :] = work[start + BLOCK :, :] - update[start + BLOCK :, :]


def params(identifier):
    return pltpu.CompilerParams(
        collective_id=identifier, has_side_effects=True, vmem_limit_bytes=32 << 20
    )


def greet(axes):
    barrier = pltpu.get_barrier_semaphore()
    total = 0
    for axis in axes:
        n = lax.axis_size(axis)
        me = lax.axis_index(axis)
        for step in range(1, n):
            pl.semaphore_signal(
                barrier, inc=1, device_id={axis: lax.rem(me + step, n)}, device_id_type=MESH
            )
        total += n - 1
    pl.semaphore_wait(barrier, total)


def remote(source, target, send_sem, recv_sem, axis, peer):
    return pltpu.make_async_remote_copy(
        src_ref=source,
        dst_ref=target,
        send_sem=send_sem,
        recv_sem=recv_sem,
        device_id={axis: peer},
        device_id_type=MESH,
    )


def paired():
    n, me = lax.axis_size("term"), lax.axis_index("term")
    return n // 2, me // 2, lax.rem(me, 2)


def semaphores(*sizes):
    return [pltpu.SemaphoreType.DMA((size,)) for size in sizes]


def split3(value):
    high = value.astype(jnp.bfloat16)
    rest = value - high.astype(jnp.float32)
    middle = rest.astype(jnp.bfloat16)
    return high, middle, (rest - middle.astype(jnp.float32)).astype(jnp.bfloat16)


def spread(value, parts):
    high, middle, low = (part.astype(jnp.float32) for part in split3(value))
    blocks, depth, lanes = parts.shape
    rows = lax.broadcasted_iota(jnp.int32, (depth, lanes), 0)
    for block in range(blocks):
        at = slice(block, block + 1)
        picked = jnp.where(rows == 0, high[at], jnp.where(rows == 1, middle[at], low[at]))
        parts[block] = jnp.where(rows < 3, picked, 0.0).astype(jnp.bfloat16)


def tile_sums(tiles, source_ids, parts, sums, target, forward):
    slots = sums.shape[0]
    for slot in range(slots):
        product = lax.dot_general(
            parts[source_ids[slot]],
            tiles[slot],
            (((1,), (1 if forward else 0,)), ((), ())),
            preferred_element_type=jnp.float32,
        )
        sums[slot : slot + 1, :] = product[0:1] + product[1:2] + product[2:3]
    stacked = jnp.concatenate(split3(sums[...]), axis=0)
    return jnp.dot(target, stacked, preferred_element_type=jnp.float32)


def start_exchange(held, axis, send_sem, recv_sem):
    n, me = lax.axis_size(axis), lax.axis_index(axis)
    copies = []
    for step in range(1, n):
        copy = remote(
            held.at[0], held.at[step], send_sem.at[step], recv_sem.at[step], axis, lax.rem(me + step, n)
        )
        copy.start()
        copies.append(copy)
    return copies


def finish_exchange(copies, held, axis):
    n, me = lax.axis_size(axis), lax.axis_index(axis)
    for copy in copies:
        copy.wait()
    total = held[me]
    for source in range(1, n):
        total = total + held[lax.rem(me - source + n, n)]
    return total


def scale_kernel(
    ids,
    live,
    tiles_hbm,
    start_ref,
    row_ref,
    col_ref,
    weight_ref,
    mean_ref,
    dense_ref,
    turned_ref,
    tiles,
    flipped,
    parts,
    sums,
    held_a,
    held_b,
    held_c,
    held_d,
    held_e,
    load_sem,
    *sems,
):
    slots = tiles_hbm.shape[0]
    load = pltpu.make_async_copy(tiles_hbm, tiles.at[pl.ds(0, slots)], load_sem)
    load.start()
    greet(("term", "doc"))
    tiles[slots] = jnp.zeros(tiles.shape[1:], tiles.dtype)
    flipped[slots] = jnp.zeros(tiles.shape[1:], tiles.dtype)
    blocks = row_ref.shape[0]
    places = lax.broadcasted_iota(jnp.int32, (blocks, live.shape[1]), 0)
    to_rows = jnp.where(places == live[0:1, :], 1.0, 0.0).astype(jnp.bfloat16)
    to_cols = jnp.where(places == live[1:2, :], 1.0, 0.0).astype(jnp.bfloat16)
    row_ids, col_ids = ids.at[pl.ds(0, slots)], ids.at[pl.ds(slots, slots)]

    def build(out_ref, source, turn):
        def place_row(outer, carry):
            at = pl.multiple_of(outer * TILE, TILE)
            for inner in range(blocks):
                place = inner * blocks + outer if turn else outer * blocks + inner
                tile = source[ids[2 * slots + place]]
                out_ref[pl.ds(at, TILE), inner * TILE : (inner + 1) * TILE] = tile
            return carry

        lax.fori_loop(0, blocks, place_row, 0)

    def flip(slot, carry):
        flipped[slot] = tiles[slot].T
        return carry

    spread(jnp.ones(row_ref.shape, jnp.float32), parts)
    mean = jnp.sum(start_ref[...].astype(jnp.float32), axis=0, keepdims=True)
    load.wait()
    held_a[0, :blocks, :] = tile_sums(tiles, col_ids, parts, sums, to_rows, True)
    extra = held_a.shape[1] - blocks
    pieces = [mean[:, at : at + TILE] for at in range(0, mean.shape[1], TILE)]
    pieces.append(jnp.zeros((extra - len(pieces), TILE), jnp.float32))
    held_a[0, blocks:, :] = jnp.concatenate(pieces, axis=0)
    copies = start_exchange(held_a, "doc", *sems[0:2])
    build(dense_ref, tiles, False)
    joined = finish_exchange(copies, held_a, "doc")
    mean_ref[...] = joined[blocks:, :]
    spread(1.0 / joined[:blocks], parts)

    held_b[0] = tile_sums(tiles, row_ids, parts, sums, to_cols, False)
    copies = start_exchange(held_b, "term", *sems[2:4])
    lax.fori_loop(0, slots, flip, 0)
    spread(1.0 / finish_exchange(copies, held_b, "term"), parts)

    held_c[0] = tile_sums(tiles, col_ids, parts, sums, to_rows, True)
    copies = start_exchange(held_c, "doc", *sems[4:6])
    build(turned_ref, flipped, True)
    row_scale = 1.0 / finish_exchange(copies, held_c, "doc")
    row_ref[...] = row_scale
    spread(row_scale, parts)

    held_d[0] = tile_sums(tiles, row_ids, parts, sums, to_cols, False)
    copies = start_exchange(held_d, "term", *sems[6:8])
    col_scale = 1.0 / finish_exchange(copies, held_d, "term")
    col_ref[...] = col_scale
    spread(col_scale, parts)

    held_e[0] = tile_sums(tiles, col_ids, parts, sums, to_rows, True)
    copies = start_exchange(held_e, "doc", *sems[8:10])
    weight_ref[...] = row_scale * finish_exchange(copies, held_e, "doc")


def scale_stage(tile_values, tile_rows, tile_cols, tile_count, start_block, identifier):
    slots = tile_values.shape[0]
    m, n = lax.axis_size("doc"), lax.axis_size("term")
    slot = jnp.arange(slots, dtype=jnp.int32)
    used = slot < tile_count[0, 0]
    rows, cols = tile_rows[0], tile_cols[0]
    cell = jnp.arange(RB * CB, dtype=jnp.int32)
    found = ((rows * CB + cols)[None, :] == cell[:, None]) & used[None, :]
    lookup = slots + jnp.sum(jnp.where(found, slot[None, :] - slots, 0), axis=1)
    ids = jnp.concatenate([rows, cols, lookup])
    live = jnp.stack([jnp.where(used, rows, RB), jnp.where(used, cols, CB)])
    live = jnp.concatenate([live, live, live], axis=1)
    vector = jax.ShapeDtypeStruct((RB, TILE), jnp.float32)
    extra = -(-start_block.shape[1] // (8 * TILE)) * 8
    square = jax.ShapeDtypeStruct((RB * TILE, CB * TILE), tile_values.dtype)
    held = pltpu.VMEM((m, RB, TILE), jnp.float32)
    return pl.pallas_call(
        scale_kernel,
        out_shape=[
            vector,
            vector,
            vector,
            jax.ShapeDtypeStruct((extra, TILE), jnp.float32),
            square,
            square,
        ],
        in_specs=[SMEM, VMEM, pl.BlockSpec(memory_space=pl.ANY), VMEM],
        out_specs=[VMEM] * 6,
        scratch_shapes=[
            pltpu.VMEM((slots + 1, TILE, TILE), tile_values.dtype),
            pltpu.VMEM((slots + 1, TILE, TILE), tile_values.dtype),
            pltpu.VMEM((RB, 16, TILE), jnp.bfloat16),
            pltpu.VMEM((slots, TILE), jnp.float32),
            pltpu.VMEM((m, RB + extra, TILE), jnp.float32),
            pltpu.VMEM((n, RB, TILE), jnp.float32),
            held,
            pltpu.VMEM((n, RB, TILE), jnp.float32),
            held,
            pltpu.SemaphoreType.DMA(()),
        ]
        + semaphores(m, m, n, n, m, m, n, n, m, m),
        compiler_params=params(identifier),
        name="scale",
    )(ids, live, tile_values, start_block)


CODES = 32760.0
OCTAVE = 256.0 / math.log(2.0)


def encode(value):
    rows, lanes = value.shape
    groups = value.reshape(rows // 8, 8, lanes)
    top = jnp.maximum(jnp.max(jnp.abs(groups), axis=0), 1e-30)
    level = jnp.ceil(jnp.log(top) * OCTAVE)
    codes = jnp.round(groups * (jnp.exp(level * (-1.0 / OCTAVE)) * CODES))
    whole = jnp.concatenate([codes.reshape(rows, lanes), level, level], axis=0)
    return whole.astype(jnp.int32).astype(jnp.int16)


def decode(block):
    rows, lanes = block.shape[0] - 16, block.shape[1]
    value = block.astype(jnp.int32).astype(jnp.float32)
    scale = jnp.exp(value[rows : rows + 8] * (1.0 / OCTAVE)) * (1.0 / CODES)
    return (value[:rows].reshape(rows // 8, 8, lanes) * scale[None]).reshape(rows, lanes)


def grid_of(n):
    nx = int(math.isqrt(n))
    while n % nx:
        nx -= 1
    return nx, n // nx


def turn_out(vector_ref, block, lanes):
    row = jnp.broadcast_to(vector_ref[pl.ds(block, 1), :], (TILE, TILE))
    column = row.T
    return jnp.concatenate([column] * (lanes // TILE), axis=1)


def precise(a, b, dims):
    return lax.dot_general(
        a, b, (dims, ((), ())), precision=PRECISE, preferred_element_type=jnp.float32
    )


def gram_steps(x_ref, o_ref, near, mid, far, second, part, done, *sems):
    nz, z, c = paired()
    m, my = lax.axis_size("doc"), lax.axis_index("doc")
    rows = part.shape[0]
    sibling = 2 * z + 1 - c

    def share(ref, there, core):
        return ref.at[pl.ds(pl.multiple_of((2 * there + core) * rows, 8), rows)]

    near_copies, far_copies = {}, []
    for step in list(range(1, nz)) + [0]:
        there = lax.rem(z + step, nz)
        near_copies[step] = remote(
            share(x_ref, there, 1 - c), near.at[step], sems[0].at[step], sems[1].at[step], "term", sibling
        )
        near_copies[step].start()
    yield
    for step in range(1, nz):
        near_copies[step].wait()
        there = lax.rem(z + step, nz)
        mid[step] = share(x_ref, there, c)[...] + near[step]
        copy = remote(
            mid.at[step], far.at[step], sems[2].at[step], sems[3].at[step], "term", 2 * there + c
        )
        copy.start()
        far_copies.append(copy)
    near_copies[0].wait()
    part[...] = share(x_ref, z, c)[...] + near[0]
    yield
    for step, copy in enumerate(far_copies):
        copy.wait()
        part[...] += far[step + 1]
    copies = []
    for step in range(1, m):
        copy = remote(
            part, second.at[step], sems[4].at[step], sems[5].at[step], "doc", lax.rem(my + step, m)
        )
        copy.start()
        copies.append(copy)
    second[0] = part[...]
    yield
    for copy in copies:
        copy.wait()
    total = second[my]
    for source in range(1, m):
        total = total + second[lax.rem(my - source + m, m)]
    done[...] = total
    far_copies = []
    here = share(o_ref, z, c)
    for step in range(1, nz):
        copy = remote(
            done, here, sems[6].at[step], sems[7].at[step], "term", 2 * lax.rem(z + step, nz) + c
        )
        copy.start()
        far_copies.append(copy)
    copy = remote(done, here, sems[8].at[0], sems[9].at[0], "term", sibling)
    copy.start()
    near_copies = [copy]
    here[...] = total
    yield
    for step in range(1, nz):
        far_copies[step - 1].wait()
        there = share(o_ref, lax.rem(z - step + nz, nz), c)
        copy = remote(there, there, sems[8].at[step], sems[9].at[step], "term", sibling)
        copy.start()
        near_copies.append(copy)
    for copy in near_copies:
        copy.wait()


def gram_scratch(width):
    nz, m = lax.axis_size("term") // 2, lax.axis_size("doc")
    rows = width // (2 * nz)
    spread_over = pltpu.VMEM((nz, rows, width), jnp.float32)
    alone = pltpu.VMEM((rows, width), jnp.float32)
    whole = pltpu.VMEM((width, width), jnp.float32)
    return [whole, whole] + [spread_over] * 3 + [pltpu.VMEM((m, rows, width), jnp.float32), alone, alone] + semaphores(
        nz, nz, nz, nz, m, m, nz, nz, nz, nz
    )


GRAM_REFS = 18


def basis_kernel(
    matrix,
    turned,
    start_ref,
    row_ref,
    col_ref,
    weight_ref,
    mean_ref,
    left_out,
    right_out,
    row_turn,
    col_turn,
    scaled,
    partial,
    send_a,
    recv_a,
    send_b,
    recv_b,
    gathered,
    factor,
    near_send,
    near_recv,
    far_send,
    far_recv,
    right_parts,
    inverse_ref,
    work,
    *rest,
):
    left_gram, right_gram = rest[:GRAM_REFS], rest[GRAM_REFS : 2 * GRAM_REFS]
    sems = rest[2 * GRAM_REFS :]
    n, m = lax.axis_size("term"), lax.axis_size("doc")
    nz, z, c = paired()
    doc = lax.axis_index("doc")
    nx, ny = grid_of(m)
    x, y = lax.rem(doc, nx), doc // nx
    terms, width = left_out.shape
    docs = right_out.shape[0]
    share, piece = terms // m, docs // n
    docs_total = docs * m

    greet(("term", "doc"))

    def axes(flow):
        return (x, nx, y, ny) if flow == 0 else (y, ny, x, nx)

    def device(flow, first, second):
        return second * nx + first if flow == 0 else first * nx + second

    def lanes(flow):
        return slice(flow * TILE, (flow + 1) * TILE)

    def prepare(block, carry):
        at = pl.ds(pl.multiple_of(block * TILE, TILE), TILE)
        column = turn_out(col_ref, block, width)
        col_turn[at, :] = column[:, :TILE]
        scaled[at, :] = (column * start_ref[at, :].astype(jnp.float32)).astype(jnp.bfloat16)
        row_turn[at, :] = turn_out(row_ref, block, TILE)
        return carry

    lax.fori_loop(0, docs // TILE, prepare, 0)

    steps = [(dx, dy) for dx in range(nx) for dy in range(ny)]
    steps.sort(key=lambda s: -((s[0] > 0) + (s[1] > 0)))
    copies_a, copies_b = {}, {}
    for dx, dy in steps:
        target = lax.rem(y + dy, ny) * nx + lax.rem(x + dx, nx)
        at = pl.ds(pl.multiple_of(target * share, share), share)
        product = jnp.dot(matrix[at, :], scaled[...], preferred_element_type=jnp.float32)
        column = row_turn[at, :]
        product = product * jnp.concatenate([column] * (width // TILE), axis=1)
        partial[dy * nx + dx] = product
        for flow in range(2):
            a, n1, b, n2 = axes(flow)
            s1, s2 = (dx, dy) if flow == 0 else (dy, dx)
            if s1 == 0:
                continue
            slot = s1 * n2 + s2
            send_a[flow, slot] = encode(product[:, lanes(flow)])
            copies_a[flow, s1, s2] = remote(
                send_a.at[flow, slot],
                recv_a.at[flow, slot],
                sems[0].at[flow, slot],
                sems[1].at[flow, slot],
                "doc",
                device(flow, lax.rem(a + s1, n1), b),
            )
            copies_a[flow, s1, s2].start()

    def own(flow, s2):
        dx, dy = (0, s2) if flow == 0 else (s2, 0)
        return partial[dy * nx + dx, :, lanes(flow)]

    def landed(flow, s2):
        a, n1, b, n2 = axes(flow)
        total = own(flow, s2)
        for s1 in range(1, n1):
            copies_a[flow, s1, s2].wait()
            total = total + decode(recv_a[flow, s1 * n2 + s2])
        return total

    for flow in range(2):
        a, n1, b, n2 = axes(flow)
        for s2 in range(1, n2):
            send_b[flow, s2] = encode(landed(flow, s2))
            copies_b[flow, s2] = remote(
                send_b.at[flow, s2],
                recv_b.at[flow, s2],
                sems[2].at[flow, s2],
                sems[3].at[flow, s2],
                "doc",
                device(flow, a, lax.rem(b + s2, n2)),
            )
            copies_b[flow, s2].start()

    blocks_of_share = share // TILE
    weight = jnp.concatenate(
        [turn_out(weight_ref, doc * blocks_of_share + k, TILE) for k in range(blocks_of_share)], axis=0
    )
    copies_c, copies_d = {}, {}
    left = []
    for flow in range(2):
        a, n1, b, n2 = axes(flow)
        total = landed(flow, 0)
        for s2 in range(1, n2):
            copies_b[flow, s2].wait()
            total = total + decode(recv_b[flow, s2])
        total = total - weight * (mean_ref[flow : flow + 1, :] * (1.0 / docs_total))
        left.append(total)
        gathered[flow, doc] = encode(total)
        for s1 in range(1, n1):
            copies_c[flow, s1] = remote(
                gathered.at[flow, doc],
                gathered.at[flow, doc],
                sems[4].at[flow, s1],
                sems[5].at[flow, s1],
                "doc",
                device(flow, lax.rem(a + s1, n1), b),
            )
            copies_c[flow, s1].start()

    left_share = jnp.concatenate(left, axis=1)
    gram_in, gram_out = left_gram[:2]
    gram_in[...] = precise(left_share, left_share, ((0,), (0,))) * (1.0 / (terms * n))
    for k in range(width // TILE):
        weighted = jnp.sum(weight * left[k], axis=0, keepdims=True)
        gram_in[width - width // TILE + k : width - width // TILE + k + 1, :TILE] = weighted
    left_steps = gram_steps(*left_gram)
    next(left_steps)

    for flow in range(2):
        a, n1, b, n2 = axes(flow)
        for s1 in range(n1):
            if s1:
                copies_c[flow, s1].wait()
            source = device(flow, lax.rem(a - s1 + n1, n1), b)
            for s2 in range(1, n2):
                copies_d[flow, s1, s2] = remote(
                    gathered.at[flow, source],
                    gathered.at[flow, source],
                    sems[6].at[flow, s1 * n2 + s2],
                    sems[7].at[flow, s1 * n2 + s2],
                    "doc",
                    device(flow, a, lax.rem(b + s2, n2)),
                )
                copies_d[flow, s1, s2].start()
    next(left_steps)
    next(left_steps)
    for copy in copies_d.values():
        copy.wait()

    def unpack(block, carry):
        at = pl.ds(pl.multiple_of(block * share, share), share)
        for flow in range(2):
            value = decode(gathered[flow, block]) * row_turn[at, :]
            high = value.astype(jnp.bfloat16)
            factor[at, lanes(flow)] = high
            low = slice(width + flow * TILE, width + (flow + 1) * TILE)
            factor[at, low] = (value - high.astype(jnp.float32)).astype(jnp.bfloat16)
        return carry

    lax.fori_loop(0, m, unpack, 0)

    def right_product(there, core):
        at = pl.ds(pl.multiple_of((2 * there + core) * piece, piece), piece)
        both = jnp.dot(turned[at, :], factor[...], preferred_element_type=jnp.float32)
        column = col_turn[at, :]
        return (both[:, :width] + both[:, width:]) * jnp.concatenate(
            [column] * (width // TILE), axis=1
        )

    sibling = 2 * z + 1 - c
    near_copies, far_copies = {}, {}
    order = list(range(1, nz)) + [0]
    for step in order:
        near_send[step] = right_product(lax.rem(z + step, nz), 1 - c)
        near_copies[step] = remote(
            near_send.at[step], near_recv.at[step], sems[8].at[step], sems[9].at[step], "term", sibling
        )
        near_copies[step].start()
    next(left_steps)
    for step in order:
        there = lax.rem(z + step, nz)
        product = right_product(there, c)
        near_copies[step].wait()
        product = product + near_recv[step]
        if step == 0:
            own_right = product
            continue
        far_send[step] = encode(product)
        far_copies[step] = remote(
            far_send.at[step], far_recv.at[step], sems[10].at[step], sems[11].at[step], "term", 2 * there + c
        )
        far_copies[step].start()
    near_send[0] = own_right
    for _ in left_steps:
        pass
    inverse_kernel(gram_out, inverse_ref, work)
    whiten = inverse_ref[...]

    def finish_left(block, carry):
        at = pl.ds(pl.multiple_of(block * share, share), share)
        value = jnp.concatenate([decode(gathered[flow, block]) for flow in range(2)], axis=1)
        left_out[at, :] = precise(value, inverse_ref[...], ((1,), (1,))).astype(jnp.bfloat16)
        return carry

    lax.fori_loop(0, m, finish_left, 0)
    pieces = width // TILE
    weighted = jnp.concatenate(
        [gram_out[width - pieces + k : width - pieces + k + 1, :TILE] for k in range(pieces)], axis=1
    )
    lean = precise(jnp.broadcast_to(weighted, (8, width)), whiten, ((1,), (1,)))[0:1]
    total = near_send[0]
    for step in range(1, nz):
        far_copies[step].wait()
        total = total + decode(far_recv[step])
    block = precise(total, inverse_ref[...], ((1,), (1,))) - lean * (1.0 / docs_total)

    me = 2 * z + c
    right_parts[me] = encode(block)
    gram_in, gram_out = right_gram[:2]
    gram_in[...] = precise(block, block, ((0,), (0,))) * (1.0 / docs_total)
    for _ in gram_steps(*right_gram):
        pass
    far_copies = []
    for step in range(1, nz):
        copy = remote(
            right_parts.at[me],
            right_parts.at[me],
            sems[12].at[step],
            sems[13].at[step],
            "term",
            2 * lax.rem(z + step, nz) + c,
        )
        copy.start()
        far_copies.append(copy)
    copy = remote(
        right_parts.at[me], right_parts.at[me], sems[14].at[0], sems[15].at[0], "term", sibling
    )
    copy.start()
    near_copies = [copy]
    inverse_kernel(gram_out, inverse_ref, work)

    def finish_right(t):
        at = pl.ds(pl.multiple_of(t * piece, piece), piece)
        right_out[at, :] = precise(
            decode(right_parts[t]), inverse_ref[...], ((1,), (1,))
        ).astype(jnp.bfloat16)

    finish_right(me)
    for step in range(1, nz):
        far_copies[step - 1].wait()
        t = 2 * lax.rem(z - step + nz, nz) + c
        copy = remote(
            right_parts.at[t], right_parts.at[t], sems[14].at[step], sems[15].at[step], "term", sibling
        )
        copy.start()
        near_copies.append(copy)
        finish_right(t)
    for step, copy in enumerate(near_copies):
        copy.wait()
        finish_right(2 * lax.rem(z - step + nz, nz) + 1 - c)


def basis_stage(matrix, turned, start_block, row, col, weight, mean, identifier):
    n, m = lax.axis_size("term"), lax.axis_size("doc")
    nz = n // 2
    terms, docs, width = matrix.shape[0], turned.shape[0], start_block.shape[1]
    share, piece = terms // m, docs // n
    wide = max(grid_of(m))
    int16, f32, bf16 = jnp.int16, jnp.float32, jnp.bfloat16
    coded = pltpu.VMEM((2, m, share + 16, TILE), int16)
    coded_b = pltpu.VMEM((2, wide, share + 16, TILE), int16)
    far = pltpu.VMEM((nz, piece + 16, width), int16)
    near = pltpu.VMEM((nz, piece, width), f32)
    pairs = [pltpu.SemaphoreType.DMA((2, size)) for size in (m, m, wide, wide, wide, wide, m, m)]
    return pl.pallas_call(
        basis_kernel,
        out_shape=[
            jax.ShapeDtypeStruct((terms, width), bf16),
            jax.ShapeDtypeStruct((docs, width), bf16),
        ],
        in_specs=[VMEM] * 7,
        out_specs=[VMEM] * 2,
        scratch_shapes=[
            pltpu.VMEM((terms, TILE), f32),
            pltpu.VMEM((docs, TILE), f32),
            pltpu.VMEM((docs, width), bf16),
            pltpu.VMEM((m, share, width), f32),
            coded,
            coded,
            coded_b,
            coded_b,
            coded,
            pltpu.VMEM((terms, 2 * width), bf16),
            near,
            near,
            far,
            far,
            pltpu.VMEM((n, piece + 16, width), int16),
            pltpu.VMEM((width, width), f32),
            pltpu.VMEM((width, 2 * width), f32),
        ]
        + gram_scratch(width)
        + gram_scratch(width)
        + pairs
        + semaphores(*[nz] * 8),
        compiler_params=pltpu.CompilerParams(
            collective_id=identifier, has_side_effects=True, vmem_limit_bytes=58 << 20
        ),
        name="basis",
    )(matrix, turned, start_block, row, col, weight, mean)


def per_device(tile_values, tile_rows, tile_cols, tile_count, start_block):
    rows_out, cols_out, weights, means, matrix, turned = scale_stage(
        tile_values, tile_rows, tile_cols, tile_count, start_block, 0
    )
    left_basis, right_basis = basis_stage(
        matrix, turned, start_block, rows_out, cols_out, weights, means, 1
    )
    return (rows_out.reshape(-1), cols_out.reshape(-1), left_basis, right_basis)


def solution(mesh):
    placed = (
        P("term", "doc", None),
        P("term", "doc"),
        P("term", "doc"),
        P("term", "doc"),
        P("doc", None),
    )
    return jax.shard_map(
        per_device,
        mesh=mesh,
        in_specs=placed,
        out_specs=(P("term"), P("doc"), P("term", None), P("doc", None)),
        check_vma=False,
    )
```

time: 187 us -> 144 us (0.77)
  Pallas kernels: 165 us -> 123 us
  matrix products: 11.8 us -> 0 us
  local copies, waits for them, and re-layouts: 6.66 us -> 16.6 us
    pallas_call x8 -> x1, Pallas kernels: 136 us -> 94.2 us  [basis_stage(): pl.pallas_call(basis_kernel, out_shape=[jax.ShapeDtypeStruct((terms, widt...]
    dot_general x7 -> x0, matrix products: 11.8 us -> none  [the longest x1 5.74 us: per_device(): jnp.dot(turned, scaled_left, preferred_element_type=jnp.float32)]
    unnamed x12 -> x24, local copies, waits for them, and re-layouts: 6.32 us -> 16.6 us
where the time goes in v2:
time: 144 us; the launch traced here: 143 us
  Pallas kernels  123 us (85%)
  local copies, waits for them, and re-layouts  16.6 us (12%)
  other arithmetic  1.62 us (1%)
    pallas_call x1, Pallas kernels, basis_stage(): pl.pallas_call(basis_kernel, out_shape=[jax.ShapeDtypeStruct((terms, widt...  94.2 us
    pallas_call x1, Pallas kernels, scale_stage(): pl.pallas_call(scale_kernel, out_shape=[vector, vector, vector, jax.Shape...  29 us
    unnamed x24, local copies, waits for them, and re-layouts  16.6 us

profile of v2, /device:TPU:0, one launch (start us, length us, event | category | flops | bytes accessed | tf_op | source)
XLA Modules:
  0.0 142.7 jit_solution(1893527891919895341)
XLA Ops:
  1.3 0.7 compare_select_fusion.1
  2.0 0.1 select_reduce_fusion
  2.1 0.8 pad_add_fusion.ids
  2.8 0.1 add_add_fusion.live
  2.9 0.0 copy-start.2
  2.9 1.2 copy-done.2
  4.1 0.0 copy-start.3
  4.2 1.4 copy-done.3
  5.6 29.0 %scale.1 = (f32[16,128]{1,0:T(8,128)S(1)}, f32[16,128]{1,0:T(8,128)S(1)}, f32[16,128]{1,0:T(8,128)S(1)}, f32[8,128]{1,0:T(8,128)S(1)}, bf16[2048,2048]{1,0:T(8,128)(2,1)S(1)}, /*index=5*/bf16[2048,2048]{1,0:T(8,128)(2,1)S(1)}) custom-call(s32[352]{0:T(512)S(1)} %pad_add_fusion.ids, s32[2,144]{1,0:T(2,128)S(1)} %add_add_fusion.live, ...), custom_call_target="tpu_custom_call" | custom-call | tf_op jit(solution)/shard_map/scale/pallas_call | solution.py:276
  34.6 0.0 copy-start
  34.6 3.2 %copy-done = bf16[2048,2048]{1,0:T(8,128)(2,1)} copy-done((bf16[2048,2048]{1,0:T(8,128)(2,1)}, bf16[2048,2048]{1,0:T(8,128)(2,1)S(1)}, u32[]{:S(2)}) %copy-start) | copy-done | bytes 8388632
  37.8 0.0 copy-start.1
  37.8 3.2 %copy-done.1 = bf16[2048,2048]{1,0:T(8,128)(2,1)} copy-done((bf16[2048,2048]{1,0:T(8,128)(2,1)}, bf16[2048,2048]{1,0:T(8,128)(2,1)S(1)}, u32[]{:S(2)}) %copy-start.1) | copy-done | bytes 8388632
  41.0 0.0 copy-start.4
  41.0 0.6 copy-done.4
  41.6 0.0 copy-start.8
  41.6 0.6 copy-done.8
  42.2 0.0 copy-start.6
  42.2 0.0 copy-start.9
  42.2 0.6 copy-done.6
  42.8 0.0 copy-done.9
  42.8 0.0 copy-start.7
  42.8 0.0 copy-start.5
  42.9 94.2 %basis.1 = (bf16[2048,256]{1,0:T(8,128)(2,1)}, bf16[2048,256]{1,0:T(8,128)(2,1)}) custom-call(bf16[2048,2048]{1,0:T(8,128)(2,1)} %copy-done, bf16[2048,2048]{1,0:T(8,128)(2,1)} %copy-done.1, bf16[2048,256]{1,0:T(8,128)(2,1)} %start_ref.3, f32[16,128]{1,0:T(8,128)} %copy-done.6, f32[16,128]{1,0:T(8,128)} %copy-done.4, f32[16,128]{1,0:T(8,128)} %copy-done.8, ...), custom_call_target="tpu_custom_call" | custom-call | tf_op jit(solution)/shard_map/basis/pallas_call | solution.py:726
  137.0 0.0 copy-done.7
  137.0 0.6 copy.14
  137.6 0.0 copy-done.5
  137.6 0.6 copy.15
  138.2 2.3 %copy.16 = bf16[2048,256]{1,0:T(8,128)(2,1)} copy(bf16[2048,256]{1,0:T(8,128)(2,1)} %get-tuple-element.29) | data formatting | bytes 2097152
  140.5 2.3 %copy.17 = bf16[2048,256]{1,0:T(8,128)(2,1)} copy(bf16[2048,256]{1,0:T(8,128)(2,1)} %get-tuple-element.30) | data formatting | bytes 2097152
  (3 shorter events, 0.0 us)
Async XLA Ops:
  2.9 1.2 copy-start.2
  4.1 1.4 copy-start.3
  34.6 3.2 %copy-start = (bf16[2048,2048]{1,0:T(8,128)(2,1)}, bf16[2048,2048]{1,0:T(8,128)(2,1)S(1)}, u32[]{:S(2)}) copy-start(bf16[2048,2048]{1,0:T(8,128)(2,1)S(1)} %get-tuple-element.14.matrix) | copy-start | bytes 25165828
  37.8 3.2 %copy-start.1 = (bf16[2048,2048]{1,0:T(8,128)(2,1)}, bf16[2048,2048]{1,0:T(8,128)(2,1)S(1)}, u32[]{:S(2)}) copy-start(bf16[2048,2048]{1,0:T(8,128)(2,1)S(1)} %get-tuple-element.15.turned) | copy-start | bytes 25165828
  41.0 0.6 copy-start.4
  41.6 0.6 copy-start.8
  42.2 0.6 copy-start.6
  42.2 0.6 copy-start.9
  42.8 94.2 %copy-start.7 = (f32[16,128]{1,0:T(8,128)S(1)}, f32[16,128]{1,0:T(8,128)}, u32[]{:S(2)}) copy-start(f32[16,128]{1,0:T(8,128)} %copy-done.6) | copy-start | bytes 24580
  42.8 94.8 %copy-start.5 = (f32[16,128]{1,0:T(8,128)S(1)}, f32[16,128]{1,0:T(8,128)}, u32[]{:S(2)}) copy-start(f32[16,128]{1,0:T(8,128)} %copy-done.4) | copy-start | bytes 24580

commit v3 on v2

--- a/solution.py
+++ b/solution.py
@@ -77,12 +77,6 @@
             work[start + BLOCK :, :] = work[start + BLOCK :, :] - update[start + BLOCK :, :]
 
 
-def params(identifier):
-    return pltpu.CompilerParams(
-        collective_id=identifier, has_side_effects=True, vmem_limit_bytes=32 << 20
-    )
-
-
 def greet(axes):
     barrier = pltpu.get_barrier_semaphore()
     total = 0
@@ -170,17 +164,19 @@
     return total
 
 
-def scale_kernel(
-    ids,
+def scale_phase(
+    ids_hbm,
     live,
     tiles_hbm,
-    start_ref,
+    start_hbm,
     row_ref,
     col_ref,
     weight_ref,
     mean_ref,
+    start_ref,
     dense_ref,
     turned_ref,
+    ids,
     tiles,
     flipped,
     parts,
@@ -194,8 +190,13 @@
     *sems,
 ):
     slots = tiles_hbm.shape[0]
-    load = pltpu.make_async_copy(tiles_hbm, tiles.at[pl.ds(0, slots)], load_sem)
-    load.start()
+    loads = [
+        pltpu.make_async_copy(ids_hbm, ids, load_sem.at[0]),
+        pltpu.make_async_copy(start_hbm, start_ref, load_sem.at[1]),
+        pltpu.make_async_copy(tiles_hbm, tiles.at[pl.ds(0, slots)], load_sem.at[2]),
+    ]
+    for load in loads:
+        load.start()
     greet(("term", "doc"))
     tiles[slots] = jnp.zeros(tiles.shape[1:], tiles.dtype)
     flipped[slots] = jnp.zeros(tiles.shape[1:], tiles.dtype)
@@ -221,8 +222,10 @@
         return carry
 
     spread(jnp.ones(row_ref.shape, jnp.float32), parts)
+    loads[0].wait()
+    loads[1].wait()
     mean = jnp.sum(start_ref[...].astype(jnp.float32), axis=0, keepdims=True)
-    load.wait()
+    loads[2].wait()
     held_a[0, :blocks, :] = tile_sums(tiles, col_ids, parts, sums, to_rows, True)
     extra = held_a.shape[1] - blocks
     pieces = [mean[:, at : at + TILE] for at in range(0, mean.shape[1], TILE)]
@@ -237,7 +240,8 @@
     held_b[0] = tile_sums(tiles, row_ids, parts, sums, to_cols, False)
     copies = start_exchange(held_b, "term", *sems[2:4])
     lax.fori_loop(0, slots, flip, 0)
-    spread(1.0 / finish_exchange(copies, held_b, "term"), parts)
+    total = finish_exchange(copies, held_b, "term")
+    spread(1.0 / total, parts)
 
     held_c[0] = tile_sums(tiles, col_ids, parts, sums, to_rows, True)
     copies = start_exchange(held_c, "doc", *sems[4:6])
@@ -253,54 +257,51 @@
     spread(col_scale, parts)
 
     held_e[0] = tile_sums(tiles, col_ids, parts, sums, to_rows, True)
-    copies = start_exchange(held_e, "doc", *sems[8:10])
-    weight_ref[...] = row_scale * finish_exchange(copies, held_e, "doc")
-
-
-def scale_stage(tile_values, tile_rows, tile_cols, tile_count, start_block, identifier):
-    slots = tile_values.shape[0]
+    return start_exchange(held_e, "doc", *sems[8:10])
+
+
+def scale_scratch(terms, docs, width, slots, kind):
     m, n = lax.axis_size("doc"), lax.axis_size("term")
+    vector = pltpu.VMEM((RB, TILE), jnp.float32)
+    extra = -(-width // (8 * TILE)) * 8
+    stack = pltpu.VMEM((slots + 1, TILE, TILE), kind)
+
+    def held(count, more=0):
+        return pltpu.VMEM((count, RB + more, TILE), jnp.float32)
+
+    return [
+        vector,
+        pltpu.VMEM((extra, TILE), jnp.float32),
+        pltpu.VMEM((docs, width), kind),
+        pltpu.VMEM((terms, docs), kind),
+        pltpu.VMEM((docs, terms), kind),
+        pltpu.SMEM((2 * slots + RB * CB,), jnp.int32),
+        stack,
+        stack,
+        pltpu.VMEM((RB, 16, TILE), jnp.bfloat16),
+        pltpu.VMEM((slots, TILE), jnp.float32),
+        held(m, extra),
+        held(n),
+        held(m),
+        held(n),
+        held(m),
+        pltpu.SemaphoreType.DMA((3,)),
+    ] + semaphores(m, m, n, n, m, m, n, n, m, m)
+
+
+SCALE_REFS = 26
+
+
+def tables(tile_rows, tile_cols, tile_count):
+    slots = tile_rows.shape[1]
     slot = jnp.arange(slots, dtype=jnp.int32)
     used = slot < tile_count[0, 0]
     rows, cols = tile_rows[0], tile_cols[0]
     cell = jnp.arange(RB * CB, dtype=jnp.int32)
     found = ((rows * CB + cols)[None, :] == cell[:, None]) & used[None, :]
     lookup = slots + jnp.sum(jnp.where(found, slot[None, :] - slots, 0), axis=1)
-    ids = jnp.concatenate([rows, cols, lookup])
     live = jnp.stack([jnp.where(used, rows, RB), jnp.where(used, cols, CB)])
-    live = jnp.concatenate([live, live, live], axis=1)
-    vector = jax.ShapeDtypeStruct((RB, TILE), jnp.float32)
-    extra = -(-start_block.shape[1] // (8 * TILE)) * 8
-    square = jax.ShapeDtypeStruct((RB * TILE, CB * TILE), tile_values.dtype)
-    held = pltpu.VMEM((m, RB, TILE), jnp.float32)
-    return pl.pallas_call(
-        scale_kernel,
-        out_shape=[
-            vector,
-            vector,
-            vector,
-            jax.ShapeDtypeStruct((extra, TILE), jnp.float32),
-            square,
-            square,
-        ],
-        in_specs=[SMEM, VMEM, pl.BlockSpec(memory_space=pl.ANY), VMEM],
-        out_specs=[VMEM] * 6,
-        scratch_shapes=[
-            pltpu.VMEM((slots + 1, TILE, TILE), tile_values.dtype),
-            pltpu.VMEM((slots + 1, TILE, TILE), tile_values.dtype),
-            pltpu.VMEM((RB, 16, TILE), jnp.bfloat16),
-            pltpu.VMEM((slots, TILE), jnp.float32),
-            pltpu.VMEM((m, RB + extra, TILE), jnp.float32),
-            pltpu.VMEM((n, RB, TILE), jnp.float32),
-            held,
-            pltpu.VMEM((n, RB, TILE), jnp.float32),
-            held,
-            pltpu.SemaphoreType.DMA(()),
-        ]
-        + semaphores(m, m, n, n, m, m, n, n, m, m),
-        compiler_params=params(identifier),
-        name="scale",
-    )(ids, live, tile_values, start_block)
+    return jnp.concatenate([rows, cols, lookup]), jnp.concatenate([live, live, live], axis=1)
 
 
 CODES = 32760.0
@@ -427,14 +428,13 @@
 GRAM_REFS = 18
 
 
-def basis_kernel(
-    matrix,
-    turned,
-    start_ref,
+def whole_kernel(
+    ids_hbm,
+    live,
+    tiles_hbm,
+    start_hbm,
     row_ref,
     col_ref,
-    weight_ref,
-    mean_ref,
     left_out,
     right_out,
     row_turn,
@@ -457,7 +457,10 @@
     *rest,
 ):
     left_gram, right_gram = rest[:GRAM_REFS], rest[GRAM_REFS : 2 * GRAM_REFS]
-    sems = rest[2 * GRAM_REFS :]
+    scale_refs = rest[2 * GRAM_REFS : 2 * GRAM_REFS + SCALE_REFS]
+    weight_ref, mean_ref, start_ref, matrix, turned = scale_refs[:5]
+    held_e = scale_refs[14]
+    sems = rest[2 * GRAM_REFS + SCALE_REFS :]
     n, m = lax.axis_size("term"), lax.axis_size("doc")
     nz, z, c = paired()
     doc = lax.axis_index("doc")
@@ -468,7 +471,9 @@
     share, piece = terms // m, docs // n
     docs_total = docs * m
 
-    greet(("term", "doc"))
+    weight_copies = scale_phase(
+        ids_hbm, live, tiles_hbm, start_hbm, row_ref, col_ref, *scale_refs
+    )
 
     def axes(flow):
         return (x, nx, y, ny) if flow == 0 else (y, ny, x, nx)
@@ -542,6 +547,7 @@
             )
             copies_b[flow, s2].start()
 
+    weight_ref[...] = row_ref[...] * finish_exchange(weight_copies, held_e, "doc")
     blocks_of_share = share // TILE
     weight = jnp.concatenate(
         [turn_out(weight_ref, doc * blocks_of_share + k, TILE) for k in range(blocks_of_share)], axis=0
@@ -711,10 +717,33 @@
         finish_right(2 * lax.rem(z - step + nz, nz) + 1 - c)
 
 
-def basis_stage(matrix, turned, start_block, row, col, weight, mean, identifier):
+def emit_kernel(row_ref, col_ref, left_ref, right_ref, *rest):
+    outs, sems = rest[:4], rest[4]
+    copies = [
+        pltpu.make_async_copy(source, target, sems.at[k])
+        for k, (source, target) in enumerate(zip((row_ref, col_ref, left_ref, right_ref), outs))
+    ]
+    for copy in copies:
+        copy.start()
+    for copy in copies:
+        copy.wait()
+
+
+def emit(arrays):
+    return pl.pallas_call(
+        emit_kernel,
+        out_shape=[jax.ShapeDtypeStruct(x.shape, x.dtype) for x in arrays],
+        in_specs=[VMEM] * 4,
+        out_specs=[pl.BlockSpec(memory_space=pl.ANY)] * 4,
+        scratch_shapes=[pltpu.SemaphoreType.DMA((4,))],
+        name="emit",
+    )(*arrays)
+
+
+def per_device(tile_values, tile_rows, tile_cols, tile_count, start_block):
     n, m = lax.axis_size("term"), lax.axis_size("doc")
     nz = n // 2
-    terms, docs, width = matrix.shape[0], turned.shape[0], start_block.shape[1]
+    terms, (docs, width) = RB * TILE, start_block.shape
     share, piece = terms // m, docs // n
     wide = max(grid_of(m))
     int16, f32, bf16 = jnp.int16, jnp.float32, jnp.bfloat16
@@ -723,14 +752,19 @@
     far = pltpu.VMEM((nz, piece + 16, width), int16)
     near = pltpu.VMEM((nz, piece, width), f32)
     pairs = [pltpu.SemaphoreType.DMA((2, size)) for size in (m, m, wide, wide, wide, wide, m, m)]
-    return pl.pallas_call(
-        basis_kernel,
+    vector = jax.ShapeDtypeStruct((RB, TILE), f32)
+    hbm = pl.BlockSpec(memory_space=pl.ANY)
+    ids, live = tables(tile_rows, tile_cols, tile_count)
+    outs = pl.pallas_call(
+        whole_kernel,
         out_shape=[
+            vector,
+            vector,
             jax.ShapeDtypeStruct((terms, width), bf16),
             jax.ShapeDtypeStruct((docs, width), bf16),
         ],
-        in_specs=[VMEM] * 7,
-        out_specs=[VMEM] * 2,
+        in_specs=[hbm, VMEM, hbm, hbm],
+        out_specs=[VMEM] * 4,
         scratch_shapes=[
             pltpu.VMEM((terms, TILE), f32),
             pltpu.VMEM((docs, TILE), f32),
@@ -752,23 +786,16 @@
         ]
         + gram_scratch(width)
         + gram_scratch(width)
+        + scale_scratch(terms, docs, width, tile_values.shape[0], tile_values.dtype)
         + pairs
         + semaphores(*[nz] * 8),
         compiler_params=pltpu.CompilerParams(
-            collective_id=identifier, has_side_effects=True, vmem_limit_bytes=58 << 20
+            collective_id=0, has_side_effects=True, vmem_limit_bytes=44 << 20
         ),
-        name="basis",
-    )(matrix, turned, start_block, row, col, weight, mean)
-
-
-def per_device(tile_values, tile_rows, tile_cols, tile_count, start_block):
-    rows_out, cols_out, weights, means, matrix, turned = scale_stage(
-        tile_values, tile_rows, tile_cols, tile_count, start_block, 0
-    )
-    left_basis, right_basis = basis_stage(
-        matrix, turned, start_block, rows_out, cols_out, weights, means, 1
-    )
-    return (rows_out.reshape(-1), cols_out.reshape(-1), left_basis, right_basis)
+        name="whole",
+    )(ids, live, tile_values, start_block)
+    row, col, left_basis, right_basis = emit(outs)
+    return (row.reshape(-1), col.reshape(-1), left_basis, right_basis)
 
 
 def solution(mesh):

time: 144 us -> 123 us (0.85)
  local copies, waits for them, and re-layouts: 16.6 us -> 5.82 us
  Pallas kernels: 123 us -> 114 us
    unnamed x24 -> x12, local copies, waits for them, and re-layouts: 16.6 us -> 5.82 us
    pallas_call x2, Pallas kernels: 123 us -> 114 us  [the longest x1 111 us: per_device(): pl.pallas_call(whole_kernel, out_shape=[vector, vector, jax.ShapeDtypeStr...]
where the time goes in v3:
time: 123 us
  Pallas kernels  114 us (93%)
  local copies, waits for them, and re-layouts  5.82 us (5%)
  other arithmetic  1.62 us (1%)
  between operations  1.5 us (1%)
    pallas_call x1, Pallas kernels, per_device(): pl.pallas_call(whole_kernel, out_shape=[vector, vector, jax.ShapeDtypeStr...  111 us
    unnamed x12, local copies, waits for them, and re-layouts  5.82 us
    pallas_call x1, Pallas kernels, emit(): pl.pallas_call(emit_kernel, out_shape=[jax.ShapeDtypeStruct(x.shape, x.dt...  2.93 us

profile of v3, /device:TPU:0, one launch (start us, length us, event | category | flops | bytes accessed | tf_op | source)
XLA Modules:
  0.0 122.5 jit_solution(18169845085847741534)
XLA Ops:
  1.3 0.7 compare_select_fusion.1
  2.0 0.1 select_reduce_fusion
  2.1 0.8 pad_add_fusion.ids_hbm
  2.8 0.1 add_add_fusion.live
  2.9 0.0 copy-start
  2.9 1.4 %copy-done = bf16[48,128,128]{2,1,0:T(8,128)(2,1)S(1)} copy-done((bf16[48,128,128]{2,1,0:T(8,128)(2,1)S(1)}, bf16[48,128,128]{2,1,0:T(8,128)(2,1)}, u32[]{:S(2)}) %copy-start) | copy-done | bytes 1572888
  4.3 0.0 copy-start.1
  4.3 1.2 copy-done.1
  5.6 110.7 %whole.1 = (f32[16,128]{1,0:T(8,128)S(1)}, f32[16,128]{1,0:T(8,128)S(1)}, bf16[2048,256]{1,0:T(8,128)(2,1)S(1)}, bf16[2048,256]{1,0:T(8,128)(2,1)S(1)}) custom-call(s32[352]{0:T(512)S(1)} %pad_add_fusion.ids_hbm, s32[2,144]{1,0:T(2,128)S(1)} %add_add_fusion.live, bf16[48,128,128]{2,1,0:T(8,128)(2,1)S(1)} %copy-done, bf16[2048,256]{1,0:T(8,128)(2,1)S(1)} %copy-done.1), custom_call_target="tpu_custom_call" | custom-call | tf_op jit(solution)/shard_map/whole/pallas_call | solution.py:758
  116.2 0.0 copy-start.2
  116.2 1.0 copy-done.2
  117.2 0.0 copy-start.3
  117.2 1.0 copy-done.3
  118.2 0.0 copy-start.4
  118.2 0.6 copy-done.4
  118.8 0.0 copy-start.5
  118.8 0.6 copy-done.5
  119.4 2.9 %emit.1 = (f32[16,128]{1,0:T(8,128)}, f32[16,128]{1,0:T(8,128)}, bf16[2048,256]{1,0:T(8,128)(2,1)}, bf16[2048,256]{1,0:T(8,128)(2,1)}) custom-call(f32[16,128]{1,0:T(8,128)} %copy-done.4, f32[16,128]{1,0:T(8,128)} %copy-done.5, bf16[2048,256]{1,0:T(8,128)(2,1)} %copy-done.2, bf16[2048,256]{1,0:T(8,128)(2,1)} %copy-done.3), custom_call_target="tpu_custom_call" | custom-call | tf_op jit(solution)/shard_map/emit/pallas_call | solution.py:733
  (3 shorter events, 0.0 us)
Async XLA Ops:
  2.9 1.4 %copy-start = (bf16[48,128,128]{2,1,0:T(8,128)(2,1)S(1)}, bf16[48,128,128]{2,1,0:T(8,128)(2,1)}, u32[]{:S(2)}) copy-start(bf16[48,128,128]{2,1,0:T(8,128)(2,1)} %tiles_hbm.1) | copy-start | bytes 4718596
  4.3 1.2 copy-start.1
  116.2 1.0 copy-start.2
  117.2 1.0 copy-start.3
  118.2 0.6 copy-start.4
  118.8 0.6 copy-start.5

commit v4 on v3

--- a/solution.py
+++ b/solution.py
@@ -77,18 +77,17 @@
             work[start + BLOCK :, :] = work[start + BLOCK :, :] - update[start + BLOCK :, :]
 
 
-def greet(axes):
+def greet():
     barrier = pltpu.get_barrier_semaphore()
-    total = 0
-    for axis in axes:
-        n = lax.axis_size(axis)
-        me = lax.axis_index(axis)
-        for step in range(1, n):
-            pl.semaphore_signal(
-                barrier, inc=1, device_id={axis: lax.rem(me + step, n)}, device_id_type=MESH
-            )
-        total += n - 1
-    pl.semaphore_wait(barrier, total)
+    n, m = lax.axis_size("term"), lax.axis_size("doc")
+    me, doc = lax.axis_index("term"), lax.axis_index("doc")
+    peers = [{"term": lax.rem(me + step, n)} for step in range(1, n)]
+    for step in range(1, m):
+        there = lax.rem(doc + step, m)
+        peers += [{"doc": there}, {"doc": there, "term": me + 1 - 2 * lax.rem(me, 2)}]
+    for peer in peers:
+        pl.semaphore_signal(barrier, inc=1, device_id=peer, device_id_type=MESH)
+    pl.semaphore_wait(barrier, len(peers))
 
 
 def remote(source, target, send_sem, recv_sem, axis, peer):
@@ -97,7 +96,7 @@
         dst_ref=target,
         send_sem=send_sem,
         recv_sem=recv_sem,
-        device_id={axis: peer},
+        device_id=axis if peer is None else {axis: peer},
         device_id_type=MESH,
     )
 
@@ -165,6 +164,7 @@
 
 
 def scale_phase(
+    meanwhile,
     ids_hbm,
     live,
     tiles_hbm,
@@ -197,7 +197,7 @@
     ]
     for load in loads:
         load.start()
-    greet(("term", "doc"))
+    greet()
     tiles[slots] = jnp.zeros(tiles.shape[1:], tiles.dtype)
     flipped[slots] = jnp.zeros(tiles.shape[1:], tiles.dtype)
     blocks = row_ref.shape[0]
@@ -252,12 +252,15 @@
 
     held_d[0] = tile_sums(tiles, row_ids, parts, sums, to_cols, False)
     copies = start_exchange(held_d, "term", *sems[6:8])
-    col_scale = 1.0 / finish_exchange(copies, held_d, "term")
-    col_ref[...] = col_scale
-    spread(col_scale, parts)
-
-    held_e[0] = tile_sums(tiles, col_ids, parts, sums, to_rows, True)
-    return start_exchange(held_e, "doc", *sems[8:10])
+    meanwhile()
+    col_ref[...] = 1.0 / finish_exchange(copies, held_d, "term")
+
+    def weigh():
+        spread(col_ref[...], parts)
+        held_e[0] = tile_sums(tiles, col_ids, parts, sums, to_rows, True)
+        return start_exchange(held_e, "doc", *sems[8:10])
+
+    return weigh
 
 
 def scale_scratch(terms, docs, width, slots, kind):
@@ -344,88 +347,99 @@
     )
 
 
-def gram_steps(x_ref, o_ref, near, mid, far, second, part, done, *sems):
+def pack_gram(gram, extras, packed):
+    groups, rows = packed.shape[0], packed.shape[1] - 8
+    row = lax.broadcasted_iota(jnp.int32, (TILE, TILE), 0)
+    lane = lax.broadcasted_iota(jnp.int32, (TILE, TILE), 1)
+    last = gram[TILE:, TILE:]
+    packed_rows = [jnp.where(row <= lane, gram[:TILE, :TILE], last), gram[:TILE, TILE:]]
+    packed_rows = jnp.concatenate(packed_rows, axis=0)
+    diagonal = jnp.sum(jnp.where(row == lane, last, 0.0), axis=0, keepdims=True)
+    extras = [diagonal] + extras
+    extras.append(jnp.zeros((8 - len(extras), TILE), jnp.float32))
+    for group in range(groups):
+        packed[group, :rows, :] = packed_rows[group * rows : (group + 1) * rows]
+        packed[group, rows:, :] = (
+            jnp.concatenate(extras, axis=0) if group == 0 else jnp.zeros((8, TILE), jnp.float32)
+        )
+
+
+def unpack_gram(packed, gram):
+    rows = packed.shape[1] - 8
+    row = lax.broadcasted_iota(jnp.int32, (TILE, TILE), 0)
+    lane = lax.broadcasted_iota(jnp.int32, (TILE, TILE), 1)
+    half = packed.shape[0] // 2
+    both = jnp.concatenate([packed[g, :rows, :] for g in range(half)], axis=0)
+    cross = jnp.concatenate([packed[half + g, :rows, :] for g in range(half)], axis=0)
+    other = both.T
+    gram[:TILE, :TILE] = jnp.where(row <= lane, both, other)
+    gram[:TILE, TILE:] = cross
+    gram[TILE:, :TILE] = jnp.zeros((TILE, TILE), jnp.float32)
+    diagonal = jnp.broadcast_to(packed[0, rows : rows + 1, :], (TILE, TILE))
+    last = jnp.where(row > lane, both, jnp.where(row == lane, diagonal, other))
+    gram[TILE:, TILE:] = last
+
+
+def gram_steps(x_ref, o_ref, landing, held, *sems):
     nz, z, c = paired()
     m, my = lax.axis_size("doc"), lax.axis_index("doc")
-    rows = part.shape[0]
-    sibling = 2 * z + 1 - c
-
-    def share(ref, there, core):
-        return ref.at[pl.ds(pl.multiple_of((2 * there + core) * rows, 8), rows)]
-
-    near_copies, far_copies = {}, []
-    for step in list(range(1, nz)) + [0]:
-        there = lax.rem(z + step, nz)
-        near_copies[step] = remote(
-            share(x_ref, there, 1 - c), near.at[step], sems[0].at[step], sems[1].at[step], "term", sibling
-        )
-        near_copies[step].start()
+    steps = [(step, flip) for step in range(m) for flip in range(2) if step or flip]
+
+    def peer(step, flip):
+        there = lax.rem(my + step, m)
+        core = 1 - c if flip else c
+        return 2 * there + core, {"doc": there, "term": 2 * z + core}
+
+    def exchange(source, target, send_sem, recv_sem):
+        copies = []
+        for step, flip in steps:
+            group, place = peer(step, flip)
+            slot = 2 * step + flip
+            copy = remote(
+                source(group), target(slot), send_sem.at[slot], recv_sem.at[slot], place, None
+            )
+            copy.start()
+            copies.append(copy)
+        return copies
+
+    mine = 2 * my + c
+    copies = exchange(lambda g: x_ref.at[g], lambda k: landing.at[k], *sems[0:2])
     yield
+    total = x_ref[mine]
+    for (step, flip), copy in zip(steps, copies):
+        copy.wait()
+        total = total + landing[2 * step + flip]
+    held[0] = total
+    copies = []
     for step in range(1, nz):
-        near_copies[step].wait()
-        there = lax.rem(z + step, nz)
-        mid[step] = share(x_ref, there, c)[...] + near[step]
         copy = remote(
-            mid.at[step], far.at[step], sems[2].at[step], sems[3].at[step], "term", 2 * there + c
-        )
-        copy.start()
-        far_copies.append(copy)
-    near_copies[0].wait()
-    part[...] = share(x_ref, z, c)[...] + near[0]
-    yield
-    for step, copy in enumerate(far_copies):
-        copy.wait()
-        part[...] += far[step + 1]
-    copies = []
-    for step in range(1, m):
-        copy = remote(
-            part, second.at[step], sems[4].at[step], sems[5].at[step], "doc", lax.rem(my + step, m)
+            held.at[0], held.at[step], sems[2].at[step], sems[3].at[step], "term", 2 * lax.rem(z + step, nz) + c
         )
         copy.start()
         copies.append(copy)
-    second[0] = part[...]
     yield
     for copy in copies:
         copy.wait()
-    total = second[my]
-    for source in range(1, m):
-        total = total + second[lax.rem(my - source + m, m)]
-    done[...] = total
-    far_copies = []
-    here = share(o_ref, z, c)
-    for step in range(1, nz):
-        copy = remote(
-            done, here, sems[6].at[step], sems[7].at[step], "term", 2 * lax.rem(z + step, nz) + c
-        )
-        copy.start()
-        far_copies.append(copy)
-    copy = remote(done, here, sems[8].at[0], sems[9].at[0], "term", sibling)
-    copy.start()
-    near_copies = [copy]
-    here[...] = total
+    total = held[z]
+    for source in range(1, nz):
+        total = total + held[lax.rem(z - source + nz, nz)]
+    o_ref[mine] = total
+    copies = exchange(lambda g: o_ref.at[mine], lambda k: o_ref.at[mine], *sems[4:6])
     yield
-    for step in range(1, nz):
-        far_copies[step - 1].wait()
-        there = share(o_ref, lax.rem(z - step + nz, nz), c)
-        copy = remote(there, there, sems[8].at[step], sems[9].at[step], "term", sibling)
-        copy.start()
-        near_copies.append(copy)
-    for copy in near_copies:
+    for copy in copies:
         copy.wait()
 
 
-def gram_scratch(width):
+def gram_scratch():
     nz, m = lax.axis_size("term") // 2, lax.axis_size("doc")
-    rows = width // (2 * nz)
-    spread_over = pltpu.VMEM((nz, rows, width), jnp.float32)
-    alone = pltpu.VMEM((rows, width), jnp.float32)
-    whole = pltpu.VMEM((width, width), jnp.float32)
-    return [whole, whole] + [spread_over] * 3 + [pltpu.VMEM((m, rows, width), jnp.float32), alone, alone] + semaphores(
-        nz, nz, nz, nz, m, m, nz, nz, nz, nz
-    )
-
-
-GRAM_REFS = 18
+    rows = TILE // m + 8
+    packed = pltpu.VMEM((2 * m, rows, TILE), jnp.float32)
+    return [packed, packed, packed, pltpu.VMEM((nz, rows, TILE), jnp.float32)] + semaphores(
+        2 * m, 2 * m, nz, nz, 2 * m, 2 * m
+    )
+
+
+GRAM_REFS = 10
 
 
 def whole_kernel(
@@ -453,6 +467,8 @@
     far_recv,
     right_parts,
     inverse_ref,
+    halves,
+    gram,
     work,
     *rest,
 ):
@@ -471,8 +487,16 @@
     share, piece = terms // m, docs // n
     docs_total = docs * m
 
-    weight_copies = scale_phase(
-        ids_hbm, live, tiles_hbm, start_hbm, row_ref, col_ref, *scale_refs
+    def turn_rows():
+        def turn(block, carry):
+            at = pl.ds(pl.multiple_of(block * TILE, TILE), TILE)
+            row_turn[at, :] = turn_out(row_ref, block, TILE)
+            return carry
+
+        lax.fori_loop(0, terms // TILE, turn, 0)
+
+    weigh = scale_phase(
+        turn_rows, ids_hbm, live, tiles_hbm, start_hbm, row_ref, col_ref, *scale_refs
     )
 
     def axes(flow):
@@ -489,7 +513,6 @@
         column = turn_out(col_ref, block, width)
         col_turn[at, :] = column[:, :TILE]
         scaled[at, :] = (column * start_ref[at, :].astype(jnp.float32)).astype(jnp.bfloat16)
-        row_turn[at, :] = turn_out(row_ref, block, TILE)
         return carry
 
     lax.fori_loop(0, docs // TILE, prepare, 0)
@@ -521,6 +544,8 @@
             )
             copies_a[flow, s1, s2].start()
 
+    weight_copies = weigh()
+
     def own(flow, s2):
         dx, dy = (0, s2) if flow == 0 else (s2, 0)
         return partial[dy * nx + dx, :, lanes(flow)]
@@ -575,14 +600,21 @@
             copies_c[flow, s1].start()
 
     left_share = jnp.concatenate(left, axis=1)
-    gram_in, gram_out = left_gram[:2]
-    gram_in[...] = precise(left_share, left_share, ((0,), (0,))) * (1.0 / (terms * n))
-    for k in range(width // TILE):
-        weighted = jnp.sum(weight * left[k], axis=0, keepdims=True)
-        gram_in[width - width // TILE + k : width - width // TILE + k + 1, :TILE] = weighted
+    pack_gram(
+        precise(left_share, left_share, ((0,), (0,))) * (1.0 / (terms * n)),
+        [jnp.sum(weight * part, axis=0, keepdims=True) for part in left],
+        left_gram[0],
+    )
     left_steps = gram_steps(*left_gram)
     next(left_steps)
 
+    def unpack(flow, block):
+        at = pl.ds(pl.multiple_of(block * share, share), share)
+        value = decode(gathered[flow, block]) * row_turn[at, :]
+        factor[at, lanes(flow)] = value.astype(jnp.bfloat16)
+
+    for flow in range(2):
+        unpack(flow, doc)
     for flow in range(2):
         a, n1, b, n2 = axes(flow)
         for s1 in range(n1):
@@ -599,84 +631,106 @@
                     device(flow, a, lax.rem(b + s2, n2)),
                 )
                 copies_d[flow, s1, s2].start()
+    for flow in range(2):
+        a, n1, b, n2 = axes(flow)
+        for s1 in range(1, n1):
+            unpack(flow, device(flow, lax.rem(a - s1 + n1, n1), b))
     next(left_steps)
-    next(left_steps)
-    for copy in copies_d.values():
-        copy.wait()
-
-    def unpack(block, carry):
-        at = pl.ds(pl.multiple_of(block * share, share), share)
-        for flow in range(2):
-            value = decode(gathered[flow, block]) * row_turn[at, :]
-            high = value.astype(jnp.bfloat16)
-            factor[at, lanes(flow)] = high
-            low = slice(width + flow * TILE, width + (flow + 1) * TILE)
-            factor[at, low] = (value - high.astype(jnp.float32)).astype(jnp.bfloat16)
-        return carry
-
-    lax.fori_loop(0, m, unpack, 0)
-
-    def right_product(there, core):
-        at = pl.ds(pl.multiple_of((2 * there + core) * piece, piece), piece)
-        both = jnp.dot(turned[at, :], factor[...], preferred_element_type=jnp.float32)
-        column = col_turn[at, :]
-        return (both[:, :width] + both[:, width:]) * jnp.concatenate(
-            [column] * (width // TILE), axis=1
-        )
+    for flow in range(2):
+        a, n1, b, n2 = axes(flow)
+        for s1 in range(n1):
+            for s2 in range(1, n2):
+                copies_d[flow, s1, s2].wait()
+                unpack(
+                    flow,
+                    device(flow, lax.rem(a - s1 + n1, n1), lax.rem(b - s2 + n2, n2)),
+                )
+    wide = 2 * piece
+
+    def right_product(chunk, core):
+        at = pl.ds(pl.multiple_of(core * (docs // 2) + chunk * wide, wide), wide)
+        product = jnp.dot(turned[at, :], factor[...], preferred_element_type=jnp.float32)
+        return product * jnp.concatenate([col_turn[at, :]] * (width // TILE), axis=1)
 
     sibling = 2 * z + 1 - c
-    near_copies, far_copies = {}, {}
-    order = list(range(1, nz)) + [0]
-    for step in order:
-        near_send[step] = right_product(lax.rem(z + step, nz), 1 - c)
-        near_copies[step] = remote(
-            near_send.at[step], near_recv.at[step], sems[8].at[step], sems[9].at[step], "term", sibling
-        )
-        near_copies[step].start()
-    next(left_steps)
-    for step in order:
+    chunks = [lax.rem(z // 2 + 1 + j, nz // 2) for j in range(nz // 2)]
+    near_copies = []
+    for j, chunk in enumerate(chunks):
+        near_send[j] = right_product(chunk, 1 - c)
+        copy = remote(near_send.at[j], near_recv.at[j], sems[8].at[j], sems[9].at[j], "term", sibling)
+        copy.start()
+        near_copies.append(copy)
+
+    def far_copy(step):
         there = lax.rem(z + step, nz)
-        product = right_product(there, c)
-        near_copies[step].wait()
-        product = product + near_recv[step]
-        if step == 0:
-            own_right = product
-            continue
-        far_send[step] = encode(product)
-        far_copies[step] = remote(
+        return remote(
             far_send.at[step], far_recv.at[step], sems[10].at[step], sems[11].at[step], "term", 2 * there + c
         )
-        far_copies[step].start()
-    near_send[0] = own_right
+
+    for j, chunk in enumerate(chunks):
+        product = right_product(chunk, c)
+        near_copies[j].wait()
+        near_recv[j] = near_recv[j] + product
+        last = j + 1 == len(chunks)
+        for k in range(2):
+            if last and k:
+                continue
+            inner = 1 - lax.rem(z, 2) if last else k
+            step = lax.rem(2 * chunk + inner - z + nz, nz)
+            at = pl.ds(pl.multiple_of(inner * piece, piece), piece)
+            far_send[step] = encode(near_recv[j, at, :])
+            far_copy(step).start()
+        if j == 0:
+            next(left_steps)
     for _ in left_steps:
         pass
-    inverse_kernel(gram_out, inverse_ref, work)
-    whiten = inverse_ref[...]
-
-    def finish_left(block, carry):
+    unpack_gram(left_gram[1], gram)
+    inverse_kernel(gram, inverse_ref, work)
+
+    def split_inverse():
+        whiten = inverse_ref[...].T
+        high = whiten.astype(jnp.bfloat16)
+        halves[0] = high
+        halves[1] = (whiten - high.astype(jnp.float32)).astype(jnp.bfloat16)
+
+    def whitened(value):
+        high = value.astype(jnp.bfloat16)
+        low = (value - high.astype(jnp.float32)).astype(jnp.bfloat16)
+        parts = [(high, 0), (low, 0), (high, 1)]
+        total = [jnp.dot(v, halves[k], preferred_element_type=jnp.float32) for v, k in parts]
+        return total[0] + (total[1] + total[2])
+
+    def finish_left(block):
         at = pl.ds(pl.multiple_of(block * share, share), share)
         value = jnp.concatenate([decode(gathered[flow, block]) for flow in range(2)], axis=1)
-        left_out[at, :] = precise(value, inverse_ref[...], ((1,), (1,))).astype(jnp.bfloat16)
-        return carry
-
-    lax.fori_loop(0, m, finish_left, 0)
-    pieces = width // TILE
+        left_out[at, :] = whitened(value).astype(jnp.bfloat16)
+
+    extra = left_gram[1].shape[1] - 8
     weighted = jnp.concatenate(
-        [gram_out[width - pieces + k : width - pieces + k + 1, :TILE] for k in range(pieces)], axis=1
-    )
-    lean = precise(jnp.broadcast_to(weighted, (8, width)), whiten, ((1,), (1,)))[0:1]
-    total = near_send[0]
+        [left_gram[1][0, extra + 1 + k : extra + 2 + k, :] for k in range(width // TILE)], axis=1
+    )
+    lean = precise(jnp.broadcast_to(weighted, (8, width)), inverse_ref[...], ((1,), (1,)))[0:1]
+    split_inverse()
+    own_rows = pl.ds(pl.multiple_of(lax.rem(z, 2) * piece, piece), piece)
+    total = near_recv[len(chunks) - 1, own_rows, :]
     for step in range(1, nz):
-        far_copies[step].wait()
+        far_copy(step).wait()
         total = total + decode(far_recv[step])
     block = precise(total, inverse_ref[...], ((1,), (1,))) - lean * (1.0 / docs_total)
 
-    me = 2 * z + c
+    me = c * nz + z
+    pack_gram(
+        precise(block, block, ((0,), (0,))) * (1.0 / docs_total), [], right_gram[0]
+    )
+    right_steps = gram_steps(*right_gram)
+    next(right_steps)
     right_parts[me] = encode(block)
-    gram_in, gram_out = right_gram[:2]
-    gram_in[...] = precise(block, block, ((0,), (0,))) * (1.0 / docs_total)
-    for _ in gram_steps(*right_gram):
-        pass
+    for k in range(m // 4):
+        finish_left(k)
+    next(right_steps)
+    for k in range(m // 4, 3 * m // 4):
+        finish_left(k)
+    next(right_steps)
     far_copies = []
     for step in range(1, nz):
         copy = remote(
@@ -694,27 +748,31 @@
     )
     copy.start()
     near_copies = [copy]
-    inverse_kernel(gram_out, inverse_ref, work)
+    for k in range(3 * m // 4, m):
+        finish_left(k)
+    for _ in right_steps:
+        pass
+    unpack_gram(right_gram[1], gram)
+    inverse_kernel(gram, inverse_ref, work)
+    split_inverse()
 
     def finish_right(t):
         at = pl.ds(pl.multiple_of(t * piece, piece), piece)
-        right_out[at, :] = precise(
-            decode(right_parts[t]), inverse_ref[...], ((1,), (1,))
-        ).astype(jnp.bfloat16)
-
-    finish_right(me)
+        right_out[at, :] = whitened(decode(right_parts[t])).astype(jnp.bfloat16)
+
     for step in range(1, nz):
         far_copies[step - 1].wait()
-        t = 2 * lax.rem(z - step + nz, nz) + c
+        t = c * nz + lax.rem(z - step + nz, nz)
         copy = remote(
             right_parts.at[t], right_parts.at[t], sems[14].at[step], sems[15].at[step], "term", sibling
         )
         copy.start()
         near_copies.append(copy)
-        finish_right(t)
+    for step in range(nz):
+        finish_right(c * nz + lax.rem(z - step + nz, nz))
     for step, copy in enumerate(near_copies):
         copy.wait()
-        finish_right(2 * lax.rem(z - step + nz, nz) + 1 - c)
+        finish_right((1 - c) * nz + lax.rem(z - step + nz, nz))
 
 
 def emit_kernel(row_ref, col_ref, left_ref, right_ref, *rest):
@@ -736,6 +794,7 @@
         in_specs=[VMEM] * 4,
         out_specs=[pl.BlockSpec(memory_space=pl.ANY)] * 4,
         scratch_shapes=[pltpu.SemaphoreType.DMA((4,))],
+        compiler_params=pltpu.CompilerParams(vmem_limit_bytes=4 << 20),
         name="emit",
     )(*arrays)
 
@@ -750,7 +809,7 @@
     coded = pltpu.VMEM((2, m, share + 16, TILE), int16)
     coded_b = pltpu.VMEM((2, wide, share + 16, TILE), int16)
     far = pltpu.VMEM((nz, piece + 16, width), int16)
-    near = pltpu.VMEM((nz, piece, width), f32)
+    near = pltpu.VMEM((nz // 2, 2 * piece, width), f32)
     pairs = [pltpu.SemaphoreType.DMA((2, size)) for size in (m, m, wide, wide, wide, wide, m, m)]
     vector = jax.ShapeDtypeStruct((RB, TILE), f32)
     hbm = pl.BlockSpec(memory_space=pl.ANY)
@@ -775,17 +834,19 @@
             coded_b,
             coded_b,
             coded,
-            pltpu.VMEM((terms, 2 * width), bf16),
+            pltpu.VMEM((terms, width), bf16),
             near,
             near,
             far,
             far,
             pltpu.VMEM((n, piece + 16, width), int16),
             pltpu.VMEM((width, width), f32),
+            pltpu.VMEM((2, width, width), bf16),
+            pltpu.VMEM((width, width), f32),
             pltpu.VMEM((width, 2 * width), f32),
         ]
-        + gram_scratch(width)
-        + gram_scratch(width)
+        + gram_scratch()
+        + gram_scratch()
         + scale_scratch(terms, docs, width, tile_values.shape[0], tile_values.dtype)
         + pairs
         + semaphores(*[nz] * 8),

time: 123 us -> 102 us (0.83)
  Pallas kernels: 114 us -> 95.6 us
  local copies, waits for them, and re-layouts: 5.82 us -> 2.64 us
    pallas_call x1, Pallas kernels: 111 us -> 94.2 us  [per_device(): pl.pallas_call(whole_kernel, out_shape=[vector, vector, jax.ShapeDtypeStr...]
    unnamed x12 -> x4, local copies, waits for them, and re-layouts: 5.82 us -> 2.64 us
    pallas_call x1, Pallas kernels: 2.93 us -> 1.36 us  [emit(): pl.pallas_call(emit_kernel, out_shape=[jax.ShapeDtypeStruct(x.shape, x.dt...]
where the time goes in v4:
time: 102 us; the launch traced here: 101 us
  Pallas kernels  95.6 us (94%)
  local copies, waits for them, and re-layouts  2.64 us (3%)
  other arithmetic  1.62 us (2%)
  between operations  1.49 us (1%)
    pallas_call x1, Pallas kernels, per_device(): pl.pallas_call(whole_kernel, out_shape=[vector, vector, jax.ShapeDtypeStr...  94.2 us
    unnamed x4, local copies, waits for them, and re-layouts  2.64 us

profile of v4, /device:TPU:0, one launch (start us, length us, event | category | flops | bytes accessed | tf_op | source)
XLA Modules:
  0.0 101.3 jit_solution(15415415783526716785)
XLA Ops:
  1.3 0.7 compare_select_fusion.1
  2.0 0.1 select_reduce_fusion
  2.1 0.8 pad_add_fusion.ids_hbm
  2.8 0.1 add_add_fusion.live
  2.9 0.0 copy-start
  2.9 1.4 %copy-done = bf16[48,128,128]{2,1,0:T(8,128)(2,1)S(1)} copy-done((bf16[48,128,128]{2,1,0:T(8,128)(2,1)S(1)}, bf16[48,128,128]{2,1,0:T(8,128)(2,1)}, u32[]{:S(2)}) %copy-start) | copy-done | bytes 1572888
  4.3 0.0 copy-start.1
  4.3 1.2 %copy-done.1 = bf16[2048,256]{1,0:T(8,128)(2,1)S(1)} copy-done((bf16[2048,256]{1,0:T(8,128)(2,1)S(1)}, bf16[2048,256]{1,0:T(8,128)(2,1)}, u32[]{:S(2)}) %copy-start.1) | copy-done | bytes 1048600
  5.6 94.2 %whole.1 = (f32[16,128]{1,0:T(8,128)S(1)}, f32[16,128]{1,0:T(8,128)S(1)}, bf16[2048,256]{1,0:T(8,128)(2,1)S(1)}, bf16[2048,256]{1,0:T(8,128)(2,1)S(1)}) custom-call(s32[352]{0:T(512)S(1)} %pad_add_fusion.ids_hbm, s32[2,144]{1,0:T(2,128)S(1)} %add_add_fusion.live, bf16[48,128,128]{2,1,0:T(8,128)(2,1)S(1)} %copy-done, bf16[2048,256]{1,0:T(8,128)(2,1)S(1)} %copy-done.1), custom_call_target="tpu_custom_call" | custom-call | tf_op jit(solution)/shard_map/whole/pallas_call | solution.py:817
  99.8 1.4 %emit.1 = (f32[16,128]{1,0:T(8,128)}, f32[16,128]{1,0:T(8,128)}, bf16[2048,256]{1,0:T(8,128)(2,1)}, bf16[2048,256]{1,0:T(8,128)(2,1)}) custom-call(f32[16,128]{1,0:T(8,128)S(1)} %get-tuple-element.12.row_ref, f32[16,128]{1,0:T(8,128)S(1)} %get-tuple-element.13.col_ref, bf16[2048,256]{1,0:T(8,128)(2,1)S(1)} %get-tuple-element.14.left_ref, ...), custom_call_target="tpu_custom_call" | custom-call | tf_op jit(solution)/shard_map/emit/pallas_call | solution.py:791
  (3 shorter events, 0.0 us)
Async XLA Ops:
  2.9 1.4 %copy-start = (bf16[48,128,128]{2,1,0:T(8,128)(2,1)S(1)}, bf16[48,128,128]{2,1,0:T(8,128)(2,1)}, u32[]{:S(2)}) copy-start(bf16[48,128,128]{2,1,0:T(8,128)(2,1)} %tiles_hbm.1) | copy-start | bytes 4718596
  4.3 1.2 %copy-start.1 = (bf16[2048,256]{1,0:T(8,128)(2,1)S(1)}, bf16[2048,256]{1,0:T(8,128)(2,1)}, u32[]{:S(2)}) copy-start(bf16[2048,256]{1,0:T(8,128)(2,1)} %start_hbm.1) | copy-start | bytes 3145732

commit v5 on v4

--- a/solution.py
+++ b/solution.py
@@ -131,7 +131,7 @@
     slots = sums.shape[0]
     for slot in range(slots):
         product = lax.dot_general(
-            parts[source_ids[slot]],
+            parts[source_ids[0, slot]],
             tiles[slot],
             (((1,), (1 if forward else 0,)), ((), ())),
             preferred_element_type=jnp.float32,
@@ -165,8 +165,9 @@
 
 def scale_phase(
     meanwhile,
-    ids_hbm,
-    live,
+    count,
+    rows_hbm,
+    cols_hbm,
     tiles_hbm,
     start_hbm,
     row_ref,
@@ -176,7 +177,11 @@
     start_ref,
     dense_ref,
     turned_ref,
-    ids,
+    row_ids,
+    col_ids,
+    lanes,
+    places,
+    lookup,
     tiles,
     flipped,
     parts,
@@ -190,28 +195,44 @@
     *sems,
 ):
     slots = tiles_hbm.shape[0]
+    sources = [rows_hbm, cols_hbm, rows_hbm, cols_hbm, start_hbm, tiles_hbm]
+    targets = [row_ids, col_ids, lanes.at[0], lanes.at[1], start_ref, tiles.at[pl.ds(0, slots)]]
     loads = [
-        pltpu.make_async_copy(ids_hbm, ids, load_sem.at[0]),
-        pltpu.make_async_copy(start_hbm, start_ref, load_sem.at[1]),
-        pltpu.make_async_copy(tiles_hbm, tiles.at[pl.ds(0, slots)], load_sem.at[2]),
+        pltpu.make_async_copy(source, target, load_sem.at[k])
+        for k, (source, target) in enumerate(zip(sources, targets))
     ]
     for load in loads:
         load.start()
-    greet()
     tiles[slots] = jnp.zeros(tiles.shape[1:], tiles.dtype)
     flipped[slots] = jnp.zeros(tiles.shape[1:], tiles.dtype)
     blocks = row_ref.shape[0]
-    places = lax.broadcasted_iota(jnp.int32, (blocks, live.shape[1]), 0)
-    to_rows = jnp.where(places == live[0:1, :], 1.0, 0.0).astype(jnp.bfloat16)
-    to_cols = jnp.where(places == live[1:2, :], 1.0, 0.0).astype(jnp.bfloat16)
-    row_ids, col_ids = ids.at[pl.ds(0, slots)], ids.at[pl.ds(slots, slots)]
+    spread(jnp.ones(row_ref.shape, jnp.float32), parts)
+    for load in loads[:4]:
+        load.wait()
+    used = count[0, 0]
+    place = lax.broadcasted_iota(jnp.int32, (blocks, slots), 0)
+    live = lax.broadcasted_iota(jnp.int32, (blocks, slots), 1) < used
+    to_rows, to_cols = (
+        jnp.concatenate([jnp.where(live & (place == lanes[k]), 1.0, 0.0)] * 3, axis=1).astype(jnp.bfloat16)
+        for k in range(2)
+    )
+    row = lax.broadcasted_iota(jnp.int32, places.shape, 0)
+    col = lax.broadcasted_iota(jnp.int32, places.shape, 1)
+    table = jnp.full(places.shape, slots, jnp.int32)
+    for slot in range(slots):
+        found = (row == row_ids[0, slot]) & (col == jnp.where(slot < used, col_ids[0, slot], -1))
+        table = jnp.where(found, slot, table)
+    places[...] = table
+    keep = pltpu.make_async_copy(places, lookup, load_sem.at[7])
+    keep.start()
+    greet()
 
     def build(out_ref, source, turn):
         def place_row(outer, carry):
             at = pl.multiple_of(outer * TILE, TILE)
             for inner in range(blocks):
-                place = inner * blocks + outer if turn else outer * blocks + inner
-                tile = source[ids[2 * slots + place]]
+                slot = lookup[inner, outer] if turn else lookup[outer, inner]
+                tile = source[slot]
                 out_ref[pl.ds(at, TILE), inner * TILE : (inner + 1) * TILE] = tile
             return carry
 
@@ -221,11 +242,10 @@
         flipped[slot] = tiles[slot].T
         return carry
 
-    spread(jnp.ones(row_ref.shape, jnp.float32), parts)
-    loads[0].wait()
-    loads[1].wait()
+    loads[4].wait()
     mean = jnp.sum(start_ref[...].astype(jnp.float32), axis=0, keepdims=True)
-    loads[2].wait()
+    keep.wait()
+    loads[5].wait()
     held_a[0, :blocks, :] = tile_sums(tiles, col_ids, parts, sums, to_rows, True)
     extra = held_a.shape[1] - blocks
     pieces = [mean[:, at : at + TILE] for at in range(0, mean.shape[1], TILE)]
@@ -243,7 +263,7 @@
     total = finish_exchange(copies, held_b, "term")
     spread(1.0 / total, parts)
 
-    held_c[0] = tile_sums(tiles, col_ids, parts, sums, to_rows, True)
+    held_c[0] = tile_sums(flipped, col_ids, parts, sums, to_rows, False)
     copies = start_exchange(held_c, "doc", *sems[4:6])
     build(turned_ref, flipped, True)
     row_scale = 1.0 / finish_exchange(copies, held_c, "doc")
@@ -257,7 +277,7 @@
 
     def weigh():
         spread(col_ref[...], parts)
-        held_e[0] = tile_sums(tiles, col_ids, parts, sums, to_rows, True)
+        held_e[0] = tile_sums(flipped, col_ids, parts, sums, to_rows, False)
         return start_exchange(held_e, "doc", *sems[8:10])
 
     return weigh
@@ -278,7 +298,11 @@
         pltpu.VMEM((docs, width), kind),
         pltpu.VMEM((terms, docs), kind),
         pltpu.VMEM((docs, terms), kind),
-        pltpu.SMEM((2 * slots + RB * CB,), jnp.int32),
+        pltpu.SMEM((1, slots), jnp.int32),
+        pltpu.SMEM((1, slots), jnp.int32),
+        pltpu.VMEM((2, 1, slots), jnp.int32),
+        pltpu.VMEM((RB, TILE), jnp.int32),
+        pltpu.SMEM((RB, TILE), jnp.int32),
         stack,
         stack,
         pltpu.VMEM((RB, 16, TILE), jnp.bfloat16),
@@ -288,23 +312,11 @@
         held(m),
         held(n),
         held(m),
-        pltpu.SemaphoreType.DMA((3,)),
+        pltpu.SemaphoreType.DMA((8,)),
     ] + semaphores(m, m, n, n, m, m, n, n, m, m)
 
 
-SCALE_REFS = 26
-
-
-def tables(tile_rows, tile_cols, tile_count):
-    slots = tile_rows.shape[1]
-    slot = jnp.arange(slots, dtype=jnp.int32)
-    used = slot < tile_count[0, 0]
-    rows, cols = tile_rows[0], tile_cols[0]
-    cell = jnp.arange(RB * CB, dtype=jnp.int32)
-    found = ((rows * CB + cols)[None, :] == cell[:, None]) & used[None, :]
-    lookup = slots + jnp.sum(jnp.where(found, slot[None, :] - slots, 0), axis=1)
-    live = jnp.stack([jnp.where(used, rows, RB), jnp.where(used, cols, CB)])
-    return jnp.concatenate([rows, cols, lookup]), jnp.concatenate([live, live, live], axis=1)
+SCALE_REFS = 30
 
 
 CODES = 32760.0
@@ -443,8 +455,9 @@
 
 
 def whole_kernel(
-    ids_hbm,
-    live,
+    count,
+    rows_hbm,
+    cols_hbm,
     tiles_hbm,
     start_hbm,
     row_ref,
@@ -475,7 +488,7 @@
     left_gram, right_gram = rest[:GRAM_REFS], rest[GRAM_REFS : 2 * GRAM_REFS]
     scale_refs = rest[2 * GRAM_REFS : 2 * GRAM_REFS + SCALE_REFS]
     weight_ref, mean_ref, start_ref, matrix, turned = scale_refs[:5]
-    held_e = scale_refs[14]
+    held_e = scale_refs[18]
     sems = rest[2 * GRAM_REFS + SCALE_REFS :]
     n, m = lax.axis_size("term"), lax.axis_size("doc")
     nz, z, c = paired()
@@ -496,7 +509,15 @@
         lax.fori_loop(0, terms // TILE, turn, 0)
 
     weigh = scale_phase(
-        turn_rows, ids_hbm, live, tiles_hbm, start_hbm, row_ref, col_ref, *scale_refs
+        turn_rows,
+        count,
+        rows_hbm,
+        cols_hbm,
+        tiles_hbm,
+        start_hbm,
+        row_ref,
+        col_ref,
+        *scale_refs,
     )
 
     def axes(flow):
@@ -812,8 +833,7 @@
     near = pltpu.VMEM((nz // 2, 2 * piece, width), f32)
     pairs = [pltpu.SemaphoreType.DMA((2, size)) for size in (m, m, wide, wide, wide, wide, m, m)]
     vector = jax.ShapeDtypeStruct((RB, TILE), f32)
-    hbm = pl.BlockSpec(memory_space=pl.ANY)
-    ids, live = tables(tile_rows, tile_cols, tile_count)
+    hbm = pl.BlockSpec(memory_space=pltpu.HBM)
     outs = pl.pallas_call(
         whole_kernel,
         out_shape=[
@@ -822,7 +842,7 @@
             jax.ShapeDtypeStruct((terms, width), bf16),
             jax.ShapeDtypeStruct((docs, width), bf16),
         ],
-        in_specs=[hbm, VMEM, hbm, hbm],
+        in_specs=[SMEM] + [hbm] * 4,
         out_specs=[VMEM] * 4,
         scratch_shapes=[
             pltpu.VMEM((terms, TILE), f32),
@@ -854,7 +874,13 @@
             collective_id=0, has_side_effects=True, vmem_limit_bytes=44 << 20
         ),
         name="whole",
-    )(ids, live, tile_values, start_block)
+    )(
+        tile_count,
+        *(
+            pltpu.with_memory_space_constraint(x, pltpu.HBM)
+            for x in (tile_rows, tile_cols, tile_values, start_block)
+        ),
+    )
     row, col, left_basis, right_basis = emit(outs)
     return (row.reshape(-1), col.reshape(-1), left_basis, right_basis)
 

time: 102 us -> 97.5 us (0.956)
  local copies, waits for them, and re-layouts: 2.64 us -> 0 us
  other arithmetic: 1.62 us -> 0 us
    unnamed x4 -> x0, local copies, waits for them, and re-layouts: 2.64 us -> none
where the time goes in v5:
time: 97.5 us; the launch traced here: 97.3 us
  Pallas kernels  95.9 us (98%)
  between operations  1.47 us (2%)
    pallas_call x1, Pallas kernels, per_device(): pl.pallas_call(whole_kernel, out_shape=[vector, vector, jax.ShapeDtypeStr...  94.5 us

profile of v5, /device:TPU:0, one launch (start us, length us, event | category | flops | bytes accessed | tf_op | source)
XLA Modules:
  0.0 97.3 jit_solution(18159370862276144691)
XLA Ops:
  1.3 94.5 %whole.1 = (f32[16,128]{1,0:T(8,128)S(1)}, f32[16,128]{1,0:T(8,128)S(1)}, bf16[2048,256]{1,0:T(8,128)(2,1)S(1)}, bf16[2048,256]{1,0:T(8,128)(2,1)S(1)}) custom-call(s32[1,1]{1,0:T(1,128)S(6)} %copy.9.count, s32[1,48]{1,0:T(1,128)} %rows_hbm.1, s32[1,48]{1,0:T(1,128)} %cols_hbm.1, bf16[48,128,128]{2,1,0:T(8,128)(2,1)} %tiles_hbm.1, bf16[2048,256]{1,0:T(8,128)(2,1)} %start_hbm.1), custom_call_target="tpu_custom_call" | custom-call | tf_op jit(solution)/shard_map/whole/pallas_call | solution.py:837
  95.8 1.4 %emit.1 = (f32[16,128]{1,0:T(8,128)}, f32[16,128]{1,0:T(8,128)}, bf16[2048,256]{1,0:T(8,128)(2,1)}, bf16[2048,256]{1,0:T(8,128)(2,1)}) custom-call(f32[16,128]{1,0:T(8,128)S(1)} %get-tuple-element.12.row_ref, f32[16,128]{1,0:T(8,128)S(1)} %get-tuple-element.13.col_ref, bf16[2048,256]{1,0:T(8,128)(2,1)S(1)} %get-tuple-element.14.left_ref, ...), custom_call_target="tpu_custom_call" | custom-call | tf_op jit(solution)/shard_map/emit/pallas_call | solution.py:812

commit v6 on v5

--- a/solution.py
+++ b/solution.py
@@ -19,26 +19,30 @@
 
 
 BLOCK = 64
-GROUP = 8
+GROUP = 16
 
 
 def block_inverse(block, low, high):
-    rows = lax.broadcasted_iota(jnp.int32, block.shape, 0)
-    pivots = jnp.ones_like(block)
+    finished = []
+    lanes = lax.broadcasted_iota(jnp.int32, (GROUP, block.shape[1]), 1)
+    inside = (lanes >= high) & (lanes < high + BLOCK)
     for base in range(0, BLOCK, GROUP):
+        rows = lax.broadcasted_iota(jnp.int32, block.shape, 0)
+        pivots = jnp.ones((GROUP, block.shape[1]), block.dtype)
         factors = []
-        for at in range(base, base + GROUP):
-            column = jnp.broadcast_to(block[:, low + at : low + at + 1], block.shape)
+        for at in range(GROUP):
+            lane = low + base + at
+            column = jnp.broadcast_to(block[:, lane : lane + 1], block.shape)
             for past, factor in enumerate(factors):
-                column = column - factor * column[base + past : base + past + 1, :]
-            pivots = jnp.where(rows == at, column, pivots)
+                column = column - factor * column[past : past + 1, :]
+            pivots = jnp.where(rows[:GROUP] == at, column[:GROUP], pivots)
             ratio = column * (1.0 / column[at : at + 1, :])
             factors.append(jnp.where(rows > at, ratio, 0.0))
         for at, factor in enumerate(factors):
-            block = block - factor * block[base + at : base + at + 1, :]
-    lanes = lax.broadcasted_iota(jnp.int32, block.shape, 1)
-    inside = (lanes >= high) & (lanes < high + BLOCK)
-    return jnp.where(inside, block * lax.rsqrt(pivots), 0.0)
+            block = block - factor * block[at : at + 1, :]
+        finished.append(jnp.where(inside, block[:GROUP] * lax.rsqrt(pivots), 0.0))
+        block = block[GROUP:]
+    return jnp.concatenate(finished, axis=0)
 
 
 def inverse_kernel(gram_ref, o_ref, work):
@@ -47,34 +51,31 @@
     rows = lax.broadcasted_iota(jnp.int32, (width, width), 0)
     lanes = lax.broadcasted_iota(jnp.int32, (width, width), 1)
     work[:, width:] = jnp.where(rows == lanes, 1.0, 0.0)
+    rows = lax.broadcasted_iota(jnp.int32, (BLOCK, TILE), 0)
+    lanes = lax.broadcasted_iota(jnp.int32, (BLOCK, TILE), 1)
+    block = gram_ref[:BLOCK, :TILE]
     for index in range(width // BLOCK):
         start = index * BLOCK
+        after = start + BLOCK
         near = start // TILE * TILE
         low = start - near
         high = TILE - BLOCK - low
-        block = work[start : start + BLOCK, near : near + TILE]
-        rows = lax.broadcasted_iota(jnp.int32, block.shape, 0)
-        lanes = lax.broadcasted_iota(jnp.int32, block.shape, 1)
         inside = (lanes >= low) & (lanes < low + BLOCK)
         block = jnp.where(inside, block, jnp.where(lanes - high == rows, 1.0, 0.0))
         inverse = block_inverse(block, low, high)
-        panel = work[start : start + BLOCK, :]
-        solved = jnp.dot(
-            inverse,
-            jnp.concatenate([panel, panel], axis=0),
-            precision=PRECISE,
-            preferred_element_type=jnp.float32,
-        )
-        o_ref[start : start + BLOCK, :] = solved[:, width:]
-        if start + BLOCK < width:
-            update = lax.dot_general(
-                solved[:, :width],
-                solved,
-                (((0,), (0,)), ((), ())),
-                precision=PRECISE,
-                preferred_element_type=jnp.float32,
+        inverse = inverse[:, high : high + BLOCK]
+        if after < width:
+            near = after // TILE * TILE
+            low = after - near
+            window = precise(inverse, work[start:after, near : near + TILE], ((1,), (0,)))
+            block = work[after : after + BLOCK, near : near + TILE] - precise(
+                window[:, low : low + BLOCK], window, ((0,), (0,))
             )
-            work[start + BLOCK :, :] = work[start + BLOCK :, :] - update[start + BLOCK :, :]
+        solved = precise(inverse, work[start:after, :], ((1,), (0,)))
+        o_ref[start:after, :] = solved[:, width:]
+        if after < width:
+            update = precise(solved[:, after:width], solved, ((0,), (0,)))
+            work[after:, :] = work[after:, :] - update
 
 
 def greet():
@@ -474,6 +475,7 @@
     recv_b,
     gathered,
     factor,
+    right_sum,
     near_send,
     near_recv,
     far_send,
@@ -634,14 +636,34 @@
         value = decode(gathered[flow, block]) * row_turn[at, :]
         factor[at, lanes(flow)] = value.astype(jnp.bfloat16)
 
+    def multiply(block, first_flow, flows, fresh):
+        at = pl.ds(pl.multiple_of(block * share, share), share)
+        cols = slice(first_flow * TILE, (first_flow + flows) * TILE)
+        tall = docs // 2
+
+        def rows_of(k, carry):
+            rows = pl.ds(pl.multiple_of(k * tall, tall), tall)
+            product = jnp.dot(
+                turned[rows, at], factor[at, cols], preferred_element_type=jnp.float32
+            )
+            right_sum[rows, cols] = product if fresh else right_sum[rows, cols] + product
+            return carry
+
+        lax.fori_loop(0, 2, rows_of, 0)
+
+    def source_of(flow, s1, s2):
+        a, n1, b, n2 = axes(flow)
+        return device(flow, lax.rem(a - s1 + n1, n1), lax.rem(b - s2 + n2, n2))
+
     for flow in range(2):
         unpack(flow, doc)
+    multiply(doc, 0, 2, True)
     for flow in range(2):
         a, n1, b, n2 = axes(flow)
         for s1 in range(n1):
             if s1:
                 copies_c[flow, s1].wait()
-            source = device(flow, lax.rem(a - s1 + n1, n1), b)
+            source = source_of(flow, s1, 0)
             for s2 in range(1, n2):
                 copies_d[flow, s1, s2] = remote(
                     gathered.at[flow, source],
@@ -652,26 +674,39 @@
                     device(flow, a, lax.rem(b + s2, n2)),
                 )
                 copies_d[flow, s1, s2].start()
-    for flow in range(2):
-        a, n1, b, n2 = axes(flow)
-        for s1 in range(1, n1):
-            unpack(flow, device(flow, lax.rem(a - s1 + n1, n1), b))
     next(left_steps)
     for flow in range(2):
-        a, n1, b, n2 = axes(flow)
-        for s1 in range(n1):
-            for s2 in range(1, n2):
-                copies_d[flow, s1, s2].wait()
-                unpack(
-                    flow,
-                    device(flow, lax.rem(a - s1 + n1, n1), lax.rem(b - s2 + n2, n2)),
-                )
+        for s1 in range(1, axes(flow)[1]):
+            block = source_of(flow, s1, 0)
+            unpack(flow, block)
+            multiply(block, flow, 1, False)
+    for flow in range(2):
+        for s2 in range(1, axes(flow)[3]):
+            copies_d[flow, 0, s2].wait()
+            block = source_of(flow, 0, s2)
+            unpack(flow, block)
+            multiply(block, flow, 1, False)
+    across = [(dx, dy) for dx in range(1, nx) for dy in range(1, ny)]
+    for dx, dy in across:
+        block = source_of(0, dx, dy)
+        copies_d[0, dx, dy].wait()
+        unpack(0, block)
+        copies_d[1, dy, dx].wait()
+        unpack(1, block)
+        if (dx, dy) != across[-1]:
+            multiply(block, 0, 2, False)
+    next(left_steps)
+
     wide = 2 * piece
+    last_terms = pl.ds(pl.multiple_of(block * share, share), share)
 
     def right_product(chunk, core):
         at = pl.ds(pl.multiple_of(core * (docs // 2) + chunk * wide, wide), wide)
-        product = jnp.dot(turned[at, :], factor[...], preferred_element_type=jnp.float32)
-        return product * jnp.concatenate([col_turn[at, :]] * (width // TILE), axis=1)
+        product = jnp.dot(
+            turned[at, last_terms], factor[last_terms, :], preferred_element_type=jnp.float32
+        )
+        column = jnp.concatenate([col_turn[at, :]] * (width // TILE), axis=1)
+        return (right_sum[at, :] + product) * column
 
     sibling = 2 * z + 1 - c
     chunks = [lax.rem(z // 2 + 1 + j, nz // 2) for j in range(nz // 2)]
@@ -701,8 +736,6 @@
             at = pl.ds(pl.multiple_of(inner * piece, piece), piece)
             far_send[step] = encode(near_recv[j, at, :])
             far_copy(step).start()
-        if j == 0:
-            next(left_steps)
     for _ in left_steps:
         pass
     unpack_gram(left_gram[1], gram)
@@ -855,6 +888,7 @@
             coded_b,
             coded,
             pltpu.VMEM((terms, width), bf16),
+            pltpu.VMEM((docs, width), f32),
             near,
             near,
             far,

time: 97.5 us -> 94.7 us (0.971)
  Pallas kernels: 95.9 us -> 93 us
    pallas_call x1, Pallas kernels: 94.5 us -> 91.7 us  [per_device(): pl.pallas_call(whole_kernel, out_shape=[vector, vector, jax.ShapeDtypeStr...]
where the time goes in v6:
time: 94.7 us; the launch traced here: 94.5 us
  Pallas kernels  93 us (98%)
  between operations  1.47 us (2%)
    pallas_call x1, Pallas kernels, per_device(): pl.pallas_call(whole_kernel, out_shape=[vector, vector, jax.ShapeDtypeStr...  91.7 us

profile of v6, /device:TPU:0, one launch (start us, length us, event | category | flops | bytes accessed | tf_op | source)
XLA Modules:
  0.0 94.5 jit_solution(14864014359649331696)
XLA Ops:
  1.3 91.7 %whole.1 = (f32[16,128]{1,0:T(8,128)S(1)}, f32[16,128]{1,0:T(8,128)S(1)}, bf16[2048,256]{1,0:T(8,128)(2,1)S(1)}, bf16[2048,256]{1,0:T(8,128)(2,1)S(1)}) custom-call(s32[1,1]{1,0:T(1,128)S(6)} %copy.9.count, s32[1,48]{1,0:T(1,128)} %rows_hbm.1, s32[1,48]{1,0:T(1,128)} %cols_hbm.1, bf16[48,128,128]{2,1,0:T(8,128)(2,1)} %tiles_hbm.1, bf16[2048,256]{1,0:T(8,128)(2,1)} %start_hbm.1), custom_call_target="tpu_custom_call" | custom-call | tf_op jit(solution)/shard_map/whole/pallas_call | solution.py:870
  92.9 1.4 %emit.1 = (f32[16,128]{1,0:T(8,128)}, f32[16,128]{1,0:T(8,128)}, bf16[2048,256]{1,0:T(8,128)(2,1)}, bf16[2048,256]{1,0:T(8,128)(2,1)}) custom-call(f32[16,128]{1,0:T(8,128)S(1)} %get-tuple-element.12.row_ref, f32[16,128]{1,0:T(8,128)S(1)} %get-tuple-element.13.col_ref, bf16[2048,256]{1,0:T(8,128)(2,1)S(1)} %get-tuple-element.14.left_ref, ...), custom_call_target="tpu_custom_call" | custom-call | tf_op jit(solution)/shard_map/emit/pallas_call | solution.py:845

commit v7 on v6

--- a/solution.py
+++ b/solution.py
@@ -522,14 +522,23 @@
         *scale_refs,
     )
 
+    halves_of = [(0, 1), (2, 3)]
+    part_rows = share // 2
+
     def axes(flow):
-        return (x, nx, y, ny) if flow == 0 else (y, ny, x, nx)
+        return (x, nx, y, ny) if flow % 2 == 0 else (y, ny, x, nx)
 
     def device(flow, first, second):
-        return second * nx + first if flow == 0 else first * nx + second
+        return second * nx + first if flow % 2 == 0 else first * nx + second
+
+    def step_of(flow, dx, dy):
+        return (dx, dy) if flow % 2 == 0 else (dy, dx)
 
     def lanes(flow):
-        return slice(flow * TILE, (flow + 1) * TILE)
+        return slice(flow // 2 * TILE, (flow // 2 + 1) * TILE)
+
+    def part(flow):
+        return slice(flow % 2 * part_rows, (flow % 2 + 1) * part_rows)
 
     def prepare(block, carry):
         at = pl.ds(pl.multiple_of(block * TILE, TILE), TILE)
@@ -543,20 +552,15 @@
     steps = [(dx, dy) for dx in range(nx) for dy in range(ny)]
     steps.sort(key=lambda s: -((s[0] > 0) + (s[1] > 0)))
     copies_a, copies_b = {}, {}
-    for dx, dy in steps:
-        target = lax.rem(y + dy, ny) * nx + lax.rem(x + dx, nx)
-        at = pl.ds(pl.multiple_of(target * share, share), share)
-        product = jnp.dot(matrix[at, :], scaled[...], preferred_element_type=jnp.float32)
-        column = row_turn[at, :]
-        product = product * jnp.concatenate([column] * (width // TILE), axis=1)
-        partial[dy * nx + dx] = product
-        for flow in range(2):
+
+    def send_first(half, dx, dy):
+        for flow in halves_of[half]:
             a, n1, b, n2 = axes(flow)
-            s1, s2 = (dx, dy) if flow == 0 else (dy, dx)
+            s1, s2 = step_of(flow, dx, dy)
             if s1 == 0:
                 continue
             slot = s1 * n2 + s2
-            send_a[flow, slot] = encode(product[:, lanes(flow)])
+            send_a[flow, slot] = encode(partial[dy * nx + dx, part(flow), lanes(flow)])
             copies_a[flow, s1, s2] = remote(
                 send_a.at[flow, slot],
                 recv_a.at[flow, slot],
@@ -567,11 +571,22 @@
             )
             copies_a[flow, s1, s2].start()
 
+    for dx, dy in steps:
+        target = lax.rem(y + dy, ny) * nx + lax.rem(x + dx, nx)
+        at = pl.ds(pl.multiple_of(target * share, share), share)
+        product = jnp.dot(matrix[at, :], scaled[...], preferred_element_type=jnp.float32)
+        column = row_turn[at, :]
+        product = product * jnp.concatenate([column] * (width // TILE), axis=1)
+        partial[dy * nx + dx] = product
+        send_first(0, dx, dy)
+    for dx, dy in steps:
+        send_first(1, dx, dy)
+
     weight_copies = weigh()
 
     def own(flow, s2):
-        dx, dy = (0, s2) if flow == 0 else (s2, 0)
-        return partial[dy * nx + dx, :, lanes(flow)]
+        dx, dy = step_of(flow, 0, s2)
+        return partial[dy * nx + dx, part(flow), lanes(flow)]
 
     def landed(flow, s2):
         a, n1, b, n2 = axes(flow)
@@ -581,7 +596,7 @@
             total = total + decode(recv_a[flow, s1 * n2 + s2])
         return total
 
-    for flow in range(2):
+    for flow in range(4):
         a, n1, b, n2 = axes(flow)
         for s2 in range(1, n2):
             send_b[flow, s2] = encode(landed(flow, s2))
@@ -602,13 +617,14 @@
     )
     copies_c, copies_d = {}, {}
     left = []
-    for flow in range(2):
+    for flow in range(4):
         a, n1, b, n2 = axes(flow)
         total = landed(flow, 0)
         for s2 in range(1, n2):
             copies_b[flow, s2].wait()
             total = total + decode(recv_b[flow, s2])
-        total = total - weight * (mean_ref[flow : flow + 1, :] * (1.0 / docs_total))
+        mean = mean_ref[flow // 2 : flow // 2 + 1, :]
+        total = total - weight[part(flow)] * (mean * (1.0 / docs_total))
         left.append(total)
         gathered[flow, doc] = encode(total)
         for s1 in range(1, n1):
@@ -622,17 +638,18 @@
             )
             copies_c[flow, s1].start()
 
+    left = [jnp.concatenate(left[2 * half : 2 * half + 2], axis=0) for half in range(2)]
     left_share = jnp.concatenate(left, axis=1)
     pack_gram(
         precise(left_share, left_share, ((0,), (0,))) * (1.0 / (terms * n)),
-        [jnp.sum(weight * part, axis=0, keepdims=True) for part in left],
+        [jnp.sum(weight * half, axis=0, keepdims=True) for half in left],
         left_gram[0],
     )
     left_steps = gram_steps(*left_gram)
     next(left_steps)
 
     def unpack(flow, block):
-        at = pl.ds(pl.multiple_of(block * share, share), share)
+        at = pl.ds(pl.multiple_of(block * share + part(flow).start, part_rows), part_rows)
         value = decode(gathered[flow, block]) * row_turn[at, :]
         factor[at, lanes(flow)] = value.astype(jnp.bfloat16)
 
@@ -655,10 +672,20 @@
         a, n1, b, n2 = axes(flow)
         return device(flow, lax.rem(a - s1 + n1, n1), lax.rem(b - s2 + n2, n2))
 
-    for flow in range(2):
+    for flow in range(4):
         unpack(flow, doc)
     multiply(doc, 0, 2, True)
-    for flow in range(2):
+
+    def landed_from(dx, dy, half):
+        block = source_of(0, dx, dy)
+        for flow in halves_of[half]:
+            s1, s2 = step_of(flow, dx, dy)
+            if s2:
+                copies_d[flow, s1, s2].wait()
+            unpack(flow, block)
+        return block
+
+    for flow in range(4):
         a, n1, b, n2 = axes(flow)
         for s1 in range(n1):
             if s1:
@@ -675,67 +702,66 @@
                 )
                 copies_d[flow, s1, s2].start()
     next(left_steps)
-    for flow in range(2):
-        for s1 in range(1, axes(flow)[1]):
-            block = source_of(flow, s1, 0)
-            unpack(flow, block)
-            multiply(block, flow, 1, False)
-    for flow in range(2):
-        for s2 in range(1, axes(flow)[3]):
-            copies_d[flow, 0, s2].wait()
-            block = source_of(flow, 0, s2)
-            unpack(flow, block)
-            multiply(block, flow, 1, False)
-    across = [(dx, dy) for dx in range(1, nx) for dy in range(1, ny)]
-    for dx, dy in across:
-        block = source_of(0, dx, dy)
-        copies_d[0, dx, dy].wait()
-        unpack(0, block)
-        copies_d[1, dy, dx].wait()
-        unpack(1, block)
-        if (dx, dy) != across[-1]:
-            multiply(block, 0, 2, False)
-    next(left_steps)
+    others = [step for step in reversed(steps) if step != (0, 0)]
 
     wide = 2 * piece
-    last_terms = pl.ds(pl.multiple_of(block * share, share), share)
-
-    def right_product(chunk, core):
-        at = pl.ds(pl.multiple_of(core * (docs // 2) + chunk * wide, wide), wide)
-        product = jnp.dot(
-            turned[at, last_terms], factor[last_terms, :], preferred_element_type=jnp.float32
-        )
-        column = jnp.concatenate([col_turn[at, :]] * (width // TILE), axis=1)
-        return (right_sum[at, :] + product) * column
-
     sibling = 2 * z + 1 - c
     chunks = [lax.rem(z // 2 + 1 + j, nz // 2) for j in range(nz // 2)]
-    near_copies = []
-    for j, chunk in enumerate(chunks):
-        near_send[j] = right_product(chunk, 1 - c)
-        copy = remote(near_send.at[j], near_recv.at[j], sems[8].at[j], sems[9].at[j], "term", sibling)
-        copy.start()
-        near_copies.append(copy)
-
-    def far_copy(step):
+
+    def far_copy(half, step):
         there = lax.rem(z + step, nz)
         return remote(
-            far_send.at[step], far_recv.at[step], sems[10].at[step], sems[11].at[step], "term", 2 * there + c
+            far_send.at[half, step],
+            far_recv.at[half, step],
+            sems[10].at[half, step],
+            sems[11].at[half, step],
+            "term",
+            2 * there + c,
         )
 
-    for j, chunk in enumerate(chunks):
-        product = right_product(chunk, c)
-        near_copies[j].wait()
-        near_recv[j] = near_recv[j] + product
-        last = j + 1 == len(chunks)
-        for k in range(2):
-            if last and k:
-                continue
-            inner = 1 - lax.rem(z, 2) if last else k
-            step = lax.rem(2 * chunk + inner - z + nz, nz)
-            at = pl.ds(pl.multiple_of(inner * piece, piece), piece)
-            far_send[step] = encode(near_recv[j, at, :])
-            far_copy(step).start()
+    for half in range(2):
+        for dx, dy in others:
+            block = landed_from(dx, dy, half)
+            if (dx, dy) != others[-1]:
+                multiply(block, half, 1, False)
+        cols = slice(half * TILE, (half + 1) * TILE)
+        last_terms = pl.ds(pl.multiple_of(block * share, share), share)
+
+        def right_product(chunk, core):
+            at = pl.ds(pl.multiple_of(core * (docs // 2) + chunk * wide, wide), wide)
+            product = jnp.dot(
+                turned[at, last_terms], factor[last_terms, cols], preferred_element_type=jnp.float32
+            )
+            return (right_sum[at, cols] + product) * col_turn[at, :]
+
+        near_copies = []
+        for j, chunk in enumerate(chunks):
+            near_send[half, j] = right_product(chunk, 1 - c)
+            copy = remote(
+                near_send.at[half, j],
+                near_recv.at[half, j],
+                sems[8].at[half, j],
+                sems[9].at[half, j],
+                "term",
+                sibling,
+            )
+            copy.start()
+            near_copies.append(copy)
+        if half == 0:
+            next(left_steps)
+        for j, chunk in enumerate(chunks):
+            product = right_product(chunk, c)
+            near_copies[j].wait()
+            near_recv[half, j] = near_recv[half, j] + product
+            last = j + 1 == len(chunks)
+            for k in range(2):
+                if last and k:
+                    continue
+                inner = 1 - lax.rem(z, 2) if last else k
+                step = lax.rem(2 * chunk + inner - z + nz, nz)
+                at = pl.ds(pl.multiple_of(inner * piece, piece), piece)
+                far_send[half, step] = encode(near_recv[half, j, at, :])
+                far_copy(half, step).start()
     for _ in left_steps:
         pass
     unpack_gram(left_gram[1], gram)
@@ -756,7 +782,13 @@
 
     def finish_left(block):
         at = pl.ds(pl.multiple_of(block * share, share), share)
-        value = jnp.concatenate([decode(gathered[flow, block]) for flow in range(2)], axis=1)
+        value = jnp.concatenate(
+            [
+                jnp.concatenate([decode(gathered[flow, block]) for flow in flows], axis=0)
+                for flows in halves_of
+            ],
+            axis=1,
+        )
         left_out[at, :] = whitened(value).astype(jnp.bfloat16)
 
     extra = left_gram[1].shape[1] - 8
@@ -766,10 +798,14 @@
     lean = precise(jnp.broadcast_to(weighted, (8, width)), inverse_ref[...], ((1,), (1,)))[0:1]
     split_inverse()
     own_rows = pl.ds(pl.multiple_of(lax.rem(z, 2) * piece, piece), piece)
-    total = near_recv[len(chunks) - 1, own_rows, :]
-    for step in range(1, nz):
-        far_copy(step).wait()
-        total = total + decode(far_recv[step])
+    totals = []
+    for half in range(2):
+        total = near_recv[half, len(chunks) - 1, own_rows, :]
+        for step in range(1, nz):
+            far_copy(half, step).wait()
+            total = total + decode(far_recv[half, step])
+        totals.append(total)
+    total = jnp.concatenate(totals, axis=1)
     block = precise(total, inverse_ref[...], ((1,), (1,))) - lean * (1.0 / docs_total)
 
     me = c * nz + z
@@ -860,11 +896,12 @@
     share, piece = terms // m, docs // n
     wide = max(grid_of(m))
     int16, f32, bf16 = jnp.int16, jnp.float32, jnp.bfloat16
-    coded = pltpu.VMEM((2, m, share + 16, TILE), int16)
-    coded_b = pltpu.VMEM((2, wide, share + 16, TILE), int16)
-    far = pltpu.VMEM((nz, piece + 16, width), int16)
-    near = pltpu.VMEM((nz // 2, 2 * piece, width), f32)
-    pairs = [pltpu.SemaphoreType.DMA((2, size)) for size in (m, m, wide, wide, wide, wide, m, m)]
+    coded = pltpu.VMEM((4, m, share // 2 + 16, TILE), int16)
+    coded_b = pltpu.VMEM((4, wide, share // 2 + 16, TILE), int16)
+    far = pltpu.VMEM((2, nz, piece + 16, TILE), int16)
+    near = pltpu.VMEM((2, nz // 2, 2 * piece, TILE), f32)
+    pairs = [pltpu.SemaphoreType.DMA((4, size)) for size in (m, m, wide, wide, wide, wide, m, m)]
+    pairs += [pltpu.SemaphoreType.DMA((2, nz))] * 4
     vector = jax.ShapeDtypeStruct((RB, TILE), f32)
     hbm = pl.BlockSpec(memory_space=pltpu.HBM)
     outs = pl.pallas_call(
@@ -903,7 +940,7 @@
         + gram_scratch()
         + scale_scratch(terms, docs, width, tile_values.shape[0], tile_values.dtype)
         + pairs
-        + semaphores(*[nz] * 8),
+        + semaphores(*[nz] * 4),
         compiler_params=pltpu.CompilerParams(
             collective_id=0, has_side_effects=True, vmem_limit_bytes=44 << 20
         ),

time: 94.7 us -> 92.2 us (0.974)
  Pallas kernels: 93 us -> 90.6 us
    pallas_call x1, Pallas kernels: 91.7 us -> 89.2 us  [per_device(): pl.pallas_call(whole_kernel, out_shape=[vector, vector, jax.ShapeDtypeStr...]
where the time goes in v7:
time: 92.2 us; the launch traced here: 92 us
  Pallas kernels  90.6 us (98%)
  between operations  1.47 us (2%)
    pallas_call x1, Pallas kernels, per_device(): pl.pallas_call(whole_kernel, out_shape=[vector, vector, jax.ShapeDtypeStr...  89.2 us

profile of v7, /device:TPU:0, one launch (start us, length us, event | category | flops | bytes accessed | tf_op | source)
XLA Modules:
  0.0 92.0 jit_solution(8445104178492155643)
XLA Ops:
  1.3 89.2 %whole.1 = (f32[16,128]{1,0:T(8,128)S(1)}, f32[16,128]{1,0:T(8,128)S(1)}, bf16[2048,256]{1,0:T(8,128)(2,1)S(1)}, bf16[2048,256]{1,0:T(8,128)(2,1)S(1)}) custom-call(s32[1,1]{1,0:T(1,128)S(6)} %copy.9.count, s32[1,48]{1,0:T(1,128)} %rows_hbm.1, s32[1,48]{1,0:T(1,128)} %cols_hbm.1, bf16[48,128,128]{2,1,0:T(8,128)(2,1)} %tiles_hbm.1, bf16[2048,256]{1,0:T(8,128)(2,1)} %start_hbm.1), custom_call_target="tpu_custom_call" | custom-call | tf_op jit(solution)/shard_map/whole/pallas_call | solution.py:907
  90.5 1.4 %emit.1 = (f32[16,128]{1,0:T(8,128)}, f32[16,128]{1,0:T(8,128)}, bf16[2048,256]{1,0:T(8,128)(2,1)}, bf16[2048,256]{1,0:T(8,128)(2,1)}) custom-call(f32[16,128]{1,0:T(8,128)S(1)} %get-tuple-element.12.row_ref, f32[16,128]{1,0:T(8,128)S(1)} %get-tuple-element.13.col_ref, bf16[2048,256]{1,0:T(8,128)(2,1)S(1)} %get-tuple-element.14.left_ref, ...), custom_call_target="tpu_custom_call" | custom-call | tf_op jit(solution)/shard_map/emit/pallas_call | solution.py:881

commit v8 on v7

--- a/solution.py
+++ b/solution.py
@@ -45,7 +45,7 @@
     return jnp.concatenate(finished, axis=0)
 
 
-def inverse_kernel(gram_ref, o_ref, work):
+def inverse_kernel(gram_ref, o_ref, work, meanwhile=None):
     width = gram_ref.shape[0]
     work[:, :width] = gram_ref[...]
     rows = lax.broadcasted_iota(jnp.int32, (width, width), 0)
@@ -60,6 +60,8 @@
         near = start // TILE * TILE
         low = start - near
         high = TILE - BLOCK - low
+        if meanwhile is not None:
+            meanwhile(width // BLOCK - 1 - index)
         inside = (lanes >= low) & (lanes < low + BLOCK)
         block = jnp.where(inside, block, jnp.where(lanes - high == rows, 1.0, 0.0))
         inverse = block_inverse(block, low, high)
@@ -360,8 +362,16 @@
     )
 
 
+def whitened(value, halves):
+    high = value.astype(jnp.bfloat16)
+    low = (value - high.astype(jnp.float32)).astype(jnp.bfloat16)
+    parts = [(high, 0), (low, 0), (high, 1)]
+    total = [jnp.dot(v, halves[k], preferred_element_type=jnp.float32) for v, k in parts]
+    return total[0] + (total[1] + total[2])
+
+
 def pack_gram(gram, extras, packed):
-    groups, rows = packed.shape[0], packed.shape[1] - 8
+    groups, rows = packed.shape[0], packed.shape[1] - 1
     row = lax.broadcasted_iota(jnp.int32, (TILE, TILE), 0)
     lane = lax.broadcasted_iota(jnp.int32, (TILE, TILE), 1)
     last = gram[TILE:, TILE:]
@@ -369,16 +379,14 @@
     packed_rows = jnp.concatenate(packed_rows, axis=0)
     diagonal = jnp.sum(jnp.where(row == lane, last, 0.0), axis=0, keepdims=True)
     extras = [diagonal] + extras
-    extras.append(jnp.zeros((8 - len(extras), TILE), jnp.float32))
+    zero = jnp.zeros((1, TILE), jnp.float32)
     for group in range(groups):
         packed[group, :rows, :] = packed_rows[group * rows : (group + 1) * rows]
-        packed[group, rows:, :] = (
-            jnp.concatenate(extras, axis=0) if group == 0 else jnp.zeros((8, TILE), jnp.float32)
-        )
+        packed[group, rows:, :] = extras[group] if group < len(extras) else zero
 
 
 def unpack_gram(packed, gram):
-    rows = packed.shape[1] - 8
+    rows = packed.shape[1] - 1
     row = lax.broadcasted_iota(jnp.int32, (TILE, TILE), 0)
     lane = lax.broadcasted_iota(jnp.int32, (TILE, TILE), 1)
     half = packed.shape[0] // 2
@@ -445,7 +453,7 @@
 
 def gram_scratch():
     nz, m = lax.axis_size("term") // 2, lax.axis_size("doc")
-    rows = TILE // m + 8
+    rows = TILE // m + 1
     packed = pltpu.VMEM((2 * m, rows, TILE), jnp.float32)
     return [packed, packed, packed, pltpu.VMEM((nz, rows, TILE), jnp.float32)] + semaphores(
         2 * m, 2 * m, nz, nz, 2 * m, 2 * m
@@ -464,7 +472,8 @@
     row_ref,
     col_ref,
     left_out,
-    right_out,
+    right_parts,
+    halves,
     row_turn,
     col_turn,
     scaled,
@@ -480,9 +489,7 @@
     near_recv,
     far_send,
     far_recv,
-    right_parts,
     inverse_ref,
-    halves,
     gram,
     work,
     *rest,
@@ -498,7 +505,7 @@
     nx, ny = grid_of(m)
     x, y = lax.rem(doc, nx), doc // nx
     terms, width = left_out.shape
-    docs = right_out.shape[0]
+    docs = start_hbm.shape[0]
     share, piece = terms // m, docs // n
     docs_total = docs * m
 
@@ -547,7 +554,7 @@
         scaled[at, :] = (column * start_ref[at, :].astype(jnp.float32)).astype(jnp.bfloat16)
         return carry
 
-    lax.fori_loop(0, docs // TILE, prepare, 0)
+    lax.fori_loop(0, docs // TILE, prepare, 0, unroll=4)
 
     steps = [(dx, dy) for dx in range(nx) for dy in range(ny)]
     steps.sort(key=lambda s: -((s[0] > 0) + (s[1] > 0)))
@@ -773,13 +780,6 @@
         halves[0] = high
         halves[1] = (whiten - high.astype(jnp.float32)).astype(jnp.bfloat16)
 
-    def whitened(value):
-        high = value.astype(jnp.bfloat16)
-        low = (value - high.astype(jnp.float32)).astype(jnp.bfloat16)
-        parts = [(high, 0), (low, 0), (high, 1)]
-        total = [jnp.dot(v, halves[k], preferred_element_type=jnp.float32) for v, k in parts]
-        return total[0] + (total[1] + total[2])
-
     def finish_left(block):
         at = pl.ds(pl.multiple_of(block * share, share), share)
         value = jnp.concatenate(
@@ -789,11 +789,11 @@
             ],
             axis=1,
         )
-        left_out[at, :] = whitened(value).astype(jnp.bfloat16)
-
-    extra = left_gram[1].shape[1] - 8
+        left_out[at, :] = whitened(value, halves).astype(jnp.bfloat16)
+
+    extra = left_gram[1].shape[1] - 1
     weighted = jnp.concatenate(
-        [left_gram[1][0, extra + 1 + k : extra + 2 + k, :] for k in range(width // TILE)], axis=1
+        [left_gram[1][1 + k, extra:, :] for k in range(width // TILE)], axis=1
     )
     lean = precise(jnp.broadcast_to(weighted, (8, width)), inverse_ref[...], ((1,), (1,)))[0:1]
     split_inverse()
@@ -815,14 +815,9 @@
     right_steps = gram_steps(*right_gram)
     next(right_steps)
     right_parts[me] = encode(block)
-    for k in range(m // 4):
-        finish_left(k)
-    next(right_steps)
-    for k in range(m // 4, 3 * m // 4):
-        finish_left(k)
-    next(right_steps)
     far_copies = []
-    for step in range(1, nz):
+
+    def send_part(step):
         copy = remote(
             right_parts.at[me],
             right_parts.at[me],
@@ -833,60 +828,91 @@
         )
         copy.start()
         far_copies.append(copy)
+
+    send_part(1)
     copy = remote(
         right_parts.at[me], right_parts.at[me], sems[14].at[0], sems[15].at[0], "term", sibling
     )
     copy.start()
     near_copies = [copy]
+    for k in range(m // 4):
+        finish_left(k)
+    next(right_steps)
+    for k in range(m // 4, 3 * m // 4):
+        finish_left(k)
+    next(right_steps)
+    for step in range(2, nz):
+        send_part(step)
     for k in range(3 * m // 4, m):
         finish_left(k)
     for _ in right_steps:
         pass
     unpack_gram(right_gram[1], gram)
-    inverse_kernel(gram, inverse_ref, work)
+    def pass_on(left):
+        if left:
+            return
+        for step in range(1, nz):
+            far_copies[step - 1].wait()
+            t = c * nz + lax.rem(z - step + nz, nz)
+            copy = remote(
+                right_parts.at[t],
+                right_parts.at[t],
+                sems[14].at[step],
+                sems[15].at[step],
+                "term",
+                sibling,
+            )
+            copy.start()
+            near_copies.append(copy)
+
+    inverse_kernel(gram, inverse_ref, work, pass_on)
     split_inverse()
 
-    def finish_right(t):
-        at = pl.ds(pl.multiple_of(t * piece, piece), piece)
-        right_out[at, :] = whitened(decode(right_parts[t])).astype(jnp.bfloat16)
-
-    for step in range(1, nz):
-        far_copies[step - 1].wait()
-        t = c * nz + lax.rem(z - step + nz, nz)
-        copy = remote(
-            right_parts.at[t], right_parts.at[t], sems[14].at[step], sems[15].at[step], "term", sibling
-        )
-        copy.start()
-        near_copies.append(copy)
-    for step in range(nz):
-        finish_right(c * nz + lax.rem(z - step + nz, nz))
-    for step, copy in enumerate(near_copies):
+    for copy in near_copies:
         copy.wait()
-        finish_right((1 - c) * nz + lax.rem(z - step + nz, nz))
-
-
-def emit_kernel(row_ref, col_ref, left_ref, right_ref, *rest):
-    outs, sems = rest[:4], rest[4]
+
+
+def emit_kernel(row_ref, col_ref, left_ref, parts_ref, halves, *rest):
+    outs, right, sems = rest[:4], rest[4], rest[5]
+    right_out = outs[3]
     copies = [
         pltpu.make_async_copy(source, target, sems.at[k])
-        for k, (source, target) in enumerate(zip((row_ref, col_ref, left_ref, right_ref), outs))
+        for k, (source, target) in enumerate(zip((left_ref, row_ref, col_ref), (outs[2], *outs[:2])))
     ]
     for copy in copies:
         copy.start()
+    shares, piece = parts_ref.shape[0], right.shape[0] // parts_ref.shape[0]
+
+    def copy_of(t):
+        at = pl.ds(pl.multiple_of(t * piece, piece), piece)
+        return pltpu.make_async_copy(right.at[at], right_out.at[at], sems.at[3 + t])
+
+    for t in range(shares):
+        right[t * piece : (t + 1) * piece, :] = whitened(decode(parts_ref[t]), halves).astype(
+            jnp.bfloat16
+        )
+        copy_of(t).start()
+        copies.append(copy_of(t))
     for copy in copies:
         copy.wait()
 
 
-def emit(arrays):
+def emit(row, col, left, parts, halves, docs):
+    width = left.shape[1]
+    hbm = pl.BlockSpec(memory_space=pl.ANY)
+    right = jax.ShapeDtypeStruct((docs, width), left.dtype)
     return pl.pallas_call(
         emit_kernel,
-        out_shape=[jax.ShapeDtypeStruct(x.shape, x.dtype) for x in arrays],
-        in_specs=[VMEM] * 4,
-        out_specs=[pl.BlockSpec(memory_space=pl.ANY)] * 4,
-        scratch_shapes=[pltpu.SemaphoreType.DMA((4,))],
-        compiler_params=pltpu.CompilerParams(vmem_limit_bytes=4 << 20),
+        out_shape=[jax.ShapeDtypeStruct(x.shape, x.dtype) for x in (row, col, left)] + [right],
+        in_specs=[VMEM] * 5,
+        out_specs=[hbm] * 4,
+        scratch_shapes=[
+            pltpu.VMEM(right.shape, right.dtype),
+            pltpu.SemaphoreType.DMA((3 + parts.shape[0],)),
+        ],
+        compiler_params=pltpu.CompilerParams(vmem_limit_bytes=6 << 20),
         name="emit",
-    )(*arrays)
+    )(row, col, left, parts, halves)
 
 
 def per_device(tile_values, tile_rows, tile_cols, tile_count, start_block):
@@ -910,10 +936,11 @@
             vector,
             vector,
             jax.ShapeDtypeStruct((terms, width), bf16),
-            jax.ShapeDtypeStruct((docs, width), bf16),
+            jax.ShapeDtypeStruct((n, piece + 16, width), int16),
+            jax.ShapeDtypeStruct((2, width, width), bf16),
         ],
         in_specs=[SMEM] + [hbm] * 4,
-        out_specs=[VMEM] * 4,
+        out_specs=[VMEM] * 5,
         scratch_shapes=[
             pltpu.VMEM((terms, TILE), f32),
             pltpu.VMEM((docs, TILE), f32),
@@ -930,9 +957,7 @@
             near,
             far,
             far,
-            pltpu.VMEM((n, piece + 16, width), int16),
             pltpu.VMEM((width, width), f32),
-            pltpu.VMEM((2, width, width), bf16),
             pltpu.VMEM((width, width), f32),
             pltpu.VMEM((width, 2 * width), f32),
         ]
@@ -952,7 +977,7 @@
             for x in (tile_rows, tile_cols, tile_values, start_block)
         ),
     )
-    row, col, left_basis, right_basis = emit(outs)
+    row, col, left_basis, right_basis = emit(*outs, docs)
     return (row.reshape(-1), col.reshape(-1), left_basis, right_basis)
 
 

time: 92.2 us -> 89.8 us (0.974)
  Pallas kernels: 90.6 us -> 88.2 us
    pallas_call x1, Pallas kernels: 89.2 us -> 86.4 us  [per_device(): pl.pallas_call(whole_kernel, out_shape=[vector, vector, jax.ShapeDtypeStr...]
where the time goes in v8:
time: 89.8 us; the launch traced here: 89.6 us
  Pallas kernels  88.2 us (98%)
  between operations  1.47 us (2%)
    pallas_call x1, Pallas kernels, per_device(): pl.pallas_call(whole_kernel, out_shape=[vector, vector, jax.ShapeDtypeStr...  86.4 us
    pallas_call x1, Pallas kernels, emit(): pl.pallas_call(emit_kernel, out_shape=[jax.ShapeDtypeStruct(x.shape, x.dt...  1.8 us

profile of v8, /device:TPU:0, one launch (start us, length us, event | category | flops | bytes accessed | tf_op | source)
XLA Modules:
  0.0 89.6 jit_solution(7101370231664455020)
XLA Ops:
  1.3 86.4 %whole.1 = (f32[16,128]{1,0:T(8,128)S(1)}, f32[16,128]{1,0:T(8,128)S(1)}, bf16[2048,256]{1,0:T(8,128)(2,1)S(1)}, s16[8,272,256]{2,1,0:T(8,128)(2,1)S(1)}, bf16[2,256,256]{2,1,0:T(8,128)(2,1)S(1)}) custom-call(s32[1,1]{1,0:T(1,128)S(6)} %copy.9.count, s32[1,48]{1,0:T(1,128)} %rows_hbm.1, s32[1,48]{1,0:T(1,128)} %cols_hbm.1, bf16[48,128,128]{2,1,0:T(8,128)(2,1)} %tiles_hbm.1, ...), custom_call_target="tpu_custom_call" | custom-call | tf_op jit(solution)/shard_map/whole/pallas_call | solution.py:933
  87.7 1.8 %emit.1 = (f32[16,128]{1,0:T(8,128)}, f32[16,128]{1,0:T(8,128)}, bf16[2048,256]{1,0:T(8,128)(2,1)}, bf16[2048,256]{1,0:T(8,128)(2,1)}) custom-call(f32[16,128]{1,0:T(8,128)S(1)} %get-tuple-element.13.row_ref, f32[16,128]{1,0:T(8,128)S(1)} %get-tuple-element.14.col_ref, bf16[2048,256]{1,0:T(8,128)(2,1)S(1)} %get-tuple-element.15.left_ref, ...), custom_call_target="tpu_custom_call" | custom-call | tf_op jit(solution)/shard_map/emit/pallas_call | solution.py:904

commit v9 on v8

--- a/solution.py
+++ b/solution.py
@@ -80,7 +80,7 @@
             work[after:, :] = work[after:, :] - update
 
 
-def greet():
+def announce():
     barrier = pltpu.get_barrier_semaphore()
     n, m = lax.axis_size("term"), lax.axis_size("doc")
     me, doc = lax.axis_index("term"), lax.axis_index("doc")
@@ -90,7 +90,7 @@
         peers += [{"doc": there}, {"doc": there, "term": me + 1 - 2 * lax.rem(me, 2)}]
     for peer in peers:
         pl.semaphore_signal(barrier, inc=1, device_id=peer, device_id_type=MESH)
-    pl.semaphore_wait(barrier, len(peers))
+    return len(peers)
 
 
 def remote(source, target, send_sem, recv_sem, axis, peer):
@@ -146,14 +146,27 @@
 
 def start_exchange(held, axis, send_sem, recv_sem):
     n, me = lax.axis_size(axis), lax.axis_index(axis)
-    copies = []
-    for step in range(1, n):
-        copy = remote(
+
+    def copy_of(step):
+        return remote(
             held.at[0], held.at[step], send_sem.at[step], recv_sem.at[step], axis, lax.rem(me + step, n)
         )
-        copy.start()
-        copies.append(copy)
-    return copies
+
+    steps = list(range(1, n))
+    if axis == "term":
+        nz, z, c = paired()
+        places = []
+        for k in range(nz - 1):
+            down, up = nz - 1 - k, k
+            down = jnp.where(down <= z, down - 1, down)
+            up = jnp.where(up >= z, up + 1, up)
+            there = jnp.where(2 * z < nz, down, up)
+            places += [2 * there + c, 2 * there + 1 - c]
+        places.append(2 * z + 1 - c)
+        steps = [lax.rem(place - me + n, n) for place in places]
+    for step in steps:
+        copy_of(step).start()
+    return [copy_of(step) for step in range(1, n)]
 
 
 def finish_exchange(copies, held, axis):
@@ -197,9 +210,17 @@
     load_sem,
     *sems,
 ):
+    expected = announce()
     slots = tiles_hbm.shape[0]
-    sources = [rows_hbm, cols_hbm, rows_hbm, cols_hbm, start_hbm, tiles_hbm]
-    targets = [row_ids, col_ids, lanes.at[0], lanes.at[1], start_ref, tiles.at[pl.ds(0, slots)]]
+    sources = [rows_hbm, cols_hbm, rows_hbm, cols_hbm]
+    targets = [row_ids, col_ids, lanes.at[0], lanes.at[1]]
+    quarter = -(-slots // 4)
+    for at in range(0, slots, quarter):
+        stretch = pl.ds(at, min(quarter, slots - at))
+        sources.append(tiles_hbm.at[stretch])
+        targets.append(tiles.at[stretch])
+    sources.append(start_hbm)
+    targets.append(start_ref)
     loads = [
         pltpu.make_async_copy(source, target, load_sem.at[k])
         for k, (source, target) in enumerate(zip(sources, targets))
@@ -219,17 +240,6 @@
         jnp.concatenate([jnp.where(live & (place == lanes[k]), 1.0, 0.0)] * 3, axis=1).astype(jnp.bfloat16)
         for k in range(2)
     )
-    row = lax.broadcasted_iota(jnp.int32, places.shape, 0)
-    col = lax.broadcasted_iota(jnp.int32, places.shape, 1)
-    table = jnp.full(places.shape, slots, jnp.int32)
-    for slot in range(slots):
-        found = (row == row_ids[0, slot]) & (col == jnp.where(slot < used, col_ids[0, slot], -1))
-        table = jnp.where(found, slot, table)
-    places[...] = table
-    keep = pltpu.make_async_copy(places, lookup, load_sem.at[7])
-    keep.start()
-    greet()
-
     def build(out_ref, source, turn):
         def place_row(outer, carry):
             at = pl.multiple_of(outer * TILE, TILE)
@@ -245,20 +255,29 @@
         flipped[slot] = tiles[slot].T
         return carry
 
-    loads[4].wait()
+    for load in loads[4:-1]:
+        load.wait()
+    held_a[0] = tile_sums(tiles, col_ids, parts, sums, to_rows, True)
+    pl.semaphore_wait(pltpu.get_barrier_semaphore(), expected)
+    copies = start_exchange(held_a, "doc", *sems[0:2])
+    row = lax.broadcasted_iota(jnp.int32, places.shape, 0)
+    col = lax.broadcasted_iota(jnp.int32, places.shape, 1)
+    table = jnp.full(places.shape, slots, jnp.int32)
+    for slot in range(slots):
+        found = (row == row_ids[0, slot]) & (col == jnp.where(slot < used, col_ids[0, slot], -1))
+        table = jnp.where(found, slot, table)
+    places[...] = table
+    keep = pltpu.make_async_copy(places, lookup, load_sem.at[9])
+    keep.start()
+    loads[-1].wait()
     mean = jnp.sum(start_ref[...].astype(jnp.float32), axis=0, keepdims=True)
-    keep.wait()
-    loads[5].wait()
-    held_a[0, :blocks, :] = tile_sums(tiles, col_ids, parts, sums, to_rows, True)
-    extra = held_a.shape[1] - blocks
+    extra = held_c.shape[1] - blocks
     pieces = [mean[:, at : at + TILE] for at in range(0, mean.shape[1], TILE)]
     pieces.append(jnp.zeros((extra - len(pieces), TILE), jnp.float32))
-    held_a[0, blocks:, :] = jnp.concatenate(pieces, axis=0)
-    copies = start_exchange(held_a, "doc", *sems[0:2])
-    build(dense_ref, tiles, False)
-    joined = finish_exchange(copies, held_a, "doc")
-    mean_ref[...] = joined[blocks:, :]
-    spread(1.0 / joined[:blocks], parts)
+    held_c[0, blocks:, :] = jnp.concatenate(pieces, axis=0)
+    keep.wait()
+    total = finish_exchange(copies, held_a, "doc")
+    spread(1.0 / total, parts)
 
     held_b[0] = tile_sums(tiles, row_ids, parts, sums, to_cols, False)
     copies = start_exchange(held_b, "term", *sems[2:4])
@@ -266,10 +285,12 @@
     total = finish_exchange(copies, held_b, "term")
     spread(1.0 / total, parts)
 
-    held_c[0] = tile_sums(flipped, col_ids, parts, sums, to_rows, False)
+    held_c[0, :blocks, :] = tile_sums(flipped, col_ids, parts, sums, to_rows, False)
     copies = start_exchange(held_c, "doc", *sems[4:6])
-    build(turned_ref, flipped, True)
-    row_scale = 1.0 / finish_exchange(copies, held_c, "doc")
+    build(dense_ref, tiles, False)
+    joined = finish_exchange(copies, held_c, "doc")
+    mean_ref[...] = joined[blocks:, :]
+    row_scale = 1.0 / joined[:blocks]
     row_ref[...] = row_scale
     spread(row_scale, parts)
 
@@ -281,7 +302,9 @@
     def weigh():
         spread(col_ref[...], parts)
         held_e[0] = tile_sums(flipped, col_ids, parts, sums, to_rows, False)
-        return start_exchange(held_e, "doc", *sems[8:10])
+        copies = start_exchange(held_e, "doc", *sems[8:10])
+        build(turned_ref, flipped, True)
+        return copies
 
     return weigh
 
@@ -310,12 +333,12 @@
         stack,
         pltpu.VMEM((RB, 16, TILE), jnp.bfloat16),
         pltpu.VMEM((slots, TILE), jnp.float32),
+        held(m),
+        held(n),
         held(m, extra),
         held(n),
         held(m),
-        held(n),
-        held(m),
-        pltpu.SemaphoreType.DMA((8,)),
+        pltpu.SemaphoreType.DMA((10,)),
     ] + semaphores(m, m, n, n, m, m, n, n, m, m)
 
 
@@ -806,7 +829,7 @@
             total = total + decode(far_recv[half, step])
         totals.append(total)
     total = jnp.concatenate(totals, axis=1)
-    block = precise(total, inverse_ref[...], ((1,), (1,))) - lean * (1.0 / docs_total)
+    block = whitened(total, halves) - lean * (1.0 / docs_total)
 
     me = c * nz + z
     pack_gram(

time: 89.8 us -> 87.5 us (0.974)
  Pallas kernels: 88.2 us -> 85.8 us
    pallas_call x1, Pallas kernels: 86.4 us -> 84 us  [per_device(): pl.pallas_call(whole_kernel, out_shape=[vector, vector, jax.ShapeDtypeStr...]
where the time goes in v9:
time: 87.5 us; the launch traced here: 87.3 us
  Pallas kernels  85.8 us (98%)
  between operations  1.47 us (2%)
    pallas_call x1, Pallas kernels, per_device(): pl.pallas_call(whole_kernel, out_shape=[vector, vector, jax.ShapeDtypeStr...  84 us
    pallas_call x1, Pallas kernels, emit(): pl.pallas_call(emit_kernel, out_shape=[jax.ShapeDtypeStruct(x.shape, x.dt...  1.8 us

profile of v9, /device:TPU:0, one launch (start us, length us, event | category | flops | bytes accessed | tf_op | source)
XLA Modules:
  0.0 87.3 jit_solution(1902290158420370868)
XLA Ops:
  1.3 84.0 %whole.1 = (f32[16,128]{1,0:T(8,128)S(1)}, f32[16,128]{1,0:T(8,128)S(1)}, bf16[2048,256]{1,0:T(8,128)(2,1)S(1)}, s16[8,272,256]{2,1,0:T(8,128)(2,1)S(1)}, bf16[2,256,256]{2,1,0:T(8,128)(2,1)S(1)}) custom-call(s32[1,1]{1,0:T(1,128)S(6)} %copy.9.count, s32[1,48]{1,0:T(1,128)} %rows_hbm.1, s32[1,48]{1,0:T(1,128)} %cols_hbm.1, bf16[48,128,128]{2,1,0:T(8,128)(2,1)} %tiles_hbm.1, ...), custom_call_target="tpu_custom_call" | custom-call | tf_op jit(solution)/shard_map/whole/pallas_call | solution.py:956
  85.3 1.8 %emit.1 = (f32[16,128]{1,0:T(8,128)}, f32[16,128]{1,0:T(8,128)}, bf16[2048,256]{1,0:T(8,128)(2,1)}, bf16[2048,256]{1,0:T(8,128)(2,1)}) custom-call(f32[16,128]{1,0:T(8,128)S(1)} %get-tuple-element.13.row_ref, f32[16,128]{1,0:T(8,128)S(1)} %get-tuple-element.14.col_ref, bf16[2048,256]{1,0:T(8,128)(2,1)S(1)} %get-tuple-element.15.left_ref, ...), custom_call_target="tpu_custom_call" | custom-call | tf_op jit(solution)/shard_map/emit/pallas_call | solution.py:927

commit v10 on v9

--- a/solution.py
+++ b/solution.py
@@ -910,12 +910,12 @@
         at = pl.ds(pl.multiple_of(t * piece, piece), piece)
         return pltpu.make_async_copy(right.at[at], right_out.at[at], sems.at[3 + t])
 
-    for t in range(shares):
-        right[t * piece : (t + 1) * piece, :] = whitened(decode(parts_ref[t]), halves).astype(
-            jnp.bfloat16
-        )
-        copy_of(t).start()
-        copies.append(copy_of(t))
+    for t in range(0, shares, 2):
+        value = jnp.concatenate([decode(parts_ref[t]), decode(parts_ref[t + 1])], axis=0)
+        right[t * piece : (t + 2) * piece, :] = whitened(value, halves).astype(jnp.bfloat16)
+        for share in (t, t + 1):
+            copy_of(share).start()
+            copies.append(copy_of(share))
     for copy in copies:
         copy.wait()
 

time: 87.5 us -> 87.6 us (level)
  no operation moved by 1% of the time
where the time goes in v10:
time: 87.6 us; the launch traced here: 87.5 us
  Pallas kernels  86 us (98%)
  between operations  1.47 us (2%)
    pallas_call x1, Pallas kernels, per_device(): pl.pallas_call(whole_kernel, out_shape=[vector, vector, jax.ShapeDtypeStr...  84 us
    pallas_call x1, Pallas kernels, emit(): pl.pallas_call(emit_kernel, out_shape=[jax.ShapeDtypeStruct(x.shape, x.dt...  1.97 us

profile of v10, /device:TPU:0, one launch (start us, length us, event | category | flops | bytes accessed | tf_op | source)
XLA Modules:
  0.0 87.5 jit_solution(3229161443093673367)
XLA Ops:
  1.3 84.0 %whole.1 = (f32[16,128]{1,0:T(8,128)S(1)}, f32[16,128]{1,0:T(8,128)S(1)}, bf16[2048,256]{1,0:T(8,128)(2,1)S(1)}, s16[8,272,256]{2,1,0:T(8,128)(2,1)S(1)}, bf16[2,256,256]{2,1,0:T(8,128)(2,1)S(1)}) custom-call(s32[1,1]{1,0:T(1,128)S(6)} %copy.9.count, s32[1,48]{1,0:T(1,128)} %rows_hbm.1, s32[1,48]{1,0:T(1,128)} %cols_hbm.1, bf16[48,128,128]{2,1,0:T(8,128)(2,1)} %tiles_hbm.1, ...), custom_call_target="tpu_custom_call" | custom-call | tf_op jit(solution)/shard_map/whole/pallas_call | solution.py:956
  85.3 2.0 %emit.1 = (f32[16,128]{1,0:T(8,128)}, f32[16,128]{1,0:T(8,128)}, bf16[2048,256]{1,0:T(8,128)(2,1)}, bf16[2048,256]{1,0:T(8,128)(2,1)}) custom-call(f32[16,128]{1,0:T(8,128)S(1)} %get-tuple-element.13.row_ref, f32[16,128]{1,0:T(8,128)S(1)} %get-tuple-element.14.col_ref, bf16[2048,256]{1,0:T(8,128)(2,1)S(1)} %get-tuple-element.15.left_ref, ...), custom_call_target="tpu_custom_call" | custom-call | tf_op jit(solution)/shard_map/emit/pallas_call | solution.py:927
